TPU v7x, 32 devices: a whole 2x2x4 slice. The times are simulated.
32 devices in a mesh: dp: 8 (over y, x, core), tensor: 4 (over z).
Axes of the slice: x: 2, y: 2, z: 4, core: 2. Of those that a mesh axis runs over, the one named last changes fastest.
Arguments:
- tokens: bfloat16 [8192, 768], P(('dp', 'tensor')), may hold values from -6 to 6
- segments: int32 [8, 1024], P('dp'), may hold values from 0 to 15, never falling along the last dimension, each value on 1 to 128 neighbouring positions
- mask_grad: float32 [8192, 150], P(('dp', 'tensor')), may hold values from -6 to 6
- gain_one: float32 [768], P('dp'), may hold values from 0.5 to 1.5
- attend_weight: float32 [768, 2304], P('dp', 'tensor'), may hold values from -0.21875 to 0.21875
- output_weight: float32 [768, 768], P('tensor', 'dp'), may hold values from -0.875 to 0.875
- gain_two: float32 [768], P('dp'), may hold values from 0.5 to 1.5
- up_weight: float32 [768, 3072], P('dp', 'tensor'), may hold values from -0.21875 to 0.21875
- down_weight: float32 [3072, 768], P('tensor', 'dp'), may hold values from -0.109375 to 0.109375
- patch_weight: float32 [768, 768], P('dp', 'tensor'), may hold values from -0.21875 to 0.21875
- class_weight: float32 [768, 768], P('dp', 'tensor'), may hold values from -0.21875 to 0.21875
- class_embed: float32 [150, 768], P(None, 'dp'), may hold values from -6 to 6
- mean_gain_one: float32 [768], P('dp'), may hold values from -12.675879002262526 to 12.675879002262526
- mean_attend_weight: float32 [768, 2304], P('dp', 'tensor'), may hold values from -8.8731153 to 8.8731153
- mean_output_weight: float32 [768, 768], P('tensor', 'dp'), may hold values from -1.774623 to 1.774623
- mean_gain_two: float32 [768], P('dp'), may hold values from -5.0703516 to 5.0703516
- mean_up_weight: float32 [768, 3072], P('dp', 'tensor'), may hold values from -2.5351758 to 2.5351758
- mean_down_weight: float32 [3072, 768], P('tensor', 'dp'), may hold values from -5.0703516 to 5.0703516
- mean_patch_weight: float32 [768, 768], P('dp', 'tensor'), may hold values from -11.408291 to 11.408291
- mean_class_weight: float32 [768, 768], P('dp', 'tensor'), may hold values from -11.154774 to 11.154774
- mean_class_embed: float32 [150, 768], P(None, 'dp'), may hold values from -0.9126633 to 0.9126633
- square_gain_one: float32 [768], P('dp'), may hold values from 19.456 to 1950.72
- square_attend_weight: float32 [768, 2304], P('dp', 'tensor'), may hold values from 9.53344 to 955.8528
- square_output_weight: float32 [768, 768], P('tensor', 'dp'), may hold values from 0.3813376 to 38.23411
- square_gain_two: float32 [768], P('dp'), may hold values from 3.11296 to 312.1152
- square_up_weight: float32 [768, 3072], P('dp', 'tensor'), may hold values from 0.77824 to 78.0288
- square_down_weight: float32 [3072, 768], P('tensor', 'dp'), may hold values from 3.11296 to 312.1152
- square_patch_weight: float32 [768, 768], P('dp', 'tensor'), may hold values from 15.75936 to 1580.0832
- square_class_weight: float32 [768, 768], P('dp', 'tensor'), may hold values from 15.0667264 to 1510.6376
- square_class_embed: float32 [150, 768], P(None, 'dp'), may hold values from 0.1008599 to 10.1125325
Outputs:
- masks: float32 [8192, 150], P(('dp', 'tensor'))
- token_grad: float32 [8192, 768], P(('dp', 'tensor'))
- update_gain_one: float32 [768], P('dp')
- update_attend_weight: float32 [768, 2304], P('dp', 'tensor')
- update_output_weight: float32 [768, 768], P('tensor', 'dp')
- update_gain_two: float32 [768], P('dp')
- update_up_weight: float32 [768, 3072], P('dp', 'tensor')
- update_down_weight: float32 [3072, 768], P('tensor', 'dp')
- update_patch_weight: float32 [768, 768], P('dp', 'tensor')
- update_class_weight: float32 [768, 768], P('dp', 'tensor')
- update_class_embed: float32 [150, 768], P(None, 'dp')
- updated_mean_gain_one: float32 [768], P('dp')
- updated_mean_attend_weight: float32 [768, 2304], P('dp', 'tensor')
- updated_mean_output_weight: float32 [768, 768], P('tensor', 'dp')
- updated_mean_gain_two: float32 [768], P('dp')
- updated_mean_up_weight: float32 [768, 3072], P('dp', 'tensor')
- updated_mean_down_weight: float32 [3072, 768], P('tensor', 'dp')
- updated_mean_patch_weight: float32 [768, 768], P('dp', 'tensor')
- updated_mean_class_weight: float32 [768, 768], P('dp', 'tensor')
- updated_mean_class_embed: float32 [150, 768], P(None, 'dp')
Inputs may be any that keep to these rules, and one draw needn't show every extreme that they name: `segments`: in each row the numbers never fall; each image holds 1 to 128 tokens and some image exactly 128.
All inputs are finite; a program needn't handle non-finite values.
Results may differ from a plain program's by a relative error of at most 0.018.
Values may be sent and summed in bfloat16 or wider, within the bound.
A program may use at most 128 MiB of HBM per device.

v0:
```python
import jax
import jax.numpy as jnp
from jax import lax
from jax.sharding import PartitionSpec as P

HD = 64


epsilon_norm = 1e-05
epsilon_unit = 1e-06
masked_score = -1000000000.0
first_decay = 0.9
second_decay = 0.999
first_fix = 0.99997343860112
second_fix = 0.09520785288629
adam_epsilon = 1e-08
block_scale = 0.65
weight_decay = 0.05


def layer_norm(values, gain):
    center = values - jnp.mean(values, axis=-1, keepdims=True)
    spread = jnp.mean(center * center, axis=-1, keepdims=True)
    return center * lax.rsqrt(spread + epsilon_norm) * gain


def class_norm(products):
    return layer_norm(products, 1.0)


def unit_rows(values):
    return values * lax.rsqrt(jnp.sum(values * values, axis=-1, keepdims=True) + epsilon_unit)


def gelu_exact(values):
    return jax.nn.gelu(values, approximate=False)


def matmul_last(left, right):
    return lax.dot_general(
        left, right, (((1,), (1,)), ((), ())), preferred_element_type=jnp.float32
    )


def matmul_first(left, right):
    return lax.dot_general(
        left, right, (((0,), (0,)), ((), ())), preferred_element_type=jnp.float32
    )


def adamw_update(current, gradient, mean_old, square_old, step_scale, decay_rate):
    mean_new = first_decay * mean_old + (1.0 - first_decay) * gradient
    square_new = second_decay * square_old + (1.0 - second_decay) * gradient * gradient
    moved = mean_new / first_fix / (jnp.sqrt(square_new / second_fix) + adam_epsilon)
    return (step_scale * (moved + decay_rate * current), mean_new)


def block_parts(queries, key_rows, values, segments, block_index, block_rows):
    length = segments.shape[1]
    per_seq = length // block_rows
    sequence = block_index // per_seq
    start_row = block_index % per_seq * block_rows
    query_part = lax.dynamic_slice_in_dim(queries, sequence * length + start_row, block_rows, 0)
    segment_row = segments[0]
    segment_query = lax.dynamic_slice_in_dim(segment_row, start_row, block_rows, 0)
    matches = segment_query[:, None] == segment_row[None, :]
    scores = jnp.einsum(
        "qhd,khd->hqk", query_part, key_rows, preferred_element_type=jnp.float32
    ) * HD ** (-0.5)
    scores = jnp.where(matches[None], scores, masked_score)
    return (query_part, key_rows, values, scores)


def attention_forward(queries, key_rows, values, segments):
    seq_count, length = segments.shape
    block_rows = min(512, length)
    block_total = seq_count * (length // block_rows)

    def one_block(block_index):
        query_part, key_part, value_part, scores = block_parts(
            queries, key_rows, values, segments, block_index, block_rows
        )
        maxima = jnp.max(scores, axis=-1, keepdims=True)
        exponent = jnp.exp(scores - maxima)
        row_total = jnp.sum(exponent, axis=-1, keepdims=True)
        weights_low = (exponent / row_total).astype(jnp.bfloat16)
        attended = jnp.einsum(
            "hqk,khd->qhd", weights_low, value_part, preferred_element_type=jnp.float32
        )
        return (attended, (maxima + jnp.log(row_total))[:, :, 0])

    attended, log_totals = lax.map(one_block, jnp.arange(block_total, dtype=jnp.int32))
    return (attended.reshape(queries.shape), log_totals)


def attention_backward(queries, key_rows, values, segments, log_totals, d_attended):
    seq_count, length = segments.shape
    block_rows = min(512, length)
    per_seq = length // block_rows
    block_total = seq_count * per_seq

    def one_block(pieces):
        block_index, log_block = pieces
        query_part, key_part, value_part, scores = block_parts(
            queries, key_rows, values, segments, block_index, block_rows
        )
        d_part = lax.dynamic_slice_in_dim(d_attended, block_index * block_rows, block_rows, 0)
        weights = jnp.exp(scores - log_block[:, :, None])
        d_weights = jnp.einsum(
            "qhd,khd->hqk", d_part, value_part, preferred_element_type=jnp.float32
        )
        row_delta = jnp.sum(weights * d_weights, axis=-1, keepdims=True)
        d_scores = (weights * (d_weights - row_delta)).astype(jnp.bfloat16)
        d_query = jnp.einsum(
            "hqk,khd->qhd", d_scores, key_part, preferred_element_type=jnp.float32
        ) * HD ** (-0.5)
        d_key = jnp.einsum(
            "hqk,qhd->khd", d_scores, query_part, preferred_element_type=jnp.float32
        ) * HD ** (-0.5)
        d_value = jnp.einsum(
            "hqk,qhd->khd", weights.astype(jnp.bfloat16), d_part, preferred_element_type=jnp.float32
        )
        return (d_query, d_key, d_value)

    d_query, d_key, d_value = lax.map(
        one_block, (jnp.arange(block_total, dtype=jnp.int32), log_totals)
    )
    heads_local = queries.shape[1]
    d_query = d_query.reshape(queries.shape)
    d_key = (
        d_key.reshape(seq_count, per_seq, length, heads_local, HD)
        .sum(axis=1)
        .reshape(queries.shape)
    )
    d_value = (
        d_value.reshape(seq_count, per_seq, length, heads_local, HD)
        .sum(axis=1)
        .reshape(queries.shape)
    )
    return (d_query, d_key, d_value)


def local(
    tokens,
    segments,
    mask_grad,
    gain_one,
    attend_weight,
    output_weight,
    gain_two,
    up_weight,
    down_weight,
    patch_weight,
    class_weight,
    class_embed,
    mean_gain_one,
    mean_attend_weight,
    mean_output_weight,
    mean_gain_two,
    mean_up_weight,
    mean_down_weight,
    mean_patch_weight,
    mean_class_weight,
    mean_class_embed,
    square_gain_one,
    square_attend_weight,
    square_output_weight,
    square_gain_two,
    square_up_weight,
    square_down_weight,
    square_patch_weight,
    square_class_weight,
    square_class_embed,
):
    low_type = jnp.bfloat16
    (
        gain_first,
        attend_full,
        output_full,
        gain_second,
        up_full,
        down_full,
        patch_part,
        class_part,
        embed_full,
    ) = (
        lax.all_gather(gain_one.astype(low_type), "dp", axis=0, tiled=True),
        lax.all_gather(attend_weight.astype(low_type), "dp", axis=0, tiled=True),
        lax.all_gather(output_weight.astype(low_type), "dp", axis=1, tiled=True),
        lax.all_gather(gain_two.astype(low_type), "dp", axis=0, tiled=True),
        lax.all_gather(up_weight.astype(low_type), "dp", axis=0, tiled=True),
        lax.all_gather(down_weight.astype(low_type), "dp", axis=1, tiled=True),
        lax.all_gather(patch_weight.astype(low_type), "dp", axis=0, tiled=True),
        lax.all_gather(class_weight.astype(low_type), "dp", axis=0, tiled=True),
        lax.all_gather(class_embed.astype(low_type), "dp", axis=1, tiled=True),
    )
    patch_full, class_full = (
        lax.all_gather(patch_part, "tensor", axis=1, tiled=True),
        lax.all_gather(class_part, "tensor", axis=1, tiled=True),
    )
    gain_first_wide = gain_first.astype(jnp.float32)
    gain_second_wide = gain_second.astype(jnp.float32)
    token_wide = tokens.astype(jnp.float32)
    norm_one = lax.all_gather(
        layer_norm(token_wide, gain_first_wide).astype(low_type), "tensor", axis=0, tiled=True
    )
    group_rows = norm_one.shape[0]
    heads_local = attend_full.shape[1] // (3 * HD)
    joint = jnp.dot(norm_one, attend_full, preferred_element_type=jnp.float32).astype(low_type)
    joint = joint.reshape(group_rows, heads_local, 3, HD)
    queries = joint[:, :, 0]
    key_rows = joint[:, :, 1]
    values = joint[:, :, 2]
    attended, log_totals = attention_forward(queries, key_rows, values, segments)
    attended_low = attended.astype(low_type).reshape(group_rows, heads_local * HD)
    resid_one = token_wide + lax.psum_scatter(
        jnp.dot(attended_low, output_full, preferred_element_type=jnp.float32),
        "tensor",
        scatter_dimension=0,
        tiled=True,
    )
    norm_two = lax.all_gather(
        layer_norm(resid_one, gain_second_wide).astype(low_type), "tensor", axis=0, tiled=True
    )
    hidden_pre = jnp.dot(norm_two, up_full, preferred_element_type=jnp.float32)
    hidden = gelu_exact(hidden_pre).astype(low_type)
    resid_two = resid_one + lax.psum_scatter(
        jnp.dot(hidden, down_full, preferred_element_type=jnp.float32),
        "tensor",
        scatter_dimension=0,
        tiled=True,
    )
    resid_low = resid_two.astype(low_type)
    patch_feat = jnp.dot(resid_low, patch_full, preferred_element_type=jnp.float32)
    patch_unit = unit_rows(patch_feat).astype(low_type)
    class_feat = jnp.dot(embed_full, class_full, preferred_element_type=jnp.float32)
    class_unit = unit_rows(class_feat).astype(low_type)
    products = matmul_last(patch_unit, class_unit)
    masks, mask_back = jax.vjp(class_norm, products)
    d_products = mask_back(mask_grad)[0].astype(low_type)
    d_patch_unit = jnp.dot(d_products, class_unit, preferred_element_type=jnp.float32)
    d_class_part = matmul_first(d_products, patch_unit)
    patch_again, patch_back = jax.vjp(unit_rows, patch_feat)
    d_patch_feat = patch_back(d_patch_unit)[0].astype(low_type)
    grad_patch_part = matmul_first(resid_low, d_patch_feat)
    d_resid_two = matmul_last(d_patch_feat, patch_full)
    d_class_unit = lax.psum(d_class_part, ("dp", "tensor"))
    class_again, class_back = jax.vjp(unit_rows, class_feat)
    d_class_feat = class_back(d_class_unit)[0].astype(low_type)
    grad_class_full = matmul_first(embed_full, d_class_feat)
    grad_embed_full = matmul_last(d_class_feat, class_full)
    d_branch_two = lax.all_gather(d_resid_two.astype(low_type), "tensor", axis=0, tiled=True)
    d_hidden = matmul_last(d_branch_two, down_full)
    grad_down_part = matmul_first(hidden, d_branch_two)
    gelu_again, gelu_back = jax.vjp(gelu_exact, hidden_pre)
    d_hidden_pre = gelu_back(d_hidden)[0].astype(low_type)
    grad_up_part = matmul_first(norm_two, d_hidden_pre)
    d_norm_two = lax.psum_scatter(
        matmul_last(d_hidden_pre, up_full).astype(jnp.bfloat16),
        "tensor",
        scatter_dimension=0,
        tiled=True,
    ).astype(jnp.float32)
    second_again, second_back = jax.vjp(layer_norm, resid_one, gain_second_wide)
    d_resid_norm, grad_gain_two = second_back(d_norm_two)
    d_resid_one = d_resid_two + d_resid_norm
    d_branch_one = lax.all_gather(d_resid_one.astype(low_type), "tensor", axis=0, tiled=True)
    d_attended = matmul_last(d_branch_one, output_full).astype(low_type)
    grad_output_part = matmul_first(attended_low, d_branch_one)
    d_query, d_key, d_value = attention_backward(
        queries,
        key_rows,
        values,
        segments,
        log_totals,
        d_attended.reshape(group_rows, heads_local, HD),
    )
    d_joint = (
        jnp.stack((d_query, d_key, d_value), axis=2)
        .astype(low_type)
        .reshape(group_rows, heads_local * 3 * HD)
    )
    grad_attend_part = matmul_first(norm_one, d_joint)
    d_norm_one = lax.psum_scatter(
        matmul_last(d_joint, attend_full).astype(jnp.bfloat16),
        "tensor",
        scatter_dimension=0,
        tiled=True,
    ).astype(jnp.float32)
    first_again, first_back = jax.vjp(layer_norm, token_wide, gain_first_wide)
    d_token_norm, grad_gain_one = first_back(d_norm_one)
    token_grad = d_resid_one + d_token_norm
    dp_index = lax.axis_index("dp")
    tensor_index = lax.axis_index("tensor")
    gain_rows = gain_one.shape[0]
    sum_attend, sum_output, sum_up, sum_down = lax.psum(
        (grad_attend_part, grad_output_part, grad_up_part, grad_down_part), "dp"
    )
    sum_gain_one, sum_gain_two, sum_patch = lax.psum(
        (grad_gain_one, grad_gain_two, grad_patch_part), ("dp", "tensor")
    )
    share_attend = lax.dynamic_slice_in_dim(
        sum_attend, dp_index * attend_weight.shape[0], attend_weight.shape[0], 0
    )
    share_output = lax.dynamic_slice_in_dim(
        sum_output, dp_index * output_weight.shape[1], output_weight.shape[1], 1
    )
    share_up = lax.dynamic_slice_in_dim(
        sum_up, dp_index * up_weight.shape[0], up_weight.shape[0], 0
    )
    share_down = lax.dynamic_slice_in_dim(
        sum_down, dp_index * down_weight.shape[1], down_weight.shape[1], 1
    )
    share_gain_one = lax.dynamic_slice_in_dim(sum_gain_one, dp_index * gain_rows, gain_rows, 0)
    share_gain_two = lax.dynamic_slice_in_dim(sum_gain_two, dp_index * gain_rows, gain_rows, 0)
    patch_rows = lax.dynamic_slice_in_dim(
        sum_patch, dp_index * patch_weight.shape[0], patch_weight.shape[0], 0
    )
    share_patch = lax.dynamic_slice_in_dim(
        patch_rows, tensor_index * patch_weight.shape[1], patch_weight.shape[1], 1
    )
    class_rows = lax.dynamic_slice_in_dim(
        grad_class_full, dp_index * class_weight.shape[0], class_weight.shape[0], 0
    )
    share_class = lax.dynamic_slice_in_dim(
        class_rows, tensor_index * class_weight.shape[1], class_weight.shape[1], 1
    )
    share_embed = lax.dynamic_slice_in_dim(
        grad_embed_full, dp_index * class_embed.shape[1], class_embed.shape[1], 1
    )
    new_gain_one = adamw_update(
        gain_one, share_gain_one, mean_gain_one, square_gain_one, block_scale, 0.0
    )
    new_attend = adamw_update(
        attend_weight,
        share_attend,
        mean_attend_weight,
        square_attend_weight,
        block_scale,
        weight_decay,
    )
    new_output = adamw_update(
        output_weight,
        share_output,
        mean_output_weight,
        square_output_weight,
        block_scale,
        weight_decay,
    )
    new_gain_two = adamw_update(
        gain_two, share_gain_two, mean_gain_two, square_gain_two, block_scale, 0.0
    )
    new_up = adamw_update(
        up_weight, share_up, mean_up_weight, square_up_weight, block_scale, weight_decay
    )
    new_down = adamw_update(
        down_weight, share_down, mean_down_weight, square_down_weight, block_scale, weight_decay
    )
    new_patch = adamw_update(
        patch_weight, share_patch, mean_patch_weight, square_patch_weight, 1.0, weight_decay
    )
    new_class = adamw_update(
        class_weight, share_class, mean_class_weight, square_class_weight, 1.0, weight_decay
    )
    new_embed = adamw_update(
        class_embed, share_embed, mean_class_embed, square_class_embed, 1.0, weight_decay
    )
    return (
        masks,
        token_grad,
        new_gain_one[0],
        new_attend[0],
        new_output[0],
        new_gain_two[0],
        new_up[0],
        new_down[0],
        new_patch[0],
        new_class[0],
        new_embed[0],
        new_gain_one[1],
        new_attend[1],
        new_output[1],
        new_gain_two[1],
        new_up[1],
        new_down[1],
        new_patch[1],
        new_class[1],
        new_embed[1],
    )


def solution(mesh):
    return jax.shard_map(
        local,
        mesh=mesh,
        in_specs=(
            P(("dp", "tensor"), None),
            P("dp", None),
            P(("dp", "tensor"), None),
            P("dp"),
            P("dp", "tensor"),
            P("tensor", "dp"),
            P("dp"),
            P("dp", "tensor"),
            P("tensor", "dp"),
            P("dp", "tensor"),
            P("dp", "tensor"),
            P(None, "dp"),
            P("dp"),
            P("dp", "tensor"),
            P("tensor", "dp"),
            P("dp"),
            P("dp", "tensor"),
            P("tensor", "dp"),
            P("dp", "tensor"),
            P("dp", "tensor"),
            P(None, "dp"),
            P("dp"),
            P("dp", "tensor"),
            P("tensor", "dp"),
            P("dp"),
            P("dp", "tensor"),
            P("tensor", "dp"),
            P("dp", "tensor"),
            P("dp", "tensor"),
            P(None, "dp"),
        ),
        out_specs=(
            P(("dp", "tensor"), None),
            P(("dp", "tensor"), None),
            P("dp"),
            P("dp", "tensor"),
            P("tensor", "dp"),
            P("dp"),
            P("dp", "tensor"),
            P("tensor", "dp"),
            P("dp", "tensor"),
            P("dp", "tensor"),
            P(None, "dp"),
            P("dp"),
            P("dp", "tensor"),
            P("tensor", "dp"),
            P("dp"),
            P("dp", "tensor"),
            P("tensor", "dp"),
            P("dp", "tensor"),
            P("dp", "tensor"),
            P(None, "dp"),
        ),
        check_vma=False,
    )
```

profile of v0, /device:TPU:0, one launch (start us, length us, event | category | flops | bytes accessed | tf_op | source)
XLA Modules:
  0.0 746.2 jit_solution(2679570672515325374)
XLA Ops:
  11.7 15.1 %all-reduce.5 = (bf16[768]{0:T(1024)(128)(2,1)S(1)}, bf16[768]{0:T(1024)(128)(2,1)S(1)}) all-reduce(bf16[768]{0:T(1024)(128)(2,1)S(1)} %dynamic-update-slice, bf16[768]{0:T(1024)(128)(2,1)S(1)} %dynamic-update-slice.1), channel_id=1, replica_groups=mesh['dp'=8,'tensor'=4] {'dp'}, use_global_device_ids=true, to_apply=%add | all-reduce | flops 1536 | bytes 6144
  33.3 8.6 %all_gather.48 = bf16[192,768]{0,1:T(8,128)(2,1)S(1)} all-gather(bf16[192,96]{0,1:T(8,128)(2,1)S(1)} %copy.81), channel_id=1, replica_groups=mesh['dp'=8,'tensor'=4] {'dp'}, dimensions={1}, use_global_device_ids=true | all-gather | bytes 331776 | tf_op jit(solution)/shard_map/all_gather | solution.py:189
  41.9 11.1 %all_gather.47 = bf16[768,576]{1,0:T(8,128)(2,1)S(1)} all-gather(bf16[96,576]{1,0:T(8,128)(2,1)S(1)} %convert_element_type.124), channel_id=1, replica_groups=mesh['dp'=8,'tensor'=4] {'dp'}, dimensions={0}, use_global_device_ids=true | all-gather | bytes 995328 | tf_op jit(solution)/shard_map/all_gather | solution.py:188
  53.0 14.8 %all-gather.10.cloned.1.call-done = bf16[1024,768]{1,0:T(8,128)(2,1)} async-done(((bf16[256,768]{1,0:T(8,128)(2,1)}), bf16[1024,768]{1,0:T(8,128)(2,1)}) %all-gather.10.cloned.1.call-update) | async-done | bytes 1572880 | tf_op jit(solution)/shard_map/all_gather | solution.py:204
  70.6 18.1 %while.30 = (s32[]{:T(128)}, bf16[2,512,3,64]{1,3,2,0:T(8,128)(2,1)S(1)}, f32[2,3,512]{2,1,0:T(4,128)S(1)}, s32[2]{0:T(128)S(1)}, s32[1,1024]{1,0:T(1,128)S(1)},...) while((s32[]{:T(128)}, ...), condition=%wide.region_5.6_spmd, body=%wide.region_2.5_spmd.sunk | while | flops 422050336 | bytes 22417860 | solution.py:92
  93.1 58.4 %reduce-scatter.5.cloned.1.call-done = f32[256,768]{1,0:T(8,128)} async-done(((f32[1024,768]{1,0:T(8,128)}), f32[256,768]{1,0:T(8,128)}) %reduce-scatter.5.cloned.1.call-update) | async-done | bytes 786448 | tf_op jit(solution)/shard_map/reduce_scatter | solution.py:216
  154.9 9.5 %all_gather.56 = bf16[768,192]{1,0:T(8,128)(2,1)S(1)} all-gather(bf16[96,192]{1,0:T(8,128)(2,1)S(1)} %convert_element_type.139), channel_id=1, replica_groups=mesh['dp'=8,'tensor'=4] {'dp'}, dimensions={0}, use_global_device_ids=true | all-gather | bytes 331776 | tf_op jit(solution)/shard_map/all_gather | solution.py:194
  165.5 25.5 %all-gather.12.cloned.1.call-done = bf16[1024,768]{1,0:T(8,128)(2,1)} async-done(((bf16[256,768]{1,0:T(8,128)(2,1)}), bf16[1024,768]{1,0:T(8,128)(2,1)}) %all-gather.12.cloned.1.call-update) | async-done | bytes 1572880 | tf_op jit(solution)/shard_map/all_gather | solution.py:222
  191.1 11.0 %multiply_convert_fusion.1 = (bf16[1024,768]{1,0:T(8,128)(2,1)}, f32[1024,768]{1,0:T(8,128)}, f32[1024,768]{1,0:T(8,128)}) fusion(bf16[1024,768]{1,0:T(8,128)(2,1)} %all-gather.12.cloned.1.call-done, bf16[768,768]{1,0:T(8,128)(2,1)} %all-gather.14.cloned.1.call-done), kind=kOutput, calls=%fused_computation.48 | convolution fusion | flops 1259077632 | bytes 10616832 | tf_op jit(solution)/shard_map/dot_general | solution.py:225
  202.1 14.1 %all-gather.16.cloned.1.call-done = bf16[768,768]{0,1:T(8,128)(2,1)} async-done(((bf16[768,96]{0,1:T(8,128)(2,1)}), bf16[768,768]{0,1:T(8,128)(2,1)}) %all-gather.16.cloned.1.call-update) | async-done | bytes 1179664 | tf_op jit(solution)/shard_map/all_gather | solution.py:192
  216.2 4.9 fusion.123
  221.9 9.5 %all_gather.53 = bf16[768,192]{1,0:T(8,128)(2,1)S(1)} all-gather(bf16[96,192]{1,0:T(8,128)(2,1)S(1)} %convert_element_type.136), channel_id=1, replica_groups=mesh['dp'=8,'tensor'=4] {'dp'}, dimensions={0}, use_global_device_ids=true | all-gather | bytes 331776 | tf_op jit(solution)/shard_map/all_gather | solution.py:193
  232.4 8.5 %all-gather = bf16[8,96,150]{1,2,0:T(8,128)(2,1)S(1)} all-gather(bf16[1,96,150]{1,2,0:T(8,128)(2,1)S(1)} %convert_bitcast_fusion.2), channel_id=1, replica_groups=mesh['dp'=8,'tensor'=4] {'dp'}, dimensions={0}, use_global_device_ids=true | all-gather | bytes 259200 | tf_op jit(solution)/shard_map/all_gather | solution.py:195
  241.3 7.3 all-gather.20.cloned.1.call-done
  250.5 59.9 %reduce-scatter.7.cloned.1.call-done = f32[256,768]{1,0:T(8,128)} async-done(((f32[1024,768]{1,0:T(8,128)}), f32[256,768]{1,0:T(8,128)}) %reduce-scatter.7.cloned.1.call-update) | async-done | bytes 786448 | tf_op jit(solution)/shard_map/reduce_scatter | solution.py:227
  312.4 30.4 %all-gather.18.cloned.1.call-done = bf16[768,768]{0,1:T(8,128)(2,1)} async-done(((bf16[768,192]{0,1:T(8,128)(2,1)}), bf16[768,768]{0,1:T(8,128)(2,1)}) %all-gather.18.cloned.1.call-update) | async-done | bytes 1179664 | tf_op jit(solution)/shard_map/all_gather | solution.py:198
  350.9 36.4 %all-gather.22.cloned.1.call-done = bf16[1024,768]{1,0:T(8,128)(2,1)} async-done(((bf16[256,768]{1,0:T(8,128)(2,1)}), bf16[1024,768]{1,0:T(8,128)(2,1)}) %all-gather.22.cloned.1.call-update) | async-done | bytes 1572880 | tf_op jit(solution)/shard_map/all_gather | solution.py:252
  387.3 5.7 add_convert_fusion
  396.8 34.2 %reduce-scatter.9.cloned.1.call-done = bf16[256,768]{1,0:T(8,128)(2,1)} async-done(((bf16[1024,768]{1,0:T(8,128)(2,1)}), bf16[256,768]{1,0:T(8,128)(2,1)}) %reduce-scatter.9.cloned.1.call-update) | async-done | bytes 393232 | tf_op jit(solution)/shard_map/reduce_scatter | solution.py:258
  441.2 36.1 %all-gather.24.cloned.1.call-done = bf16[1024,768]{1,0:T(8,128)(2,1)} async-done(((bf16[256,768]{1,0:T(8,128)(2,1)}), bf16[1024,768]{1,0:T(8,128)(2,1)}) %all-gather.24.cloned.1.call-update) | async-done | bytes 1572880 | tf_op jit(solution)/shard_map/all_gather | solution.py:267
  479.5 38.5 %while.31 = (s32[]{:T(128)}, bf16[2,512,3,64]{1,3,2,0:T(8,128)(2,1)S(1)}, f32[2,1024,3,64]{1,3,2,0:T(8,128)}, f32[2,1024,3,64]{1,3,2,0:T(8,128)}, s32[2]{0:T(128...) while((s32[]{:T(128)}, ...), condition=%wide.region_22.23_spmd, body=%wide.region_20.22_spmd.sunk | while | flops 1031043584 | bytes 84731008 | solution.py:125
  482.7 3.7 fusion.208
  487.4 4.8 multiply_reduce_fusion.9
  496.0 2.7 fusion.211
  502.0 3.7 fusion.208
  506.7 4.8 multiply_reduce_fusion.9
  526.0 4.9 fusion.127
  531.0 2.9 fusion.126
  535.2 2.7 fusion.124
  538.0 73.7 %all-reduce.9.cloned.1.call-done = (f32[768,768]{1,0:T(8,128)}, f32[150,768]{1,0:T(8,128)}) async-done(((f32[768,768]{1,0:T(8,128)}, f32[150,768]{1,0:T(8,128)}), (f32[768,768]{1,0:T(8,128)}, f32[150,768]{1,0:T(8,128)})) %all-reduce.9.cloned.1.call-update) | async-done | bytes 2820112 | tf_op jit(solution)/shard_map/psum | solution.py:299
  622.0 39.9 %all-reduce.2 = (f32[768]{0:T(1024)S(1)}, f32[768]{0:T(1024)S(1)}) all-reduce(f32[768]{0:T(1024)S(1)} %get-tuple-element.274, f32[768]{0:T(1024)S(1)} %copy-done.56), channel_id=1, replica_groups=mesh['dp'=8,'tensor'=4] {'dp','tensor'}, use_global_device_ids=true, to_apply=%region_29.30 | all-reduce | flops 1536 | bytes 12288 | tf_op jit(solution)/shard_map/psum | solution.py:299
  664.9 65.6 %all-reduce.11.cloned.1.call-done = (f32[768,576]{1,0:T(8,128)}, f32[192,768]{1,0:T(8,128)}, f32[768,768]{1,0:T(8,128)}, f32[768,768]{0,1:T(8,128)}) async-done(((f32[768,576]{1,0:T(8,128)}, f32[192,768]{1,0:T(8,128)}, f32[768,768]{1,0:T(8,128)}, f32[768,768]{0,1:T(8,128)}), (f32[768,576]{1,0:T(8,128)}, f32[192,768]{1,0:T(8,128)}, f32[768,768]{1,0:T(8,128)}, ...) | async-done | bytes 7077904 | tf_op jit(solution)/shard_map/psum | solution.py:296
  (313 shorter events, 105.7 us)
Async XLA Ops:
  8.0 59.9 %all-gather.10.cloned.1.call-start = ((), (), s32[]{:S(2)}) async-start(), calls=%async_computation.4 | async-start | bytes 1966080 | tf_op jit(solution)/shard_map/all_gather | solution.py:204
  31.3 120.2 %reduce-scatter.5.cloned.1.call-start = ((), (), s32[]{:S(2)}) async-start(), calls=%async_computation.5 | async-start | bytes 3932160 | tf_op jit(solution)/shard_map/reduce_scatter | solution.py:216
  92.2 73.3 %all-gather.14.cloned.1.call-start = ((), (), s32[]{:S(2)}) async-start(), calls=%async_computation.7 | async-start | bytes 1327104 | tf_op jit(solution)/shard_map/all_gather | solution.py:191
  93.0 98.1 %all-gather.12.cloned.1.call-start = ((), (), s32[]{:S(2)}) async-start(), calls=%async_computation.6 | async-start | bytes 1966080 | tf_op jit(solution)/shard_map/all_gather | solution.py:222
  154.0 62.2 %all-gather.16.cloned.1.call-start = ((), (), s32[]{:S(2)}) async-start(), calls=%async_computation.8 | async-start | bytes 1327104 | tf_op jit(solution)/shard_map/all_gather | solution.py:192
  154.8 93.8 %all-gather.20.cloned.1.call-start = ((), (), s32[]{:S(2)}) async-start(), calls=%async_computation.11 | async-start | bytes 1474560 | tf_op jit(solution)/shard_map/all_gather | solution.py:199
  165.3 145.1 %reduce-scatter.7.cloned.1.call-start = ((), (), s32[]{:S(2)}) async-start(), calls=%async_computation.9 | async-start | bytes 3932160 | tf_op jit(solution)/shard_map/reduce_scatter | solution.py:227
  221.1 121.6 %all-gather.18.cloned.1.call-start = ((), (), s32[]{:S(2)}) async-start(), calls=%async_computation.10 | async-start | bytes 1474560 | tf_op jit(solution)/shard_map/all_gather | solution.py:198
  232.4 154.9 %all-gather.22.cloned.1.call-start = ((), (), s32[]{:S(2)}) async-start(), calls=%async_computation.12 | async-start | bytes 1966080 | tf_op jit(solution)/shard_map/all_gather | solution.py:252
  241.3 103.4 %copy-start.16 = (bf16[768,150]{0,1:T(8,128)(2,1)}, bf16[768,150]{0,1:T(8,128)(2,1)S(1)}, u32[]{:S(2)}) copy-start(bf16[768,150]{0,1:T(8,128)(2,1)S(1)} %reshape.282) | copy-start | bytes 691204
  250.5 94.2 %copy-start.60 = (f32[150]{0:T(256)}, f32[150]{0:T(256)S(1)}, u32[]{:S(2)}) copy-start(f32[150]{0:T(256)S(1)} %get-tuple-element.361) | copy-start | bytes 1804
  250.5 98.2 %copy-start.2 = (f32[150,768]{1,0:T(8,128)}, f32[150,768]{1,0:T(8,128)S(1)}, u32[]{:S(2)}) copy-start(f32[150,768]{1,0:T(8,128)S(1)} %get-tuple-element.362) | copy-start | bytes 1382404
  350.8 80.2 %reduce-scatter.9.cloned.1.call-start = ((), (), s32[]{:S(2)}) async-start(), calls=%async_computation.13 | async-start | bytes 1966080 | tf_op jit(solution)/shard_map/reduce_scatter | solution.py:258
  396.8 80.5 %all-gather.24.cloned.1.call-start = ((), (), s32[]{:S(2)}) async-start(), calls=%async_computation.14 | async-start | bytes 1966080 | tf_op jit(solution)/shard_map/all_gather | solution.py:267
  436.9 174.8 %all-reduce.9.cloned.1.call-start = ((), (), s32[]{:S(2)}) async-start(), calls=%async_computation.16 | async-start | bytes 5652480 | tf_op jit(solution)/shard_map/psum | solution.py:299
  440.9 178.1 %reduce-scatter.11.cloned.1.call-start = ((), (), s32[]{:S(2)}) async-start(), calls=%async_computation.15 | async-start | bytes 1966080 | tf_op jit(solution)/shard_map/reduce_scatter | solution.py:284
  525.7 204.8 %all-reduce.11.cloned.1.call-start = ((), (), s32[]{:S(2)}) async-start(), calls=%async_computation.17 | async-start | bytes 14548992 | tf_op jit(solution)/shard_map/psum | solution.py:296
  537.9 73.7 %copy-start.3 = (f32[150,768]{1,0:T(8,128)S(1)}, f32[150,768]{1,0:T(8,128)}, u32[]{:S(2)}) copy-start(f32[150,768]{1,0:T(8,128)} %copy-done.2) | copy-start | bytes 1382404
  537.9 74.9 %copy-start.61 = (f32[150]{0:T(256)S(1)}, f32[150]{0:T(256)}, u32[]{:S(2)}) copy-start(f32[150]{0:T(256)} %copy-done.60) | copy-start | bytes 1804
  537.9 76.2 %copy-start.7 = (bf16[768,768]{0,1:T(8,128)(2,1)S(1)}, bf16[768,768]{0,1:T(8,128)(2,1)}, u32[]{:S(2)}) copy-start(bf16[768,768]{0,1:T(8,128)(2,1)} %all-gather.20.cloned.1.call-done) | copy-start | bytes 3538948
  538.0 76.7 %copy-start.35 = (f32[150,96]{1,0:T(8,128)S(1)}, f32[150,96]{1,0:T(8,128)}, u32[]{:S(2)}) copy-start(f32[150,96]{1,0:T(8,128)} %param.45) | copy-start | bytes 172804
  538.0 76.7 %copy-start.50 = (f32[150,96]{1,0:T(8,128)S(1)}, f32[150,96]{1,0:T(8,128)}, u32[]{:S(2)}) copy-start(f32[150,96]{1,0:T(8,128)} %param.63) | copy-start | bytes 172804
  538.0 78.5 %copy-start.17 = (bf16[768,150]{0,1:T(8,128)(2,1)S(1)}, bf16[768,150]{0,1:T(8,128)(2,1)}, u32[]{:S(2)}) copy-start(bf16[768,150]{0,1:T(8,128)(2,1)} %copy-done.16) | copy-start | bytes 691204
  617.0 113.6 %copy-start.21 = (f32[768,96]{0,1:T(8,128)S(1)}, f32[768,96]{0,1:T(8,128)}, u32[]{:S(2)}) copy-start(f32[768,96]{0,1:T(8,128)} %param.42) | copy-start | bytes 884740
  617.0 113.5 %copy-start.36 = (f32[768,96]{0,1:T(8,128)S(1)}, f32[768,96]{0,1:T(8,128)}, u32[]{:S(2)}) copy-start(f32[768,96]{0,1:T(8,128)} %param.60) | copy-start | bytes 884740
  617.0 113.5 %copy-start.37 = (f32[768,96]{0,1:T(8,128)S(1)}, f32[768,96]{0,1:T(8,128)}, u32[]{:S(2)}) copy-start(f32[768,96]{0,1:T(8,128)} %param.51) | copy-start | bytes 884740
  619.0 113.6 %copy-start.23 = (f32[96,768]{1,0:T(8,128)S(1)}, f32[96,768]{1,0:T(8,128)}, u32[]{:S(2)}) copy-start(f32[96,768]{1,0:T(8,128)} %param.41) | copy-start | bytes 884740
  662.6 72.1 %copy-start.26 = (f32[96,576]{1,0:T(8,128)S(1)}, f32[96,576]{1,0:T(8,128)}, u32[]{:S(2)}) copy-start(f32[96,576]{1,0:T(8,128)} %param.38) | copy-start | bytes 663556
  664.9 69.8 %copy-start.39 = (f32[96,576]{1,0:T(8,128)S(1)}, f32[96,576]{1,0:T(8,128)}, u32[]{:S(2)}) copy-start(f32[96,576]{1,0:T(8,128)} %param.47) | copy-start | bytes 663556
  664.9 71.7 %copy-start.29 = (f32[192,96]{1,0:T(8,128)S(1)}, f32[192,96]{1,0:T(8,128)}, u32[]{:S(2)}) copy-start(f32[192,96]{1,0:T(8,128)} %param.39) | copy-start | bytes 221188
  664.9 71.7 %copy-start.44 = (f32[192,96]{1,0:T(8,128)S(1)}, f32[192,96]{1,0:T(8,128)}, u32[]{:S(2)}) copy-start(f32[192,96]{1,0:T(8,128)} %param.57) | copy-start | bytes 221188
  664.9 71.7 %copy-start.45 = (f32[192,96]{1,0:T(8,128)S(1)}, f32[192,96]{1,0:T(8,128)}, u32[]{:S(2)}) copy-start(f32[192,96]{1,0:T(8,128)} %param.48) | copy-start | bytes 221188
  (62 other events, 1017.0 us)
Sparse Core Ops, SparseCore 0:
  31.4 36.4 all-gather.9
  92.3 59.1 reduce-scatter.4
  351.0 36.2 all-gather.21
  396.9 34.1 reduce-scatter.8
  437.0 40.2 all-gather.23
  525.8 35.1 reduce-scatter.10
Sparse Core Ops, SparseCore 1:
  95.2 22.7 all-gather.13
  154.1 36.9 all-gather.11
  193.4 22.7 all-gather.15
  218.3 30.2 all-gather.19
  250.9 59.4 reduce-scatter.6
  312.6 30.1 all-gather.17
  442.9 168.7 all-reduce.8
  615.2 115.3 all-reduce.10
where the time goes:
time: 755 us; the launch traced here: 746 us
  waiting for transfers between devices  457 us (61%)
  blocking collectives  102 us (14%)
  matrix products  89.4 us (12%)
  other arithmetic  52.8 us (7%)
  between operations  17.8 us (2%)
  local copies, waits for them, and re-layouts  13.7 us (2%)
  loops' own time  12.1 us (2%)
    psum x1, waiting for transfers between devices, local(): lax.psum((grad_gain_one, grad_gain_two, grad_patch_part), ('dp', 'tensor'))  73.7 us
    psum x1, waiting for transfers between devices, local(): lax.psum((grad_attend_part, grad_output_part, grad_up_part, grad_down_par...  65.6 us
    reduce_scatter x1, waiting for transfers between devices, local(): lax.psum_scatter(jnp.dot(hidden, down_full, preferred_element_type=jnp.fl...  59.9 us
    reduce_scatter x1, waiting for transfers between devices, local(): lax.psum_scatter(jnp.dot(attended_low, output_full, preferred_element_typ...  58.4 us
    psum x1, blocking collectives, local(): lax.psum((grad_gain_one, grad_gain_two, grad_patch_part), ('dp', 'tensor'))  39.9 us
    all_gather x1, waiting for transfers between devices, local(): lax.all_gather(d_resid_two.astype(low_type), 'tensor', axis=0, tiled=True)  36.4 us
    all_gather x1, waiting for transfers between devices, local(): lax.all_gather(d_resid_one.astype(low_type), 'tensor', axis=0, tiled=True)  36.1 us
    reduce_scatter x1, waiting for transfers between devices, local(): lax.psum_scatter(matmul_last(d_hidden_pre, up_full).astype(jnp.bfloat16),...  34.2 us
  transfers between devices with their start and end apart: 14, of which 12 were waited for; matrix products, arithmetic and copies ran while one was open for 13% of the time, Pallas kernels for 0%

commit v1 on v0

v1 whole, which is shorter than its diff:
```python
import functools

import jax
import jax.numpy as jnp
from jax import lax
from jax.experimental import pallas as pl
from jax.experimental.pallas import tpu as pltpu
from jax.sharding import PartitionSpec as P

HD = 64
HALO = 128
BF = jnp.bfloat16
F32 = jnp.float32
MESH = pl.DeviceIdType.MESH

epsilon_norm = 1e-05
epsilon_unit = 1e-06
masked_score = -1000000000.0
first_decay = 0.9
second_decay = 0.999
first_fix = 0.99997343860112
second_fix = 0.09520785288629
adam_epsilon = 1e-08
block_scale = 0.65
weight_decay = 0.05


def dot(left, right, dims=((1,), (0,))):
    return lax.dot_general(left, right, (dims, ((), ())), preferred_element_type=F32)


def layer_norm(values, gain):
    center = values - jnp.mean(values, axis=-1, keepdims=True)
    spread = jnp.mean(center * center, axis=-1, keepdims=True)
    return center * lax.rsqrt(spread + epsilon_norm) * gain


def norm_parts(values):
    center = values - jnp.mean(values, axis=-1, keepdims=True)
    spread = jnp.mean(center * center, axis=-1, keepdims=True)
    inverse = lax.rsqrt(spread + epsilon_norm)
    return center * inverse, inverse


def norm_back(gradient, xhat, inverse):
    return inverse * (
        gradient
        - jnp.mean(gradient, axis=-1, keepdims=True)
        - xhat * jnp.mean(gradient * xhat, axis=-1, keepdims=True)
    )


def unit_parts(values):
    inverse = lax.rsqrt(jnp.sum(values * values, axis=-1, keepdims=True) + epsilon_unit)
    return values * inverse, inverse


def unit_back(gradient, unit, inverse):
    return inverse * (gradient - unit * jnp.sum(unit * gradient, axis=-1, keepdims=True))


def adamw_update(current, gradient, mean_old, square_old, step_scale, decay_rate):
    mean_new = first_decay * mean_old + (1.0 - first_decay) * gradient
    square_new = second_decay * square_old + (1.0 - second_decay) * gradient * gradient
    moved = mean_new / first_fix / (jnp.sqrt(square_new / second_fix) + adam_epsilon)
    return (step_scale * (moved + decay_rate * current), mean_new)


def places():
    dp = lax.axis_index("dp")
    tensor = lax.axis_index("tensor")
    core = dp % 2
    col = (dp // 2) % 2
    row = dp // 4
    over_x = dp + 2 * (1 - 2 * col)
    over_y = dp + 4 * (1 - 2 * row)
    sibling = dp + 1 - 2 * core
    return dp, tensor, over_x, over_y, sibling


def greet():
    dp, tensor, over_x, over_y, sibling = places()
    barrier = pltpu.get_barrier_semaphore()
    targets = [(over_x, tensor), (over_y, tensor), (sibling, tensor)]
    targets += [(dp, (tensor + j) % 4) for j in (1, 2, 3)]
    for target in targets:
        pl.semaphore_signal(barrier, inc=1, device_id=target, device_id_type=MESH)
    pl.semaphore_wait(barrier, 6)


def remote(source, target_ref, sends, receives, device):
    return pltpu.make_async_remote_copy(
        src_ref=source,
        dst_ref=target_ref,
        send_sem=sends,
        recv_sem=receives,
        device_id=device,
        device_id_type=MESH,
    )


def gather_kernel(count, *refs):
    shards, fulls = refs[:count], refs[count : 2 * count]
    sends, receives = refs[2 * count :]
    dp, tensor, over_x, over_y, sibling = places()
    across = over_x + over_y - dp
    greet()

    def copy(w, k):
        full = fulls[w]
        if full.shape[0] == 8:
            half = full.shape[1] // 2
            own = full.at[dp]
            views = {3: own, 4: own, 5: own}
            views[6] = full.at[over_x, 0:half]
            views[7] = full.at[over_y, half : 2 * half]
            views[8], views[9], views[10] = (full.at[d] for d in (over_x, over_y, across))
        else:
            own = full.at[:, dp]
            views = {k: full.at[tensor, dp] for k in (0, 1, 2)}
            views.update({3: own, 4: own, 5: own})
            views[6] = full.at[0:2, over_x]
            views[7] = full.at[2:4, over_y]
            views[8], views[9], views[10] = (full.at[:, d] for d in (over_x, over_y, across))
        target = {
            0: (dp, (tensor + 1) % 4),
            1: (dp, (tensor + 2) % 4),
            2: (dp, (tensor + 3) % 4),
            3: (over_x, tensor),
            4: (over_y, tensor),
            5: (sibling, tensor),
            6: (over_y, tensor),
            7: (over_x, tensor),
            8: (sibling, tensor),
            9: (sibling, tensor),
            10: (sibling, tensor),
        }[k]
        return remote(views[k], views[k], sends.at[w, k], receives.at[w, k], target)

    for w in range(count):
        if fulls[w].shape[0] == 8:
            fulls[w][dp] = shards[w][...]
        else:
            fulls[w][tensor, dp] = shards[w][...]
            for k in (0, 1, 2):
                copy(w, k).start()
    for stage in range(count + 3):
        w = stage
        if w < count:
            if fulls[w].shape[0] != 8:
                for k in (0, 1, 2):
                    copy(w, k).wait_recv()
            for k in (3, 4, 5):
                copy(w, k).start()
        w = stage - 1
        if 0 <= w < count:
            copy(w, 3).wait_recv()
            copy(w, 6).start()
            copy(w, 8).start()
            copy(w, 4).wait_recv()
            copy(w, 7).start()
            copy(w, 9).start()
        w = stage - 2
        if 0 <= w < count:
            copy(w, 6).wait_recv()
            copy(w, 7).wait_recv()
            copy(w, 10).start()
        w = stage - 3
        if 0 <= w < count:
            for k in (5, 8, 9, 10):
                copy(w, k).wait_recv()
    for w in range(count):
        for k in range(3 if fulls[w].shape[0] == 8 else 0, 11):
            copy(w, k).wait_send()


def gather_call(shards, embed):
    operands = list(shards) + [embed]
    count = len(operands)
    outs = [jax.ShapeDtypeStruct((4, 8) + s.shape, BF) for s in shards]
    outs.append(jax.ShapeDtypeStruct((8,) + embed.shape, BF))
    return pl.pallas_call(
        functools.partial(gather_kernel, count),
        out_shape=outs,
        in_specs=[pl.BlockSpec(memory_space=pltpu.VMEM)] * count,
        out_specs=[pl.BlockSpec(memory_space=pltpu.VMEM)] * count,
        scratch_shapes=[pltpu.SemaphoreType.DMA((count, 11))] * 2,
        compiler_params=pltpu.CompilerParams(
            collective_id=0, has_side_effects=True, vmem_limit_bytes=60 << 20
        ),
    )(*operands)


def scatter_kernel(count, *refs):
    grads, outs = refs[:count], refs[count : 2 * count]
    scratch = refs[2 * count :]
    sends, receives = scratch[-2:]
    bufs = [scratch[6 * w : 6 * w + 6] for w in range(count)]
    dp, tensor, over_x, over_y, sibling = places()
    core, col, row = dp % 2, (dp // 2) % 2, dp // 4
    greet()

    def copy(w, k):
        g = grads[w]
        r1, r2a, r2b, r3a, r3b, r4 = bufs[w]
        if k == 0:
            pair = (g.at[:, :, :, 1 - core], r1, (sibling, tensor))
        elif k == 1:
            pair = (r1.at[0:2, :, 1 - col], r2a, (over_x, tensor))
        elif k == 2:
            pair = (r1.at[2:4, 1 - row], r2b, (over_y, tensor))
        elif k == 3:
            pair = (r1.at[0:2, 1 - row, col], r3a, (over_y, tensor))
        elif k == 4:
            pair = (r1.at[2:4, row, 1 - col], r3b, (over_x, tensor))
        else:
            j = k - 4
            peer = (tensor + j) % 4
            pair = (r1.at[peer, row, col], r4.at[j - 1], (dp, peer))
        return remote(pair[0], pair[1], sends.at[w, k], receives.at[w, k], pair[2])

    def add(ref, index, other):
        ref[index] = (ref[index].astype(F32) + other.astype(F32)).astype(BF)

    for w in range(count):
        copy(w, 0).start()
    for stage in range(count + 3):
        w = stage
        if w < count:
            copy(w, 0).wait_recv()
            r1 = bufs[w][0]
            for t in range(4):
                add(r1, t, grads[w][t, :, :, core])
            copy(w, 1).start()
            copy(w, 2).start()
        w = stage - 1
        if 0 <= w < count:
            r1, r2a, r2b, r3a, r3b, r4 = bufs[w]
            copy(w, 1).wait_recv()
            for t in range(2):
                for y in range(2):
                    add(r1, (t, y, col), r2a[t, y])
            copy(w, 3).start()
            copy(w, 2).wait_recv()
            for t in range(2):
                for x in range(2):
                    add(r1, (2 + t, row, x), r2b[t, x])
            copy(w, 4).start()
        w = stage - 2
        if 0 <= w < count:
            r1, r2a, r2b, r3a, r3b, r4 = bufs[w]
            copy(w, 3).wait_recv()
            for t in range(2):
                add(r1, (t, row, col), r3a[t])
            copy(w, 4).wait_recv()
            for t in range(2):
                add(r1, (2 + t, row, col), r3b[t])
            for j in (1, 2, 3):
                copy(w, 4 + j).start()
        w = stage - 3
        if 0 <= w < count:
            r1, r4 = bufs[w][0], bufs[w][5]
            for j in (1, 2, 3):
                copy(w, 4 + j).wait_recv()
            total = r1[tensor, row, col].astype(F32)
            for j in range(3):
                total = total + r4[j].astype(F32)
            outs[w][...] = total
    for w in range(count):
        for k in range(8):
            copy(w, k).wait_send()


def scatter_call(grads):
    count = len(grads)
    grads = [g.reshape(4, 2, 2, 2, 96, g.shape[-1]) for g in grads]
    scratch = []
    for g in grads:
        c = g.shape[-1]
        scratch += [
            pltpu.VMEM((4, 2, 2, 96, c), BF),
            pltpu.VMEM((2, 2, 96, c), BF),
            pltpu.VMEM((2, 2, 96, c), BF),
            pltpu.VMEM((2, 96, c), BF),
            pltpu.VMEM((2, 96, c), BF),
            pltpu.VMEM((3, 96, c), BF),
        ]
    return pl.pallas_call(
        functools.partial(scatter_kernel, count),
        out_shape=[jax.ShapeDtypeStruct((96, g.shape[-1]), F32) for g in grads],
        in_specs=[pl.BlockSpec(memory_space=pltpu.VMEM)] * count,
        out_specs=[pl.BlockSpec(memory_space=pltpu.VMEM)] * count,
        scratch_shapes=scratch + [pltpu.SemaphoreType.DMA((count, 8))] * 2,
        compiler_params=pltpu.CompilerParams(
            collective_id=1, has_side_effects=True, vmem_limit_bytes=60 << 20
        ),
    )(*grads)


def gather_plain(shards, embed):
    def full(s):
        return lax.all_gather(lax.all_gather(s, "dp", axis=0), "tensor", axis=0)

    return [full(s) for s in shards] + [lax.all_gather(embed, "dp", axis=0)]


def scatter_plain(grads):
    def share(g):
        part = lax.psum_scatter(g, "dp", scatter_dimension=1, tiled=True)
        return lax.psum_scatter(part, "tensor", scatter_dimension=0, tiled=True)[0]

    return [share(g).astype(F32) for g in grads]


def with_halo(rows, parts):
    forward = [(i, i + 1) for i in range(parts - 1)]
    backward = [(i + 1, i) for i in range(parts - 1)]
    before = lax.ppermute(rows[-HALO:], "tensor", forward)
    after = lax.ppermute(rows[:HALO], "tensor", backward)
    return jnp.concatenate((before, rows, after), axis=0)


def local(
    custom,
    parts,
    tokens,
    segments,
    mask_grad,
    gain_one,
    attend_weight,
    output_weight,
    gain_two,
    up_weight,
    down_weight,
    patch_weight,
    class_weight,
    class_embed,
    *moments,
):
    means, squares = moments[:9], moments[9:]
    own = tokens.shape[0]
    width = tokens.shape[1]
    classes = class_embed.shape[0]
    dp_index = lax.axis_index("dp")
    tensor_index = lax.axis_index("tensor")
    low = lambda v: v.astype(BF)

    shard_a = jnp.concatenate((low(attend_weight), low(output_weight).T), axis=1)
    shard_u = low(up_weight)
    shard_d = low(down_weight).T
    shard_p = jnp.concatenate((low(patch_weight), low(class_weight)), axis=1)
    rows_e = -(-(classes + 2) // 32) * 32
    shard_e = jnp.zeros((rows_e, class_embed.shape[1]), BF)
    shard_e = shard_e.at[:classes].set(low(class_embed))
    shard_e = shard_e.at[classes].set(low(gain_one)).at[classes + 1].set(low(gain_two))
    gather = gather_call if custom else gather_plain
    full_a, full_u, full_d, full_p, full_e = gather(
        (shard_a, shard_u, shard_d, shard_p), shard_e
    )
    full_a, full_u, full_d, full_p = (
        v.reshape(v.shape[0], width, v.shape[-1]) for v in (full_a, full_u, full_d, full_p)
    )
    embed_rows = full_e.transpose(1, 0, 2).reshape(rows_e, width)
    embed = embed_rows[:classes]
    gain_first = embed_rows[classes].astype(F32)[None]
    gain_second = embed_rows[classes + 1].astype(F32)[None]

    cut = attend_weight.shape[1]
    heads = cut // (3 * HD)
    w_attend, w_output = full_a[:, :, :cut], full_a[:, :, cut:]
    narrow = patch_weight.shape[1]
    w_patch, w_class = full_p[:, :, :narrow], full_p[:, :, narrow:]
    w_patch = w_patch.transpose(1, 0, 2).reshape(width, -1)
    w_class = w_class.transpose(1, 0, 2).reshape(width, -1)

    window = with_halo(tokens, parts)
    token_wide = window.astype(F32)
    xhat_one, inverse_one = norm_parts(token_wide)
    norm_one = low(xhat_one * gain_first)
    joint = jnp.einsum("sd,tdn->stn", norm_one, w_attend, preferred_element_type=F32)
    joint = low(joint).reshape(own + 2 * HALO, parts * heads, 3, HD)
    queries, keys, values = joint[:, :, 0], joint[:, :, 1], joint[:, :, 2]
    padded = jnp.pad(segments[0], HALO, constant_values=-1)
    seg = lax.dynamic_slice_in_dim(padded, tensor_index * own, own + 2 * HALO, 0)
    scores = jnp.einsum("qhd,khd->hqk", queries, keys, preferred_element_type=F32) * HD**-0.5
    scores = jnp.where(seg[None, :, None] == seg[None, None, :], scores, masked_score)
    exponent = jnp.exp(scores - jnp.max(scores, axis=-1, keepdims=True))
    prob = exponent / jnp.sum(exponent, axis=-1, keepdims=True)
    prob_low = low(prob)
    mine = slice(HALO, HALO + own)
    attended = jnp.einsum(
        "hqk,khd->qhd", prob_low[:, mine], values, preferred_element_type=F32
    )
    attended = low(attended).reshape(own, parts, heads * HD)
    resid_one = token_wide[mine] + jnp.einsum(
        "stn,tdn->sd", attended, w_output, preferred_element_type=F32
    )
    xhat_two, inverse_two = norm_parts(resid_one)
    norm_two = low(xhat_two * gain_second)
    hidden_pre = jnp.einsum("sd,tdn->stn", norm_two, full_u, preferred_element_type=F32)
    hidden, gelu_back = jax.vjp(lambda v: jax.nn.gelu(v, approximate=False), hidden_pre)
    hidden = low(hidden)
    resid_two = resid_one + jnp.einsum(
        "stn,tdn->sd", hidden, full_d, preferred_element_type=F32
    )
    resid_low = low(resid_two)
    patch_feat = dot(resid_low, w_patch)
    patch_wide, patch_inverse = unit_parts(patch_feat)
    patch_unit = low(patch_wide)
    class_feat = dot(embed, w_class)
    class_wide, class_inverse = unit_parts(class_feat)
    class_unit = low(class_wide)
    products = dot(patch_unit, class_unit, ((1,), (1,)))
    masks, mask_inverse = norm_parts(products)
    d_products = low(norm_back(mask_grad, masks, mask_inverse))
    d_class_unit = lax.psum(dot(d_products, patch_unit, ((0,), (0,))), ("dp", "tensor"))
    d_patch_unit = dot(d_products, class_unit)
    d_patch_feat = low(unit_back(d_patch_unit, patch_wide, patch_inverse))
    grad_patch = dot(resid_low, d_patch_feat, ((0,), (0,)))
    d_resid_two = dot(d_patch_feat, w_patch, ((1,), (1,)))
    d_branch_two = low(d_resid_two)
    d_hidden = jnp.einsum("sd,tdn->stn", d_branch_two, full_d, preferred_element_type=F32)
    grad_down = jnp.einsum("sd,stn->tdn", d_branch_two, hidden, preferred_element_type=F32)
    d_hidden_pre = low(gelu_back(d_hidden)[0])
    grad_up = jnp.einsum("sd,stn->tdn", norm_two, d_hidden_pre, preferred_element_type=F32)
    d_norm_two = jnp.einsum("stn,tdn->sd", d_hidden_pre, full_u, preferred_element_type=F32)
    d_resid_one = d_resid_two + norm_back(d_norm_two * gain_second, xhat_two, inverse_two)
    grad_gain_two = jnp.sum(d_norm_two * xhat_two, axis=0)
    d_branch_one = with_halo(low(d_resid_one), parts)
    d_attended = low(
        jnp.einsum("sd,tdn->stn", d_branch_one, w_output, preferred_element_type=F32)
    )
    grad_output = jnp.einsum(
        "sd,stn->tdn", d_branch_one[mine], attended, preferred_element_type=F32
    )
    d_attended = d_attended.reshape(own + 2 * HALO, parts * heads, HD)
    d_prob = jnp.einsum("qhd,khd->hqk", d_attended, values, preferred_element_type=F32)
    delta = jnp.sum(prob * d_prob, axis=-1, keepdims=True)
    d_scores = low(prob * (d_prob - delta))
    d_query = jnp.einsum(
        "hqk,khd->qhd", d_scores[:, mine], keys, preferred_element_type=F32
    )
    d_key = jnp.einsum(
        "hqk,qhd->khd", d_scores[:, :, mine], queries, preferred_element_type=F32
    )
    d_value = jnp.einsum(
        "hqk,qhd->khd", prob_low[:, :, mine], d_attended, preferred_element_type=F32
    )
    d_joint = low(
        jnp.stack((d_query * HD**-0.5, d_key * HD**-0.5, d_value), axis=2)
    ).reshape(own, parts, cut)
    grad_attend = jnp.einsum(
        "sd,stn->tdn", norm_one[mine], d_joint, preferred_element_type=F32
    )
    d_norm_one = jnp.einsum("stn,tdn->sd", d_joint, w_attend, preferred_element_type=F32)
    token_grad = d_resid_one + norm_back(
        d_norm_one * gain_first, xhat_one[mine], inverse_one[mine]
    )
    grad_gain_one = jnp.sum(d_norm_one * xhat_one[mine], axis=0)

    grad_patch = grad_patch.reshape(width, parts, narrow).transpose(1, 0, 2)
    scatter = scatter_call if custom else scatter_plain
    share_p, share_d, share_u, share_a = scatter(
        [
            low(grad_patch),
            low(grad_down),
            low(grad_up),
            low(jnp.concatenate((grad_attend, grad_output), axis=2)),
        ]
    )
    gains = lax.psum((grad_gain_one, grad_gain_two), ("dp", "tensor"))
    step = gain_one.shape[0]
    share_one, share_two = (lax.dynamic_slice_in_dim(g, dp_index * step, step, 0) for g in gains)
    d_class_feat = low(unit_back(d_class_unit, class_wide, class_inverse))
    d_class_own = lax.dynamic_slice_in_dim(d_class_feat, tensor_index * narrow, narrow, 1)
    share_class = dot(low(class_embed), d_class_own, ((0,), (0,)))
    class_rows = lax.dynamic_slice_in_dim(w_class, dp_index * step, step, 0)
    share_embed = dot(d_class_feat, class_rows, ((1,), (1,)))
    grads = (
        share_one,
        share_a[:, :cut],
        share_a[:, cut:].T,
        share_two,
        share_u,
        share_d.T,
        share_p,
        share_class,
        share_embed,
    )
    params = (
        gain_one,
        attend_weight,
        output_weight,
        gain_two,
        up_weight,
        down_weight,
        patch_weight,
        class_weight,
        class_embed,
    )
    scales = (block_scale,) * 6 + (1.0,) * 3
    decays = (0.0, weight_decay, weight_decay, 0.0) + (weight_decay,) * 5
    new = [adamw_update(*v) for v in zip(params, grads, means, squares, scales, decays)]
    return (masks, token_grad) + tuple(n[0] for n in new) + tuple(n[1] for n in new)


def solution(mesh):
    parts = mesh.shape["tensor"]
    custom = mesh.shape["dp"] == 8 and parts == 4
    params = (
        P("dp"),
        P("dp", "tensor"),
        P("tensor", "dp"),
        P("dp"),
        P("dp", "tensor"),
        P("tensor", "dp"),
        P("dp", "tensor"),
        P("dp", "tensor"),
        P(None, "dp"),
    )
    rows = P(("dp", "tensor"), None)
    return jax.shard_map(
        functools.partial(local, custom, parts),
        mesh=mesh,
        in_specs=(rows, P("dp", None), rows) + params * 3,
        out_specs=(rows, rows) + params * 2,
        check_vma=False,
    )
```

time: 755 us -> 438 us (0.58)
  waiting for transfers between devices: 457 us -> 0.03 us
  Pallas kernels: 0 us -> 194 us
  blocking collectives: 102 us -> 40.2 us
  local copies, waits for them, and re-layouts: 13.7 us -> 32.1 us
  starting transfers between devices: 1.24 us -> 17.4 us
  matrix products: 89.4 us -> 76.5 us
  loops' own time: 12.1 us -> 0 us
    pallas_call x0 -> x2, Pallas kernels: none -> 194 us  [the longest x1 100 us: gather_call(): pl.pallas_call(functools.partial(gather_kernel, count), out_shape=outs, i...]
    all_gather x8 -> x0, waiting for transfers between devices: 165 us -> none  [the longest x1 36.4 us: local(): lax.all_gather(d_resid_two.astype(low_type), 'tensor', axis=0, tiled=True)]
    reduce_scatter x4 -> x0, waiting for transfers between devices: 153 us -> none  [the longest x1 59.9 us: local(): lax.psum_scatter(jnp.dot(hidden, down_full, preferred_element_type=jnp.fl...]
    psum x2 -> x1, waiting for transfers between devices: 139 us -> 0.01 us  [local(): lax.psum(dot(d_products, patch_unit, ((0,), (0,))), ('dp', 'tensor'))]
    all_gather x5 -> x0, blocking collectives: 47.3 us -> none  [the longest x1 11.1 us: local(): lax.all_gather(attend_weight.astype(low_type), 'dp', axis=0, tiled=True)]
    dot_general x35 -> x24, matrix products: 89.4 us -> 51.5 us  [the longest x9 8.09 us: dot(): lax.dot_general(left, right, (dims, ((), ())), preferred_element_type=F32)]
    sub x0 -> x2, matrix products: none -> 24.2 us  [the longest x1 13.7 us: local(): d_scores = low(prob * (d_prob - delta))]
    ppermute x0 -> x4, starting transfers between devices: none -> 17.4 us  [the longest x2 14.8 us: with_halo(): before = lax.ppermute(rows[-HALO:], 'tensor', forward)]
  transfers between devices with their start and end apart: 14 -> 5, of which waited for: 12 -> 0; matrix products, arithmetic and copies ran while one was open for 13% -> 20% of each run, Pallas kernels for 0% -> 45%
where the time goes in v1:
time: 438 us; the launch traced here: 431 us
  Pallas kernels  194 us (44%)
  matrix products  76.5 us (17%)
  other arithmetic  54.7 us (12%)
  blocking collectives  40.2 us (9%)
  local copies, waits for them, and re-layouts  32.1 us (7%)
  starting transfers between devices  17.4 us (4%)
  between operations  15.2 us (3%)
    pallas_call x1, Pallas kernels, gather_call(): pl.pallas_call(functools.partial(gather_kernel, count), out_shape=outs, i...  100 us
    pallas_call x1, Pallas kernels, scatter_call(): pl.pallas_call(functools.partial(scatter_kernel, count), out_shape=[jax.S...  94.1 us
    psum x1, blocking collectives, local(): gains = lax.psum((grad_gain_one, grad_gain_two), ('dp', 'tensor'))  40.2 us
    convert_element_type x12, other arithmetic, local(): low = lambda v: v.astype(BF)  24.3 us
    unnamed x121, local copies, waits for them, and re-layouts  15.5 us
    ppermute x2, starting transfers between devices, with_halo(): before = lax.ppermute(rows[-HALO:], 'tensor', forward)  14.8 us
    sub x1, matrix products, local(): d_scores = low(prob * (d_prob - delta))  13.7 us
    sub x1, matrix products, local(): exponent = jnp.exp(scores - jnp.max(scores, axis=-1, keepdims=True))  10.5 us
  transfers between devices with their start and end apart: 5, of which 0 were waited for; matrix products, arithmetic and copies ran while one was open for 20% of the time, Pallas kernels for 45%

profile of v1, /device:TPU:0, one launch (start us, length us, event | category | flops | bytes accessed | tf_op | source)
XLA Modules:
  0.0 430.5 jit_solution(9384982355460615084)
XLA Ops:
  10.3 6.3 %collective-permute-start = (bf16[128,768]{1,0:T(8,128)(2,1)}, bf16[128,768]{1,0:T(8,128)(2,1)}, u32[]{:S(2)}, u32[]{:S(2)}) collective-permute-start(bf16[128,768]{1,0:T(8,128)(2,1)} %get-tuple-element.157), channel_id=1, source_target_pairs={{0,1},{1,2},{2,3},{4,5},{5,6},{6,7},{8,9},{9,10},{10,11},{12,13},{... | collective-permute-start | bytes 589832 | tf_op jit(solution)/shard_map/ppermute | solution.py:318
  28.0 100.2 %shard_map.437 = (bf16[4,8,96,768]{3,2,1,0:T(8,128)(2,1)}, bf16[4,8,96,768]{3,2,1,0:T(8,128)(2,1)}, bf16[4,8,96,768]{3,2,1,0:T(8,128)(2,1)}, bf16[4,8,96,384]{3,2,1,0:T(8,128)(2,1)}, bf16[8,160,96]{2,1,0:T(8,128)(2,1)}) custom-call(bf16[96,768]{1,0:T(8,128)(2,1)} %pad_maximum_fusion.3.refs_0_, bf16[96,768]{1,0:T(8,128)(2,1)} %convert_element_type.136.refs_1_, ...), custom_call_target="tpu_custom_call" | custom-call | tf_op jit(solution)/shard_map/pallas_call | solution.py:182
  131.2 3.8 fusion.160
  135.0 2.5 copy.111
  139.3 3.4 slice.157
  142.7 2.7 copy.109
  151.1 2.4 subtract_multiply_fusion
  153.5 5.9 %fusion.27 = bf16[512,4,576]{0,2,1:T(8,128)(2,1)} fusion(bf16[4,768,768]{2,1,0:T(8,128)(2,1)} %bitcast.197, bf16[512,768]{1,0:T(8,128)(2,1)S(1)} %get-tuple-element.154), kind=kOutput, calls=%fused_computation.49 | convolution fusion | flops 1813118976 | bytes 7077888 | tf_op jit(solution)/shard_map/sd,tdn->stn/dot_general | solution.py:380
  159.4 10.5 %fusion.163 = (f32[12,512]{1,0:T(8,128)S(1)}, f32[12,512,512]{1,2,0:T(8,128)}) fusion(pred[512,512]{0,1:T(8,128)(4,1)S(1)} %copy-done.25, bf16[512,12,3,64]{0,3,2,1:T(8,128)(2,1)} %bitcast.215), kind=kOutput, calls=%fused_computation.238 | convolution fusion | flops 415236608 | bytes 14442496 | tf_op jit(solution)/shard_map/sub | solution.py:387
  169.9 9.0 %fusion.154 = bf16[12,512,512]{1,2,0:T(8,128)(2,1)} fusion(f32[12,512,512]{1,2,0:T(8,128)} %get-tuple-element.162, f32[12,512]{1,0:T(8,128)S(1)} %get-tuple-element.161), kind=kLoop, calls=%fused_computation.232 | loop fusion | flops 6291456 | bytes 18898944 | tf_op jit(solution)/shard_map/convert_element_type | solution.py:346
  178.9 2.8 fusion.52
  182.7 2.8 fusion.164
  185.7 4.7 %fusion.75 = (u8[256,768]{1,0:T(8,128)(4,1)S(1)}, u8[256,768]{1,0:T(8,128)(4,1)S(1)}, f32[256,4,768]{2,0,1:T(8,128)S(1)}) fusion(bf16[4,768,768]{2,1,0:T(8,128)(2,1)} %bitcast.207, f32[256,768]{1,0:T(8,128)S(1)} %get-tuple-element.164, f32[768]{0:T(1024)S(1)} %reshape.320, f32[256]{0:T(256)S(1)} %add_rsqrt_fusion.4, f32[256]{0:T(256)S(1)} %broadcast_multiply_fusion.8), kind=kOutput, calls=%fused_computation.100 | convolution fusion | flops 1218576384 | bytes 9049088 | tf_op jit(solution)/shard_map/sd,tdn->stn/dot_general | solution.py:400
  190.4 7.2 %multiply_convert_fusion.1 = (bf16[256,4,768]{2,0,1:T(8,128)(2,1)S(1)}, f32[256,4,768]{2,0,1:T(8,128)S(1)}) fusion(f32[256,4,768]{2,0,1:T(8,128)S(1)} %get-tuple-element.165, u8[256,768]{1,0:T(8,128)(4,1)S(1)} %get-tuple-element.115, u8[256,768]{1,0:T(8,128)(4,1)S(1)} %get-tuple-element.114), kind=kLoop, calls=%fused_computation.34 | loop fusion | flops 55050240 | bytes 8257536 | tf_op jit(solution)/shard_map/convert_element_type | solution.py:346
  202.6 3.7 convolution_convert_fusion.1
  208.2 2.1 multiply_reduce_fusion.2
  210.3 3.6 convolution_convert_fusion
  218.0 8.6 %collective-permute-start.2 = (bf16[128,768]{1,0:T(8,128)(2,1)S(1)}, bf16[128,768]{1,0:T(8,128)(2,1)S(1)}, u32[]{:S(2)}, u32[]{:S(2)}) collective-permute-start(bf16[128,768]{1,0:T(8,128)(2,1)S(1)} %get-tuple-element.155), channel_id=1, source_target_pairs={{0,1},{1,2},{2,3},{4,5},{5,6},{6,7},{8,9},{9,10},{10,11},{12,13},{... | collective-permute-start | bytes 589832 | tf_op jit(solution)/shard_map/ppermute | solution.py:318
  228.5 2.6 copy.89
  233.3 3.0 fusion.58
  236.2 13.7 %multiply_convert_fusion = bf16[12,512,512]{1,2,0:T(8,128)(2,1)} fusion(bf16[512,12,64]{0,2,1:T(8,128)(2,1)S(1)} %bitcast.195, bf16[512,12,3,64]{0,3,2,1:T(8,128)(2,1)} %bitcast.217, f32[12,512,512]{1,2,0:T(8,128)} %get-tuple-element.162, f32[12,512]{1,0:T(8,128)S(1)} %get-tuple-element.161), kind=kOutput, calls=%fused_computation.2 | convolution fusion | flops 824187392 | bytes 34668544 | tf_op jit(solution)/shard_map/sub | solution.py:439
  249.9 3.4 fusion.64
  253.3 2.8 fusion.61
  258.4 2.8 multiply_reduce_fusion.3
  261.8 4.0 copy.88
  265.7 40.2 %all-reduce.2 = (f32[768]{0:T(1024)S(1)}, f32[768]{0:T(1024)S(1)}) all-reduce(f32[768]{0:T(1024)} %get-tuple-element.116, f32[768]{0:T(1024)} %get-tuple-element.118), channel_id=1, replica_groups=mesh['dp'=8,'tensor'=4] {'dp','tensor'}, use_global_device_ids=true, to_apply=%region_19.20 | all-reduce | flops 1536 | bytes 12288 | tf_op jit(solution)/shard_map/psum | solution.py:471
  305.9 5.8 %pad_maximum_fusion.refs_3_ = bf16[4,2,2,2,96,768]{5,4,3,2,1,0:T(8,128)(2,1)} fusion(bf16[4,2,2,2,96,192]{5,4,3,2,1,0:T(8,128)(2,1)} %bitcast.184, bf16[4,2,2,2,96,576]{5,4,3,2,1,0:T(8,128)(2,1)} %bitcast.181), kind=kLoop, calls=%fused_computation.13 | loop fusion | flops 9437184 | bytes 9437184 | tf_op jit(solution)/shard_map/concatenate | solution.py:468
  311.8 94.1 %shard_map.438 = (f32[96,192]{1,0:T(8,128)}, f32[96,768]{1,0:T(8,128)}, f32[96,768]{1,0:T(8,128)}, f32[96,768]{1,0:T(8,128)}) custom-call(bf16[4,2,2,2,96,192]{5,4,3,2,1,0:T(8,128)(2,1)} %bitcast.185, bf16[4,2,2,2,96,768]{5,4,3,2,1,0:T(8,128)(2,1)} %bitcast.180, bf16[4,2,2,2,96,768]{5,4,3,2,1,0:T(8,128)(2,1)} %bitcast.179, ...), custom_call_target="tpu_custom_call" | custom-call | tf_op jit(solution)/shard_map/pallas_call | solution.py:288
  406.1 2.0 fusion.103
  409.2 2.0 fusion.96
  411.3 2.1 fusion.95
  420.5 2.0 fusion.133
  (201 shorter events, 52.9 us)
Async XLA Ops:
  7.2 410.9 %all-reduce.5.cloned.1.call-start = ((), (), s32[]{:S(2)}) async-start(), calls=%async_computation | async-start | bytes 933888 | tf_op jit(solution)/shard_map/psum | solution.py:416
  9.0 139.5 %collective-permute-start.1 = (bf16[128,768]{1,0:T(8,128)(2,1)}, bf16[128,768]{1,0:T(8,128)(2,1)S(1)}, u32[]{:S(2)}, u32[]{:S(2)}) collective-permute-start(bf16[128,768]{1,0:T(8,128)(2,1)} %get-tuple-element.158), channel_id=1, source_target_pairs={{1,0},{2,1},{3,2},{5,4},{6,5},{7,6},{9,8},{10,9},{11,10},{13,12},{... | collective-permute-start | bytes 589832 | tf_op jit(solution)/shard_map/ppermute | solution.py:319
  10.3 138.2 %collective-permute-start = (bf16[128,768]{1,0:T(8,128)(2,1)}, bf16[128,768]{1,0:T(8,128)(2,1)}, u32[]{:S(2)}, u32[]{:S(2)}) collective-permute-start(bf16[128,768]{1,0:T(8,128)(2,1)} %get-tuple-element.157), channel_id=1, source_target_pairs={{0,1},{1,2},{2,3},{4,5},{5,6},{6,7},{8,9},{9,10},{10,11},{12,13},{... | collective-permute-start | bytes 589832 | tf_op jit(solution)/shard_map/ppermute | solution.py:318
  17.6 110.7 %copy-start.13 = (f32[192,96]{0,1:T(8,128)}, f32[192,96]{0,1:T(8,128)S(1)}, u32[]{:S(2)}) copy-start(f32[192,96]{0,1:T(8,128)S(1)} %copy.71) | copy-start | bytes 221188
  24.5 105.6 %copy-start.29 = (bf16[150,96]{1,0:T(8,128)(2,1)}, bf16[150,96]{1,0:T(8,128)(2,1)S(1)}, u32[]{:S(2)}) copy-start(bf16[150,96]{1,0:T(8,128)(2,1)S(1)} %convert_element_type.140) | copy-start | bytes 86404
  139.3 7.6 %copy-start.3 = (bf16[4,768,192]{1,2,0:T(8,128)(2,1)S(1)}, bf16[4,768,192]{1,2,0:T(8,128)(2,1)}, u32[]{:S(2)}) copy-start(bf16[4,768,192]{1,2,0:T(8,128)(2,1)} %copy.111) | copy-start | bytes 3538948
  148.5 52.5 %copy-start = (f32[150,768]{1,0:T(8,128)}, f32[150,768]{1,0:T(8,128)S(1)}, u32[]{:S(2)}) copy-start(f32[150,768]{1,0:T(8,128)S(1)} %get-tuple-element.160) | copy-start | bytes 1382404
  182.7 14.9 %slice-start.4 = ((s8[4718592]{0:T(1024)(128)(4,1)}), s8[4194304]{0:T(1024)(128)(4,1)S(1)}, s32[]{:S(2)}) async-start(s8[4718592]{0:T(1024)(128)(4,1)} %bitcast.211), calls=%async_computation.5 | async-start | bytes 8388608
  185.7 11.9 %slice-start.5 = ((s8[4718592]{0:T(1024)(128)(4,1)}), s8[524288]{0:T(1024)(128)(4,1)S(1)}, s32[]{:S(2)}) async-start(s8[4718592]{0:T(1024)(128)(4,1)} %bitcast.211), calls=%async_computation.6 | async-start | bytes 1048576
  216.7 15.6 %collective-permute-start.3 = (bf16[128,768]{1,0:T(8,128)(2,1)S(1)}, bf16[128,768]{1,0:T(8,128)(2,1)S(1)}, u32[]{:S(2)}, u32[]{:S(2)}) collective-permute-start(bf16[128,768]{1,0:T(8,128)(2,1)S(1)} %get-tuple-element.156), channel_id=1, source_target_pairs={{1,0},{2,1},{3,2},{5,4},{6,5},{7,6},{9,8},{10,9},{11,10},{13,12},{... | collective-permute-start | bytes 589832 | tf_op jit(solution)/shard_map/ppermute | solution.py:319
  218.0 14.3 %collective-permute-start.2 = (bf16[128,768]{1,0:T(8,128)(2,1)S(1)}, bf16[128,768]{1,0:T(8,128)(2,1)S(1)}, u32[]{:S(2)}, u32[]{:S(2)}) collective-permute-start(bf16[128,768]{1,0:T(8,128)(2,1)S(1)} %get-tuple-element.155), channel_id=1, source_target_pairs={{0,1},{1,2},{2,3},{4,5},{5,6},{6,7},{8,9},{9,10},{10,11},{12,13},{... | collective-permute-start | bytes 589832 | tf_op jit(solution)/shard_map/ppermute | solution.py:318
  249.9 8.4 %slice-start = ((s8[4718592]{0:T(1024)(128)(4,1)}), s8[4194304]{0:T(1024)(128)(4,1)S(1)}, s32[]{:S(2)}) async-start(s8[4718592]{0:T(1024)(128)(4,1)} %bitcast.199), calls=%async_computation.1 | async-start | bytes 8388608
  311.8 94.3 %copy-start.12 = (f32[96,576]{1,0:T(8,128)S(1)}, f32[96,576]{1,0:T(8,128)}, u32[]{:S(2)}) copy-start(f32[96,576]{1,0:T(8,128)} %param.40) | copy-start | bytes 663556
  311.8 94.3 %copy-start.26 = (f32[96,576]{1,0:T(8,128)S(1)}, f32[96,576]{1,0:T(8,128)}, u32[]{:S(2)}) copy-start(f32[96,576]{1,0:T(8,128)} %param.58) | copy-start | bytes 663556
  311.8 94.3 %copy-start.27 = (f32[96,576]{1,0:T(8,128)S(1)}, f32[96,576]{1,0:T(8,128)}, u32[]{:S(2)}) copy-start(f32[96,576]{1,0:T(8,128)} %param.49) | copy-start | bytes 663556
  311.8 96.4 %copy-start.14 = (f32[192,96]{0,1:T(8,128)S(1)}, f32[192,96]{0,1:T(8,128)}, u32[]{:S(2)}) copy-start(f32[192,96]{0,1:T(8,128)} %copy-done.13) | copy-start | bytes 221188
  311.8 96.4 %copy-start.19 = (f32[192,96]{0,1:T(8,128)S(1)}, f32[192,96]{0,1:T(8,128)}, u32[]{:S(2)}) copy-start(f32[192,96]{0,1:T(8,128)} %copy.91) | copy-start | bytes 221188
  311.8 96.4 %copy-start.20 = (f32[192,96]{0,1:T(8,128)S(1)}, f32[192,96]{0,1:T(8,128)}, u32[]{:S(2)}) copy-start(f32[192,96]{0,1:T(8,128)} %copy.90) | copy-start | bytes 221188
  311.8 97.4 %copy-start.9 = (f32[96,768]{1,0:T(8,128)S(1)}, f32[96,768]{1,0:T(8,128)}, u32[]{:S(2)}) copy-start(f32[96,768]{1,0:T(8,128)} %param.43) | copy-start | bytes 884740
  311.8 97.4 %copy-start.21 = (f32[96,768]{1,0:T(8,128)S(1)}, f32[96,768]{1,0:T(8,128)}, u32[]{:S(2)}) copy-start(f32[96,768]{1,0:T(8,128)} %param.61) | copy-start | bytes 884740
  311.8 97.4 %copy-start.22 = (f32[96,768]{1,0:T(8,128)S(1)}, f32[96,768]{1,0:T(8,128)}, u32[]{:S(2)}) copy-start(f32[96,768]{1,0:T(8,128)} %param.52) | copy-start | bytes 884740
  311.8 99.5 %copy-start.24 = (f32[768,96]{0,1:T(8,128)S(1)}, f32[768,96]{0,1:T(8,128)}, u32[]{:S(2)}) copy-start(f32[768,96]{0,1:T(8,128)} %param.53) | copy-start | bytes 884740
  406.0 7.4 %copy-start.18 = (f32[96,192]{1,0:T(8,128)S(1)}, f32[96,192]{1,0:T(8,128)}, u32[]{:S(2)}) copy-start(f32[96,192]{1,0:T(8,128)} %param.45) | copy-start | bytes 221188
  406.0 7.4 %copy-start.31 = (f32[96,192]{1,0:T(8,128)S(1)}, f32[96,192]{1,0:T(8,128)}, u32[]{:S(2)}) copy-start(f32[96,192]{1,0:T(8,128)} %param.63) | copy-start | bytes 221188
  406.0 8.1 %copy-start.5 = (f32[512,768]{1,0:T(8,128)S(1)}, f32[512,768]{1,0:T(8,128)}, u32[]{:S(2)}) copy-start(f32[512,768]{1,0:T(8,128)} %get-tuple-element.153) | copy-start | bytes 4718596
  406.0 8.1 %copy-start.6 = (f32[256,768]{1,0:T(8,128)S(1)}, f32[256,768]{1,0:T(8,128)}, u32[]{:S(2)}) copy-start(f32[256,768]{1,0:T(8,128)} %get-tuple-element.147) | copy-start | bytes 2359300
  406.1 8.1 %copy-start.15 = (f32[256,768]{1,0:T(8,128)S(1)}, f32[256,768]{1,0:T(8,128)}, u32[]{:S(2)}) copy-start(f32[256,768]{1,0:T(8,128)} %get-tuple-element.173) | copy-start | bytes 2359300
  406.1 8.1 %copy-start.38 = (f32[256]{0:T(256)S(1)}, f32[256]{0:T(256)}, u32[]{:S(2)}) copy-start(f32[256]{0:T(256)} %broadcast_multiply_fusion.5) | copy-start | bytes 3076
  414.2 8.3 %copy-start.30 = (bf16[150,96]{1,0:T(8,128)(2,1)S(1)}, bf16[150,96]{1,0:T(8,128)(2,1)}, u32[]{:S(2)}) copy-start(bf16[150,96]{1,0:T(8,128)(2,1)} %copy-done.29) | copy-start | bytes 86404
  414.2 8.3 %copy-start.36 = (f32[96,192]{1,0:T(8,128)S(1)}, f32[96,192]{1,0:T(8,128)}, u32[]{:S(2)}) copy-start(f32[96,192]{1,0:T(8,128)} %param.46) | copy-start | bytes 221188
  414.2 8.3 %copy-start.46 = (f32[96,192]{1,0:T(8,128)S(1)}, f32[96,192]{1,0:T(8,128)}, u32[]{:S(2)}) copy-start(f32[96,192]{1,0:T(8,128)} %param.64) | copy-start | bytes 221188
  414.2 8.3 %copy-start.47 = (f32[96,192]{1,0:T(8,128)S(1)}, f32[96,192]{1,0:T(8,128)}, u32[]{:S(2)}) copy-start(f32[96,192]{1,0:T(8,128)} %param.55) | copy-start | bytes 221188
  (29 other events, 143.4 us)
Sparse Core Ops, SparseCore 0:
  232.4 125.7 all-reduce.4

commit v2 on v1

--- a/solution.py
+++ b/solution.py
@@ -12,6 +12,7 @@
 BF = jnp.bfloat16
 F32 = jnp.float32
 MESH = pl.DeviceIdType.MESH
+VMEM_LIMIT = 64 * 1024 * 1024 - 512 * 1024
 
 epsilon_norm = 1e-05
 epsilon_unit = 1e-06
@@ -99,202 +100,770 @@
     )
 
 
-def gather_kernel(count, *refs):
-    shards, fulls = refs[:count], refs[count : 2 * count]
-    sends, receives = refs[2 * count :]
-    dp, tensor, over_x, over_y, sibling = places()
-    across = over_x + over_y - dp
+def plain_copy(source, target, semaphore):
+    return pltpu.make_async_copy(source, target, semaphore)
+
+
+class Gather:
+    def __init__(self, full, sends, receives, w):
+        self.full, self.sends, self.receives, self.w = full, sends, receives, w
+        self.flat = full.shape[0] == 8
+
+    def copy(self, k):
+        dp, tensor, over_x, over_y, sibling = places()
+        across = over_x + over_y - dp
+        full = self.full
+        if k < 3:
+            view = full.at[tensor, dp]
+            target = (dp, (tensor + 1 + k) % 4)
+        elif k < 15:
+            j = (k - 3) // 3
+            view = full.at[dp] if self.flat else full.at[(tensor + j) % 4, dp]
+            target = ((over_x, over_y, sibling)[(k - 3) % 3], tensor)
+        elif k < 17:
+            other = over_x if k == 15 else over_y
+            if self.flat:
+                half = full.shape[1] // 2
+                view = full.at[other, pl.ds((k - 15) * half, half)]
+            else:
+                view = full.at[pl.ds((k - 15) * 2, 2), other]
+            target = (over_y if k == 15 else over_x, tensor)
+        else:
+            other = (over_x, over_y, across)[k - 17]
+            view = full.at[other] if self.flat else full.at[:, other]
+            target = (sibling, tensor)
+        return remote(view, view, self.sends.at[self.w, k], self.receives.at[self.w, k], target)
+
+    def pieces(self):
+        return range(1 if self.flat else 4)
+
+    def first(self, shard):
+        dp, tensor = places()[:2]
+        if self.flat:
+            self.full[dp] = shard[...]
+        else:
+            self.full[tensor, dp] = shard[...]
+            for k in range(3):
+                self.copy(k).start()
+        for k in (3, 4, 5):
+            self.copy(k).start()
+
+    def spread(self):
+        if not self.flat:
+            for j in (3, 2, 1):
+                self.copy(j - 1).wait_recv()
+                for k in range(3):
+                    self.copy(3 + 3 * (4 - j) + k).start()
+
+    def forward(self):
+        for j in self.pieces():
+            self.copy(3 + 3 * j).wait_recv()
+        self.copy(15).start()
+        self.copy(17).start()
+        for j in self.pieces():
+            self.copy(4 + 3 * j).wait_recv()
+        self.copy(16).start()
+        self.copy(18).start()
+
+    def across(self):
+        self.copy(15).wait_recv()
+        self.copy(16).wait_recv()
+        self.copy(19).start()
+
+    def last(self):
+        for j in self.pieces():
+            self.copy(5 + 3 * j).wait_recv()
+        for k in (17, 18, 19):
+            self.copy(k).wait_recv()
+
+    def drain(self):
+        if not self.flat:
+            for k in range(3):
+                self.copy(k).wait_send()
+        for j in self.pieces():
+            for k in range(3):
+                self.copy(3 + 3 * j + k).wait_send()
+        for k in range(15, 20):
+            self.copy(k).wait_send()
+
+
+def whole(value):
+    return value.reshape(value.shape[0] * value.shape[1], value.shape[2])
+
+
+def gelu_parts(values):
+    cumulative = 0.5 * (1.0 + lax.erf(values * 0.7071067811865476))
+    density = 0.3989422804014327 * jnp.exp(-0.5 * values * values)
+    return values * cumulative, cumulative + values * density
+
+
+HEAD_SET = 3
+SPAN = 3 * HD
+
+
+def forward_kernel(classes, *refs):
+    (tokens, seg_col, seg_row, mask_grad, shard_e, shard_a, shard_u, shard_d, shard_p) = refs[:9]
+    (masks_out, d_class_out, class_out, gains_out) = refs[9:13]
+    saves_out = refs[13:25]
+    scratch = refs[25:]
+    (
+        full_a,
+        full_u,
+        full_d,
+        full_p,
+        joint,
+        attended,
+        norm_two,
+        hidden,
+        slope,
+        d_resid,
+        grad_p,
+        resid_one,
+        full_e,
+        window,
+        norm_one,
+        embed,
+        feat,
+        unit_low,
+        class_low,
+        resid_low,
+        sends,
+        receives,
+        halo_sems,
+        save_sems,
+    ) = scratch
+    kept = (
+        full_a,
+        full_u,
+        full_d,
+        full_p,
+        joint,
+        attended,
+        norm_two,
+        hidden,
+        slope,
+        resid_one,
+        d_resid,
+        grad_p,
+    )
+
+    def save(n):
+        return plain_copy(kept[n], saves_out[n], save_sems.at[n])
+
+    dp, tensor = places()[:2]
+    own = tokens.shape[0]
+    span = own + 2 * HALO
     greet()
-
-    def copy(w, k):
-        full = fulls[w]
-        if full.shape[0] == 8:
-            half = full.shape[1] // 2
-            own = full.at[dp]
-            views = {3: own, 4: own, 5: own}
-            views[6] = full.at[over_x, 0:half]
-            views[7] = full.at[over_y, half : 2 * half]
-            views[8], views[9], views[10] = (full.at[d] for d in (over_x, over_y, across))
-        else:
-            own = full.at[:, dp]
-            views = {k: full.at[tensor, dp] for k in (0, 1, 2)}
-            views.update({3: own, 4: own, 5: own})
-            views[6] = full.at[0:2, over_x]
-            views[7] = full.at[2:4, over_y]
-            views[8], views[9], views[10] = (full.at[:, d] for d in (over_x, over_y, across))
-        target = {
-            0: (dp, (tensor + 1) % 4),
-            1: (dp, (tensor + 2) % 4),
-            2: (dp, (tensor + 3) % 4),
-            3: (over_x, tensor),
-            4: (over_y, tensor),
-            5: (sibling, tensor),
-            6: (over_y, tensor),
-            7: (over_x, tensor),
-            8: (sibling, tensor),
-            9: (sibling, tensor),
-            10: (sibling, tensor),
-        }[k]
-        return remote(views[k], views[k], sends.at[w, k], receives.at[w, k], target)
-
-    for w in range(count):
-        if fulls[w].shape[0] == 8:
-            fulls[w][dp] = shards[w][...]
-        else:
-            fulls[w][tensor, dp] = shards[w][...]
-            for k in (0, 1, 2):
-                copy(w, k).start()
-    for stage in range(count + 3):
-        w = stage
-        if w < count:
-            if fulls[w].shape[0] != 8:
-                for k in (0, 1, 2):
-                    copy(w, k).wait_recv()
-            for k in (3, 4, 5):
-                copy(w, k).start()
-        w = stage - 1
-        if 0 <= w < count:
-            copy(w, 3).wait_recv()
-            copy(w, 6).start()
-            copy(w, 8).start()
-            copy(w, 4).wait_recv()
-            copy(w, 7).start()
-            copy(w, 9).start()
-        w = stage - 2
-        if 0 <= w < count:
-            copy(w, 6).wait_recv()
-            copy(w, 7).wait_recv()
-            copy(w, 10).start()
-        w = stage - 3
-        if 0 <= w < count:
-            for k in (5, 8, 9, 10):
-                copy(w, k).wait_recv()
-    for w in range(count):
-        for k in range(3 if fulls[w].shape[0] == 8 else 0, 11):
-            copy(w, k).wait_send()
-
-
-def gather_call(shards, embed):
-    operands = list(shards) + [embed]
-    count = len(operands)
-    outs = [jax.ShapeDtypeStruct((4, 8) + s.shape, BF) for s in shards]
-    outs.append(jax.ShapeDtypeStruct((8,) + embed.shape, BF))
+    ge, ga, gu, gd, gp = (
+        Gather(full, sends, receives, w)
+        for w, full in enumerate((full_e, full_a, full_u, full_d, full_p))
+    )
+    ge.first(shard_e)
+    window[HALO : HALO + own] = tokens[...]
+    halo_before = remote(
+        window.at[pl.ds(HALO, HALO)],
+        window.at[pl.ds(HALO + own, HALO)],
+        halo_sems.at[0],
+        halo_sems.at[1],
+        (dp, (tensor + 3) % 4),
+    )
+    halo_after = remote(
+        window.at[pl.ds(own, HALO)],
+        window.at[pl.ds(0, HALO)],
+        halo_sems.at[2],
+        halo_sems.at[3],
+        (dp, (tensor + 1) % 4),
+    )
+    halo_before.start()
+    halo_after.start()
+    ga.first(shard_a)
+    gu.first(shard_u)
+    gd.first(shard_d)
+    gp.first(shard_p)
+    ge.forward()
+    ge.across()
+    ga.spread()
+    ge.last()
+    halo_before.wait_recv()
+    halo_after.wait_recv()
+    for d in range(8):
+        embed[:, d * 96 : (d + 1) * 96] = full_e[d]
+    gains = embed[classes : classes + 2, :].astype(F32)
+    gains_out[...] = gains
+    gain_first, gain_second = gains[0:1], gains[1:2]
+
+    def first_norm(i, carry):
+        rows = pl.ds(pl.multiple_of(i * 128, 128), 128)
+        xhat, _ = norm_parts(window[rows].astype(F32))
+        norm_one[rows] = (xhat * gain_first).astype(BF)
+        return carry
+
+    lax.fori_loop(0, span // 128, first_norm, 0)
+    gu.spread()
+    ga.forward()
+    ga.across()
+    gd.spread()
+    ga.last()
+    save(0).start()
+
+    def project(t, carry):
+        weight = whole(full_a[t])[:, : HEAD_SET * SPAN]
+        joint[t] = dot(norm_one[...], weight).astype(BF)
+        return carry
+
+    lax.fori_loop(0, 4, project, 0)
+    save(4).start()
+    gu.forward()
+
+    def attend(t, carry):
+        for h in range(HEAD_SET):
+            for b in range(own // 128):
+                near = slice(b * 128, b * 128 + 384)
+                query = joint[t, HALO + b * 128 : HALO + (b + 1) * 128, h * SPAN : h * SPAN + HD]
+                key = joint[t, near, h * SPAN + HD : h * SPAN + 2 * HD]
+                value = joint[t, near, h * SPAN + 2 * HD : h * SPAN + 3 * HD]
+                scores = dot(query, key, ((1,), (1,))) * HD**-0.5
+                match = seg_col[HALO + b * 128 : HALO + (b + 1) * 128] == seg_row[:, near]
+                scores = jnp.where(match, scores, masked_score)
+                exponent = jnp.exp(scores - jnp.max(scores, axis=-1, keepdims=True))
+                total = jnp.sum(exponent, axis=-1, keepdims=True)
+                prob = (exponent / total).astype(BF)
+                attended[t, b * 128 : (b + 1) * 128, h * HD : (h + 1) * HD] = dot(
+                    prob, value
+                ).astype(BF)
+        return carry
+
+    lax.fori_loop(0, 2, attend, 0)
+    gp.spread()
+    gu.across()
+    lax.fori_loop(2, 4, attend, 0)
+    save(5).start()
+    gd.forward()
+    resid_one[...] = tokens[...].astype(F32)
+
+    def output(t, carry):
+        weight = whole(full_a[t])[:, HEAD_SET * SPAN :]
+        resid_one[...] += dot(attended[t], weight, ((1,), (1,)))
+        return carry
+
+    lax.fori_loop(0, 4, output, 0)
+    xhat, _ = norm_parts(resid_one[...])
+    norm_two[...] = (xhat * gain_second).astype(BF)
+    save(6).start()
+    save(9).start()
+    gu.last()
+    save(1).start()
+    gp.forward()
+
+    def expand(t, carry):
+        value, derivative = gelu_parts(dot(norm_two[...], whole(full_u[t])))
+        hidden[t] = value.astype(BF)
+        slope[t] = derivative.astype(BF)
+        return carry
+
+    lax.fori_loop(0, 4, expand, 0)
+    save(7).start()
+    save(8).start()
+    gd.across()
+    gp.across()
+    gd.last()
+    save(2).start()
+    feat[...] = resid_one[...]
+
+    def contract(t, carry):
+        feat[...] += dot(hidden[t], whole(full_d[t]), ((1,), (1,)))
+        return carry
+
+    lax.fori_loop(0, 4, contract, 0)
+    resid_low[...] = feat[...].astype(BF)
+    gp.last()
+    save(3).start()
+    narrow = unit_low.shape[2]
+
+    square = jnp.zeros((own, 1), F32)
+    class_square = jnp.zeros((embed.shape[0], 1), F32)
+    pieces, class_pieces = [], []
+    for t in range(4):
+        both = whole(full_p[t])
+        piece = dot(resid_low[...], both[:, :narrow])
+        square += jnp.sum(piece * piece, axis=-1, keepdims=True)
+        pieces.append(piece)
+        piece = dot(embed[...], both[:, narrow:])
+        class_square += jnp.sum(piece * piece, axis=-1, keepdims=True)
+        class_pieces.append(piece)
+        class_out[t] = piece[:classes]
+    inverse = lax.rsqrt(square + epsilon_unit)
+    class_inverse = lax.rsqrt(class_square + epsilon_unit)
+    products = jnp.zeros((own, embed.shape[0]), F32)
+    for t in range(4):
+        pieces[t] = pieces[t] * inverse
+        unit_low[t] = pieces[t].astype(BF)
+        class_low[t] = (class_pieces[t] * class_inverse).astype(BF)
+        products += dot(unit_low[t], class_low[t], ((1,), (1,)))
+    masks, mask_inverse = norm_parts(products[:, :classes])
+    masks_out[...] = masks
+    d_products = norm_back(mask_grad[...], masks, mask_inverse).astype(BF)
+    along = jnp.zeros((own, 1), F32)
+    d_pieces = []
+    for t in range(4):
+        d_class_out[t] = dot(d_products, unit_low[t], ((0,), (0,)))
+        piece = dot(d_products, class_low[t, :classes])
+        along += jnp.sum(piece * pieces[t], axis=-1, keepdims=True)
+        d_pieces.append(piece)
+    total = jnp.zeros(feat.shape, F32)
+    flipped = resid_low[...].T
+    for t in range(4):
+        piece = (inverse * (d_pieces[t] - pieces[t] * along)).astype(BF)
+        total += dot(piece, whole(full_p[t])[:, :narrow], ((1,), (1,)))
+        block = dot(flipped, piece).astype(BF)
+        grad_p[t] = block.reshape((2, 2, 2, block.shape[0] // 8, narrow))
+    d_resid[...] = total
+    save(10).start()
+    save(11).start()
+    for n in range(len(kept)):
+        save(n).wait()
+    halo_before.wait_send()
+    halo_after.wait_send()
+    for gather in (ge, ga, gu, gd, gp):
+        gather.drain()
+
+
+def any_specs(count):
+    return [pl.BlockSpec(memory_space=pl.ANY)] * count
+
+
+def vmem_specs(count):
+    return [pl.BlockSpec(memory_space=pltpu.VMEM)] * count
+
+
+def kept_shapes(own, width, cut, narrow, high):
+    piece = width // 8
+    span = own + 2 * HALO
+    return [
+        ((4, 8, piece, width), BF),
+        ((4, 8, piece, high), BF),
+        ((4, 8, piece, high), BF),
+        ((4, 8, piece, 2 * narrow), BF),
+        ((4, span, cut), BF),
+        ((4, own, cut // 3), BF),
+        ((own, width), BF),
+        ((4, own, high), BF),
+        ((4, own, high), BF),
+        ((own, width), F32),
+        ((own, width), F32),
+        ((4, 2, 2, 2, piece, narrow), BF),
+    ]
+
+
+def forward_call(classes, kept, tokens, seg_col, seg_row, mask_grad, shard_e, shards):
+    own, width = tokens.shape
+    rows_e = shard_e.shape[0]
+    narrow = shards[3].shape[1] // 2
+    span = own + 2 * HALO
+    count = len(shards) + 1
+    scratch = [pltpu.VMEM(*k) for k in kept[:9]] + [
+        pltpu.VMEM(*kept[10]),
+        pltpu.VMEM(*kept[11]),
+        pltpu.VMEM(*kept[9]),
+        pltpu.VMEM((8,) + shard_e.shape, BF),
+        pltpu.VMEM((span, width), BF),
+        pltpu.VMEM((span, width), BF),
+        pltpu.VMEM((rows_e, width), BF),
+        pltpu.VMEM((own, width), F32),
+        pltpu.VMEM((4, own, narrow), BF),
+        pltpu.VMEM((4, rows_e, narrow), BF),
+        pltpu.VMEM((own, width), BF),
+        pltpu.SemaphoreType.DMA((count, 20)),
+        pltpu.SemaphoreType.DMA((count, 20)),
+        pltpu.SemaphoreType.DMA((4,)),
+        pltpu.SemaphoreType.DMA((len(kept),)),
+    ]
+    outs = [
+        jax.ShapeDtypeStruct((own, classes), F32),
+        jax.ShapeDtypeStruct((4, classes, narrow), F32),
+        jax.ShapeDtypeStruct((4, classes, narrow), F32),
+        jax.ShapeDtypeStruct((2, width), F32),
+    ]
     return pl.pallas_call(
-        functools.partial(gather_kernel, count),
-        out_shape=outs,
-        in_specs=[pl.BlockSpec(memory_space=pltpu.VMEM)] * count,
-        out_specs=[pl.BlockSpec(memory_space=pltpu.VMEM)] * count,
-        scratch_shapes=[pltpu.SemaphoreType.DMA((count, 11))] * 2,
+        functools.partial(forward_kernel, classes),
+        out_shape=outs + [jax.ShapeDtypeStruct(*k) for k in kept],
+        in_specs=vmem_specs(9),
+        out_specs=vmem_specs(4) + any_specs(len(kept)),
+        scratch_shapes=scratch,
         compiler_params=pltpu.CompilerParams(
-            collective_id=0, has_side_effects=True, vmem_limit_bytes=60 << 20
+            collective_id=0, has_side_effects=True, vmem_limit_bytes=VMEM_LIMIT
         ),
-    )(*operands)
-
-
-def scatter_kernel(count, *refs):
-    grads, outs = refs[:count], refs[count : 2 * count]
-    scratch = refs[2 * count :]
-    sends, receives = scratch[-2:]
-    bufs = [scratch[6 * w : 6 * w + 6] for w in range(count)]
-    dp, tensor, over_x, over_y, sibling = places()
-    core, col, row = dp % 2, (dp // 2) % 2, dp // 4
-    greet()
-
-    def copy(w, k):
-        g = grads[w]
-        r1, r2a, r2b, r3a, r3b, r4 = bufs[w]
+    )(tokens, seg_col, seg_row, mask_grad, shard_e, *shards)
+
+
+class Scatter:
+    def __init__(self, grad, buffers, sends, receives, w):
+        self.grad, self.sends, self.receives, self.w = grad, sends, receives, w
+        self.r1, self.r2a, self.r2b, self.r3a, self.r3b, self.r4 = buffers
+
+    def copy(self, k):
+        dp, tensor, over_x, over_y, sibling = places()
+        core, col, row = dp % 2, (dp // 2) % 2, dp // 4
+        r1 = self.r1
         if k == 0:
-            pair = (g.at[:, :, :, 1 - core], r1, (sibling, tensor))
+            pair = (self.grad.at[:, :, :, 1 - core], r1, (sibling, tensor))
         elif k == 1:
-            pair = (r1.at[0:2, :, 1 - col], r2a, (over_x, tensor))
+            pair = (r1.at[0:2, :, 1 - col], self.r2a, (over_x, tensor))
         elif k == 2:
-            pair = (r1.at[2:4, 1 - row], r2b, (over_y, tensor))
+            pair = (r1.at[2:4, 1 - row], self.r2b, (over_y, tensor))
         elif k == 3:
-            pair = (r1.at[0:2, 1 - row, col], r3a, (over_y, tensor))
+            pair = (r1.at[0:2, 1 - row, col], self.r3a, (over_y, tensor))
         elif k == 4:
-            pair = (r1.at[2:4, row, 1 - col], r3b, (over_x, tensor))
+            pair = (r1.at[2:4, row, 1 - col], self.r3b, (over_x, tensor))
         else:
             j = k - 4
             peer = (tensor + j) % 4
-            pair = (r1.at[peer, row, col], r4.at[j - 1], (dp, peer))
-        return remote(pair[0], pair[1], sends.at[w, k], receives.at[w, k], pair[2])
-
-    def add(ref, index, other):
-        ref[index] = (ref[index].astype(F32) + other.astype(F32)).astype(BF)
-
-    for w in range(count):
-        copy(w, 0).start()
-    for stage in range(count + 3):
-        w = stage
-        if w < count:
-            copy(w, 0).wait_recv()
-            r1 = bufs[w][0]
-            for t in range(4):
-                add(r1, t, grads[w][t, :, :, core])
-            copy(w, 1).start()
-            copy(w, 2).start()
-        w = stage - 1
-        if 0 <= w < count:
-            r1, r2a, r2b, r3a, r3b, r4 = bufs[w]
-            copy(w, 1).wait_recv()
-            for t in range(2):
-                for y in range(2):
-                    add(r1, (t, y, col), r2a[t, y])
-            copy(w, 3).start()
-            copy(w, 2).wait_recv()
-            for t in range(2):
-                for x in range(2):
-                    add(r1, (2 + t, row, x), r2b[t, x])
-            copy(w, 4).start()
-        w = stage - 2
-        if 0 <= w < count:
-            r1, r2a, r2b, r3a, r3b, r4 = bufs[w]
-            copy(w, 3).wait_recv()
-            for t in range(2):
-                add(r1, (t, row, col), r3a[t])
-            copy(w, 4).wait_recv()
-            for t in range(2):
-                add(r1, (2 + t, row, col), r3b[t])
-            for j in (1, 2, 3):
-                copy(w, 4 + j).start()
-        w = stage - 3
-        if 0 <= w < count:
-            r1, r4 = bufs[w][0], bufs[w][5]
-            for j in (1, 2, 3):
-                copy(w, 4 + j).wait_recv()
-            total = r1[tensor, row, col].astype(F32)
-            for j in range(3):
-                total = total + r4[j].astype(F32)
-            outs[w][...] = total
-    for w in range(count):
+            pair = (r1.at[peer, row, col], self.r4.at[j - 1], (dp, peer))
+        return remote(
+            pair[0], pair[1], self.sends.at[self.w, k], self.receives.at[self.w, k], pair[2]
+        )
+
+    def add(self, index, other):
+        ref = self.r1
+        ref[index] = (ref[index].astype(F32) + other.astype(F32)).astype(ref.dtype)
+
+    def start(self):
+        self.copy(0).start()
+
+    def planes(self):
+        dp = lax.axis_index("dp")
+        core = dp % 2
+        self.copy(0).wait_recv()
+
+        def step(i, carry):
+            t, y = i // 2, i % 2
+            self.add((t, y), self.grad[t, y, :, core])
+            return carry
+
+        lax.fori_loop(0, 8, step, 0)
+        self.copy(1).start()
+        self.copy(2).start()
+
+    def lines(self):
+        dp = lax.axis_index("dp")
+        col, row = (dp // 2) % 2, dp // 4
+        self.copy(1).wait_recv()
+        for t in range(2):
+            for y in range(2):
+                self.add((t, y, col), self.r2a[t, y])
+        self.copy(3).start()
+        self.copy(2).wait_recv()
+        for t in range(2):
+            for x in range(2):
+                self.add((2 + t, row, x), self.r2b[t, x])
+        self.copy(4).start()
+
+    def points(self):
+        dp = lax.axis_index("dp")
+        col, row = (dp // 2) % 2, dp // 4
+        self.copy(3).wait_recv()
+        for t in range(2):
+            self.add((t, row, col), self.r3a[t])
+        self.copy(4).wait_recv()
+        for t in range(2):
+            self.add((2 + t, row, col), self.r3b[t])
+        for j in (1, 2, 3):
+            self.copy(4 + j).start()
+
+    def result(self, out):
+        dp, tensor = places()[:2]
+        col, row = (dp // 2) % 2, dp // 4
+        for j in (1, 2, 3):
+            self.copy(4 + j).wait_recv()
+        total = self.r1[tensor, row, col].astype(F32)
+        for j in range(3):
+            total = total + self.r4[j].astype(F32)
+        out[...] = total
+
+    def drain(self):
         for k in range(8):
-            copy(w, k).wait_send()
-
-
-def scatter_call(grads):
-    count = len(grads)
-    grads = [g.reshape(4, 2, 2, 2, 96, g.shape[-1]) for g in grads]
-    scratch = []
-    for g in grads:
-        c = g.shape[-1]
-        scratch += [
-            pltpu.VMEM((4, 2, 2, 96, c), BF),
-            pltpu.VMEM((2, 2, 96, c), BF),
-            pltpu.VMEM((2, 2, 96, c), BF),
-            pltpu.VMEM((2, 96, c), BF),
-            pltpu.VMEM((2, 96, c), BF),
-            pltpu.VMEM((3, 96, c), BF),
-        ]
+            self.copy(k).wait_send()
+
+
+def scatter_buffers(rows, cols, dtype):
+    return [
+        pltpu.VMEM((4, 2, 2, rows, cols), dtype),
+        pltpu.VMEM((2, 2, rows, cols), dtype),
+        pltpu.VMEM((2, 2, rows, cols), dtype),
+        pltpu.VMEM((2, rows, cols), dtype),
+        pltpu.VMEM((2, rows, cols), dtype),
+        pltpu.VMEM((3, rows, cols), dtype),
+    ]
+
+
+def backward_kernel(*refs):
+    (tokens, seg_col, seg_row, gains) = refs[:4]
+    loads_in = refs[4:15]
+    token_grad, share_p, share_d, share_u, share_a, share_n = refs[15:21]
+    scratch = refs[21:]
+    loaded = scratch[:11]
+    (
+        d_resid,
+        grad_p,
+        hidden,
+        full_d,
+        slope,
+        norm_two,
+        full_u,
+        resid_one,
+        attended,
+        full_a,
+        joint,
+    ) = loaded
+    (grad_d, grad_u, grad_a, grad_n, window, d_attended, norm_one, total, stack_p, stack_s) = scratch[
+        11:21
+    ]
+    buffers = scratch[21:51]
+    sends, receives, halo_sems, load_sems = scratch[51:]
+
+    def load(n):
+        return plain_copy(loads_in[n], loaded[n], load_sems.at[n])
+
+    for n in range(11):
+        load(n).start()
+    dp, tensor = places()[:2]
+    own, width = tokens.shape
+    cut = joint.shape[2]
+    piece = width // 8
+    sp, sd, su, sa, sn = (
+        Scatter(g, buffers[6 * w : 6 * w + 6], sends, receives, w)
+        for w, g in enumerate((grad_p, grad_d, grad_u, grad_a, grad_n))
+    )
+    greet()
+    load(1).wait()
+    sp.start()
+    load(0).wait()
+    load(2).wait()
+    branch = d_resid[...].astype(BF)
+    flipped = branch.T
+
+    def down(t, carry):
+        grad_d[t] = dot(flipped, hidden[t]).astype(BF).reshape(grad_d.shape[1:])
+        return carry
+
+    lax.fori_loop(0, 4, down, 0)
+    sd.start()
+    load(3).wait()
+    load(4).wait()
+    load(5).wait()
+    flipped = norm_two[...].T
+
+    def up(t, carry):
+        back = dot(branch, whole(full_d[t])) * slope[t].astype(F32)
+        back = back.astype(BF)
+        slope[t] = back
+        grad_u[t] = dot(flipped, back).astype(BF).reshape(grad_u.shape[1:])
+        return carry
+
+    lax.fori_loop(0, 4, up, 0)
+    su.start()
+    sp.planes()
+    sd.planes()
+    load(6).wait()
+    load(7).wait()
+    total[...] = jnp.zeros_like(total)
+
+    def narrow_back(t, carry):
+        total[...] += dot(slope[t], whole(full_u[t]), ((1,), (1,)))
+        return carry
+
+    lax.fori_loop(0, 4, narrow_back, 0)
+    gain_first, gain_second = gains[0:1], gains[1:2]
+    xhat, inverse = norm_parts(resid_one[...])
+    gain_two = jnp.sum(total[...] * xhat, axis=0, keepdims=True)
+    d_resid[...] += norm_back(total[...] * gain_second, xhat, inverse)
+    window[HALO : HALO + own] = d_resid[...].astype(BF)
+    halo_before = remote(
+        window.at[pl.ds(HALO, HALO)],
+        window.at[pl.ds(HALO + own, HALO)],
+        halo_sems.at[0],
+        halo_sems.at[1],
+        (dp, (tensor + 3) % 4),
+    )
+    halo_after = remote(
+        window.at[pl.ds(own, HALO)],
+        window.at[pl.ds(0, HALO)],
+        halo_sems.at[2],
+        halo_sems.at[3],
+        (dp, (tensor + 1) % 4),
+    )
+    halo_before.start()
+    halo_after.start()
+    su.planes()
+    sp.lines()
+    load(8).wait()
+    flipped = window[HALO : HALO + own].T
+
+    def outer(t, carry):
+        block = dot(flipped, attended[t]).astype(BF)
+        grad_a[t, :, :, :, :, cut:] = block.reshape((2, 2, 2, piece, cut // 3))
+        return carry
+
+    lax.fori_loop(0, 4, outer, 0)
+    xhat, inverse = norm_parts(tokens[...].astype(F32))
+    norm_one[...] = (xhat * gain_first).astype(BF)
+    load(9).wait()
+    load(10).wait()
+    halo_before.wait_recv()
+    halo_after.wait_recv()
+
+    def attended_back(t, carry):
+        weight = whole(full_a[t])[:, cut:]
+        d_attended[t] = dot(window[...], weight).astype(BF)
+        return carry
+
+    lax.fori_loop(0, 4, attended_back, 0)
+    sd.lines()
+    sp.points()
+    mine = slice(HALO, HALO + own)
+    stack_p[...] = jnp.zeros_like(stack_p)
+    stack_s[...] = jnp.zeros_like(stack_s)
+
+    def attend(t, carry):
+        for h in range(HEAD_SET):
+            q_cols = slice(h * SPAN, h * SPAN + HD)
+            k_cols = slice(h * SPAN + HD, h * SPAN + 2 * HD)
+            v_cols = slice(h * SPAN + 2 * HD, h * SPAN + 3 * HD)
+            d_cols = slice(h * HD, (h + 1) * HD)
+            for b in range(4):
+                rows = slice(b * 128, (b + 1) * 128)
+                low_key, high_key = max(b - 1, 0) * 128, min(b + 2, 4) * 128
+                near = slice(low_key, high_key)
+                key = joint[t, near, k_cols]
+                scores = dot(joint[t, rows, q_cols], key, ((1,), (1,))) * HD**-0.5
+                match = seg_col[rows] == seg_row[:, near]
+                scores = jnp.where(match, scores, masked_score)
+                exponent = jnp.exp(scores - jnp.max(scores, axis=-1, keepdims=True))
+                prob = exponent / jnp.sum(exponent, axis=-1, keepdims=True)
+                d_prob = dot(d_attended[t, rows, d_cols], joint[t, near, v_cols], ((1,), (1,)))
+                delta = jnp.sum(prob * d_prob, axis=-1, keepdims=True)
+                d_scores = (prob * (d_prob - delta)).astype(BF)
+                prob = prob.astype(BF)
+                first, last = max(low_key, HALO), min(high_key, HALO + own)
+                stack_p[rows, first - HALO : last - HALO] = prob[:, first - low_key : last - low_key]
+                stack_s[rows, first - HALO : last - HALO] = d_scores[
+                    :, first - low_key : last - low_key
+                ]
+                if b in (1, 2):
+                    hidden[t, (b - 1) * 128 : b * 128, q_cols] = (
+                        dot(d_scores, key) * HD**-0.5
+                    ).astype(BF)
+            hidden[t, :, k_cols] = (
+                dot(stack_s[...], joint[t, :, q_cols], ((0,), (0,))) * HD**-0.5
+            ).astype(BF)
+            hidden[t, :, v_cols] = dot(
+                stack_p[...], d_attended[t, :, d_cols], ((0,), (0,))
+            ).astype(BF)
+        return carry
+
+    lax.fori_loop(0, 2, attend, 0)
+    su.lines()
+    lax.fori_loop(2, 4, attend, 0)
+    flipped = norm_one[...].T
+
+    def attend_grad(t, carry):
+        block = dot(flipped, hidden[t, :, :cut]).astype(BF)
+        grad_a[t, :, :, :, :, :cut] = block.reshape((2, 2, 2, piece, cut))
+        return carry
+
+    lax.fori_loop(0, 4, attend_grad, 0)
+    sa.start()
+    sd.points()
+    sa.planes()
+    total[...] = jnp.zeros_like(total)
+
+    def joint_back(t, carry):
+        weight = whole(full_a[t])[:, :cut]
+        total[...] += dot(hidden[t, :, :cut], weight, ((1,), (1,)))
+        return carry
+
+    lax.fori_loop(0, 4, joint_back, 0)
+    su.points()
+    xhat, inverse = norm_parts(tokens[...].astype(F32))
+    gain_one = jnp.sum(total[...] * xhat, axis=0, keepdims=True)
+    token_grad[...] = d_resid[...] + norm_back(total[...] * gain_first, xhat, inverse)
+    grad_n[...] = jnp.zeros_like(grad_n)
+    for d in range(8):
+        cols = slice(d * piece, (d + 1) * piece)
+        y, x, c = d // 4, (d // 2) % 2, d % 2
+        for t in range(4):
+            grad_n[t, y, x, c, 0:1, 0:piece] = gain_one[:, cols]
+            grad_n[t, y, x, c, 1:2, 0:piece] = gain_two[:, cols]
+    sn.start()
+    sn.planes()
+    sp.result(share_p)
+    sa.lines()
+    sn.lines()
+    sd.result(share_d)
+    sa.points()
+    sn.points()
+    su.result(share_u)
+    sa.result(share_a)
+    sn.result(share_n)
+    halo_before.wait_send()
+    halo_after.wait_send()
+    for scatter in (sp, sd, su, sa, sn):
+        scatter.drain()
+
+
+LOADED = (10, 11, 7, 2, 8, 6, 1, 9, 5, 0, 4)
+
+
+def backward_call(kept, tokens, seg_col, seg_row, gains, saved):
+    own, width = tokens.shape
+    cut, narrow, high = kept[4][0][2], kept[11][0][5], kept[7][0][2]
+    piece = width // 8
+    span = own + 2 * HALO
+    scratch = [pltpu.VMEM(*kept[n]) for n in LOADED] + [
+        pltpu.VMEM((4, 2, 2, 2, piece, high), BF),
+        pltpu.VMEM((4, 2, 2, 2, piece, high), BF),
+        pltpu.VMEM((4, 2, 2, 2, piece, width), BF),
+        pltpu.VMEM((4, 2, 2, 2, 8, 128), F32),
+        pltpu.VMEM((span, width), BF),
+        pltpu.VMEM((4, span, cut // 3), BF),
+        pltpu.VMEM((own, width), BF),
+        pltpu.VMEM((own, width), F32),
+        pltpu.VMEM((span, own), BF),
+        pltpu.VMEM((span, own), BF),
+    ]
+    for cols in (narrow, high, high, width):
+        scratch += scatter_buffers(piece, cols, BF)
+    scratch += scatter_buffers(8, 128, F32)
+    scratch += [
+        pltpu.SemaphoreType.DMA((5, 8)),
+        pltpu.SemaphoreType.DMA((5, 8)),
+        pltpu.SemaphoreType.DMA((4,)),
+        pltpu.SemaphoreType.DMA((len(LOADED),)),
+    ]
     return pl.pallas_call(
-        functools.partial(scatter_kernel, count),
-        out_shape=[jax.ShapeDtypeStruct((96, g.shape[-1]), F32) for g in grads],
-        in_specs=[pl.BlockSpec(memory_space=pltpu.VMEM)] * count,
-        out_specs=[pl.BlockSpec(memory_space=pltpu.VMEM)] * count,
-        scratch_shapes=scratch + [pltpu.SemaphoreType.DMA((count, 8))] * 2,
+        backward_kernel,
+        out_shape=[
+            jax.ShapeDtypeStruct((own, width), F32),
+            jax.ShapeDtypeStruct((piece, narrow), F32),
+            jax.ShapeDtypeStruct((piece, high), F32),
+            jax.ShapeDtypeStruct((piece, high), F32),
+            jax.ShapeDtypeStruct((piece, width), F32),
+            jax.ShapeDtypeStruct((8, 128), F32),
+        ],
+        in_specs=vmem_specs(4) + any_specs(len(LOADED)),
+        out_specs=vmem_specs(6),
+        scratch_shapes=scratch,
         compiler_params=pltpu.CompilerParams(
-            collective_id=1, has_side_effects=True, vmem_limit_bytes=60 << 20
+            collective_id=1, has_side_effects=True, vmem_limit_bytes=VMEM_LIMIT
         ),
-    )(*grads)
+    )(tokens, seg_col, seg_row, gains, *(saved[n] for n in LOADED))
+
+
+def finish(masks, token_grad, grads, params, means, squares):
+    scales = (block_scale,) * 6 + (1.0,) * 3
+    decays = (0.0, weight_decay, weight_decay, 0.0) + (weight_decay,) * 5
+    new = [adamw_update(*v) for v in zip(params, grads, means, squares, scales, decays)]
+    return (masks, token_grad) + tuple(n[0] for n in new) + tuple(n[1] for n in new)
 
 
 def gather_plain(shards, embed):
@@ -320,8 +889,7 @@
     return jnp.concatenate((before, rows, after), axis=0)
 
 
-def local(
-    custom,
+def local_plain(
     parts,
     tokens,
     segments,
@@ -353,8 +921,7 @@
     shard_e = jnp.zeros((rows_e, class_embed.shape[1]), BF)
     shard_e = shard_e.at[:classes].set(low(class_embed))
     shard_e = shard_e.at[classes].set(low(gain_one)).at[classes + 1].set(low(gain_two))
-    gather = gather_call if custom else gather_plain
-    full_a, full_u, full_d, full_p, full_e = gather(
+    full_a, full_u, full_d, full_p, full_e = gather_plain(
         (shard_a, shard_u, shard_d, shard_p), shard_e
     )
     full_a, full_u, full_d, full_p = (
@@ -459,13 +1026,12 @@
     grad_gain_one = jnp.sum(d_norm_one * xhat_one[mine], axis=0)
 
     grad_patch = grad_patch.reshape(width, parts, narrow).transpose(1, 0, 2)
-    scatter = scatter_call if custom else scatter_plain
-    share_p, share_d, share_u, share_a = scatter(
+    share_p, share_d, share_u, share_a = scatter_plain(
         [
-            low(grad_patch),
-            low(grad_down),
-            low(grad_up),
-            low(jnp.concatenate((grad_attend, grad_output), axis=2)),
+            grad_patch,
+            grad_down,
+            grad_up,
+            jnp.concatenate((grad_attend, grad_output), axis=2),
         ]
     )
     gains = lax.psum((grad_gain_one, grad_gain_two), ("dp", "tensor"))
@@ -476,32 +1042,129 @@
     share_class = dot(low(class_embed), d_class_own, ((0,), (0,)))
     class_rows = lax.dynamic_slice_in_dim(w_class, dp_index * step, step, 0)
     share_embed = dot(d_class_feat, class_rows, ((1,), (1,)))
-    grads = (
-        share_one,
-        share_a[:, :cut],
-        share_a[:, cut:].T,
-        share_two,
-        share_u,
-        share_d.T,
-        share_p,
-        share_class,
-        share_embed,
-    )
-    params = (
-        gain_one,
-        attend_weight,
-        output_weight,
-        gain_two,
-        up_weight,
-        down_weight,
-        patch_weight,
-        class_weight,
-        class_embed,
-    )
-    scales = (block_scale,) * 6 + (1.0,) * 3
-    decays = (0.0, weight_decay, weight_decay, 0.0) + (weight_decay,) * 5
-    new = [adamw_update(*v) for v in zip(params, grads, means, squares, scales, decays)]
-    return (masks, token_grad) + tuple(n[0] for n in new) + tuple(n[1] for n in new)
+    return finish(
+        masks,
+        token_grad,
+        (
+            share_one,
+            share_a[:, :cut],
+            share_a[:, cut:].T,
+            share_two,
+            share_u,
+            share_d.T,
+            share_p,
+            share_class,
+            share_embed,
+        ),
+        (
+            gain_one,
+            attend_weight,
+            output_weight,
+            gain_two,
+            up_weight,
+            down_weight,
+            patch_weight,
+            class_weight,
+            class_embed,
+        ),
+        means,
+        squares,
+    )
+
+
+def local_kernels(
+    tokens,
+    segments,
+    mask_grad,
+    gain_one,
+    attend_weight,
+    output_weight,
+    gain_two,
+    up_weight,
+    down_weight,
+    patch_weight,
+    class_weight,
+    class_embed,
+    *moments,
+):
+    means, squares = moments[:9], moments[9:]
+    own, width = tokens.shape
+    classes = class_embed.shape[0]
+    dp_index = lax.axis_index("dp")
+    tensor_index = lax.axis_index("tensor")
+    low = lambda v: v.astype(BF)
+
+    shard_a = jnp.concatenate((low(attend_weight), low(output_weight).T), axis=1)
+    shard_u = low(up_weight)
+    shard_d = low(down_weight).T
+    shard_p = jnp.concatenate((low(patch_weight), low(class_weight)), axis=1)
+    rows_e = -(-(classes + 2) // 32) * 32
+    shard_e = jnp.concatenate(
+        (
+            low(class_embed),
+            low(gain_one)[None],
+            low(gain_two)[None],
+            jnp.zeros((rows_e - classes - 2, class_embed.shape[1]), BF),
+        )
+    )
+    padded = jnp.pad(segments[0], HALO, constant_values=-1)
+    seg = lax.dynamic_slice_in_dim(padded, tensor_index * own, own + 2 * HALO, 0)
+    seg_col, seg_row = seg[:, None], seg[None, :]
+    cut, narrow = attend_weight.shape[1], patch_weight.shape[1]
+    kept = kept_shapes(own, width, cut, narrow, up_weight.shape[1])
+    masks, d_class_part, class_feat, gains, *saved = forward_call(
+        classes,
+        kept,
+        tokens,
+        seg_col,
+        seg_row,
+        mask_grad,
+        shard_e,
+        (shard_a, shard_u, shard_d, shard_p),
+    )
+    d_class_unit = lax.psum(d_class_part, ("dp", "tensor"))
+    token_grad, share_p, share_d, share_u, share_a, share_n = backward_call(
+        kept, tokens, seg_col, seg_row, gains, saved
+    )
+    inverse = lax.rsqrt(jnp.sum(class_feat * class_feat, axis=(0, 2), keepdims=True) + epsilon_unit)
+    class_wide = class_feat * inverse
+    along = jnp.sum(class_wide * d_class_unit, axis=(0, 2), keepdims=True)
+    d_class_feat = low(inverse * (d_class_unit - class_wide * along))
+    d_class_own = lax.dynamic_index_in_dim(d_class_feat, tensor_index, 0, False)
+    share_class = dot(low(class_embed), d_class_own, ((0,), (0,)))
+    class_rows = lax.dynamic_index_in_dim(saved[3], dp_index, 1, False)[:, :, narrow:]
+    share_embed = jnp.einsum(
+        "tcn,trn->cr", d_class_feat, class_rows, preferred_element_type=F32
+    )
+    step = gain_one.shape[0]
+    return finish(
+        masks,
+        token_grad,
+        (
+            share_n[0, :step],
+            share_a[:, :cut],
+            share_a[:, cut:].T,
+            share_n[1, :step],
+            share_u,
+            share_d.T,
+            share_p,
+            share_class,
+            share_embed,
+        ),
+        (
+            gain_one,
+            attend_weight,
+            output_weight,
+            gain_two,
+            up_weight,
+            down_weight,
+            patch_weight,
+            class_weight,
+            class_embed,
+        ),
+        means,
+        squares,
+    )
 
 
 def solution(mesh):
@@ -520,7 +1183,7 @@
     )
     rows = P(("dp", "tensor"), None)
     return jax.shard_map(
-        functools.partial(local, custom, parts),
+        local_kernels if custom else functools.partial(local_plain, parts),
         mesh=mesh,
         in_specs=(rows, P("dp", None), rows) + params * 3,
         out_specs=(rows, rows) + params * 2,

time: 438 us -> 275 us (0.63); the launches traced: 431 us -> 274 us
  matrix products: 76.5 us -> 1.92 us
  blocking collectives: 40.2 us -> 0 us
  other arithmetic: 54.7 us -> 20.7 us
  Pallas kernels: 194 us -> 221 us
  local copies, waits for them, and re-layouts: 32.1 us -> 12 us
  starting transfers between devices: 17.4 us -> 0.04 us
    dot_general x15 -> x1, matrix products: 43.4 us -> 0.99 us  [local_kernels(): jnp.einsum('tcn,trn->cr', d_class_feat, class_rows, preferred_element_typ...]
    psum x1 -> x0, blocking collectives: 40.2 us -> none  [local(): gains = lax.psum((grad_gain_one, grad_gain_two), ('dp', 'tensor'))]
    pallas_call x2, Pallas kernels: 194 us -> 221 us  [the longest x1 120 us: backward_call(): pl.pallas_call(backward_kernel, out_shape=[jax.ShapeDtypeStruct((own, wid...]
    sub x2 -> x0, matrix products: 24.2 us -> none  [the longest x1 13.7 us: local(): d_scores = low(prob * (d_prob - delta))]
    convert_element_type x14 -> x6, other arithmetic: 26.1 us -> 5.58 us  [local_kernels(): low = lambda v: v.astype(BF)]
    ppermute x4 -> x0, starting transfers between devices: 17.4 us -> none  [the longest x2 14.8 us: with_halo(): before = lax.ppermute(rows[-HALO:], 'tensor', forward)]
    slice x7 -> x0, local copies, waits for them, and re-layouts: 7.65 us -> none  [the longest x1 3.79 us: local(): w_patch, w_class = (full_p[:, :, :narrow], full_p[:, :, narrow:])]
    dot_general x9 -> x1, matrix products: 8.09 us -> 0.93 us  [dot(): lax.dot_general(left, right, (dims, ((), ())), preferred_element_type=F32)]
  transfers between devices with their start and end apart: 5 -> 1, of which waited for: 0 -> 1; matrix products, arithmetic and copies ran while one was open for 20% -> 6% of each run, Pallas kernels for 45% -> 44%
where the time goes in v2:
time: 275 us; the launch traced here: 274 us
  Pallas kernels  221 us (80%)
  other arithmetic  20.7 us (8%)
  between operations  14.4 us (5%)
  local copies, waits for them, and re-layouts  12 us (4%)
  waiting for transfers between devices  4.26 us (2%)
    pallas_call x1, Pallas kernels, backward_call(): pl.pallas_call(backward_kernel, out_shape=[jax.ShapeDtypeStruct((own, wid...  120 us
    pallas_call x1, Pallas kernels, forward_call(): pl.pallas_call(functools.partial(forward_kernel, classes), out_shape=outs...  100 us
    unnamed x58, local copies, waits for them, and re-layouts  9.24 us
    mul x5, other arithmetic, adamw_update(): return (step_scale * (moved + decay_rate * current), mean_new)  8.07 us
    convert_element_type x6, other arithmetic, local_kernels(): low = lambda v: v.astype(BF)  5.58 us
  transfers between devices with their start and end apart: 1, of which 1 were waited for; matrix products, arithmetic and copies ran while one was open for 6% of the time, Pallas kernels for 44%

profile of v2, /device:TPU:0, one launch (start us, length us, event | category | flops | bytes accessed | tf_op | source)
XLA Modules:
  0.0 274.0 jit_solution(5572207800323863153)
XLA Ops:
  7.3 0.8 pad_dynamic-slice_fusion
  8.1 0.9 copy.60.refs_1_
  8.9 0.9 convert_element_type.31
  9.8 1.0 copy.59
  10.8 1.0 convert_element_type.34
  11.8 1.8 copy.61.refs_3_
  13.5 0.9 convert_element_type.38
  14.4 0.9 convert_element_type.39
  15.3 1.6 convert_bitcast_fusion.refs_7_
  17.8 0.7 pad_maximum_fusion.refs_5_
  18.5 0.7 pad_maximum_fusion.1.refs_8_
  19.9 100.3 %shard_map.437 = (f32[256,150]{1,0:T(8,128)}, f32[4,150,192]{2,1,0:T(8,128)}, f32[4,150,192]{2,1,0:T(8,128)}, f32[2,768]{1,0:T(2,128)}, bf16[4,8,96,768]{3,2,1,0...) custom-call(bf16[256,768]{1,0:T(8,128)(2,1)} %refs_0_.3, ...), custom_call_target="tpu_custom_call" | custom-call | tf_op jit(solution)/shard_map/pallas_call | solution.py:487
  120.2 1.2 multiply_reduce_fusion.1
  121.5 1.6 copy.63
  123.1 1.6 copy.64
  124.7 120.4 %shard_map.438 = (f32[256,768]{1,0:T(8,128)}, f32[96,192]{1,0:T(8,128)}, f32[96,768]{1,0:T(8,128)}, f32[96,768]{1,0:T(8,128)}, f32[96,768]{1,0:T(8,128)}, /*index=5*/f32[8,128]{1,0:T(8,128)}) custom-call(bf16[256,768]{1,0:T(8,128)(2,1)} %refs_0_.3, s32[512,1]{1,0:T(8,128)} %copy.60.refs_1_, s32[1,512]{1,0:T(1,128)} %bitcast.58, ...), custom_call_target="tpu_custom_call" | custom-call | tf_op jit(solution)/shard_map/pallas_call | solution.py:843
  245.2 1.2 fusion.42
  246.4 2.3 fusion.21
  248.8 2.2 fusion.14
  251.0 1.0 fusion.13
  252.1 0.7 fusion.34
  252.8 1.0 dynamic-slice_bitcast_fusion
  253.9 0.7 copy.68
  254.6 0.7 copy.69
  255.4 0.8 copy.67
  256.2 1.3 add_multiply_fusion
  257.5 4.2 %all-reduce.3.cloned.1.call-done = f32[4,150,192]{2,1,0:T(8,128)} async-done(((f32[4,150,192]{2,1,0:T(8,128)}), f32[4,150,192]{2,1,0:T(8,128)}) %all-reduce.3.cloned.1.call-update) | async-done | bytes 460816 | tf_op jit(solution)/shard_map/psum | solution.py:1125
  261.7 1.3 multiply_reduce_fusion
  263.0 1.3 multiply_convert_fusion
  264.3 1.0 fusion.48
  265.3 0.9 fusion.40
  266.2 0.9 copy.73
  (59 shorter events, 1.7 us)
Async XLA Ops:
  7.2 9.8 %copy-start.1 = (f32[96,768]{1,0:T(8,128)S(1)}, f32[96,768]{1,0:T(8,128)}, u32[]{:S(2)}) copy-start(f32[96,768]{1,0:T(8,128)} %param.37) | copy-start | bytes 884740
  7.2 10.5 %copy-start.16 = (f32[96]{0:T(128)S(1)}, f32[96]{0:T(128)}, u32[]{:S(2)}) copy-start(f32[96]{0:T(128)} %param.33) | copy-start | bytes 1156
  7.2 10.5 %copy-start.15 = (f32[96]{0:T(128)S(1)}, f32[96]{0:T(128)}, u32[]{:S(2)}) copy-start(f32[96]{0:T(128)} %param.36) | copy-start | bytes 1156
  7.2 254.5 %all-reduce.3.cloned.1.call-start = ((), (), s32[]{:S(2)}) async-start(), calls=%async_computation | async-start | bytes 1245184 | tf_op jit(solution)/shard_map/psum | solution.py:1125
  8.1 11.9 %copy-start.14 = (s32[512]{0:T(512)}, s32[512]{0:T(512)S(1)}, u32[]{:S(2)}) copy-start(s32[512]{0:T(512)S(1)} %pad_dynamic-slice_fusion) | copy-start | bytes 6148
  245.1 5.9 %copy-start.2 = (f32[768,96]{0,1:T(8,128)S(1)}, f32[768,96]{0,1:T(8,128)}, u32[]{:S(2)}) copy-start(f32[768,96]{0,1:T(8,128)} %param.38) | copy-start | bytes 884740
  245.1 5.9 %copy-start.5 = (f32[768,96]{0,1:T(8,128)S(1)}, f32[768,96]{0,1:T(8,128)}, u32[]{:S(2)}) copy-start(f32[768,96]{0,1:T(8,128)} %param.56) | copy-start | bytes 884740
  245.1 5.9 %copy-start.6 = (f32[768,96]{0,1:T(8,128)S(1)}, f32[768,96]{0,1:T(8,128)}, u32[]{:S(2)}) copy-start(f32[768,96]{0,1:T(8,128)} %param.47) | copy-start | bytes 884740
  245.2 5.9 %copy-start.7 = (f32[96,768]{1,0:T(8,128)S(1)}, f32[96,768]{1,0:T(8,128)}, u32[]{:S(2)}) copy-start(f32[96,768]{1,0:T(8,128)} %get-tuple-element.59) | copy-start | bytes 884740
  246.4 5.7 %copy-start.4 = (f32[96,192]{1,0:T(8,128)S(1)}, f32[96,192]{1,0:T(8,128)}, u32[]{:S(2)}) copy-start(f32[96,192]{1,0:T(8,128)} %param.39) | copy-start | bytes 221188
  246.4 5.6 %copy-start.9 = (f32[96,192]{1,0:T(8,128)S(1)}, f32[96,192]{1,0:T(8,128)}, u32[]{:S(2)}) copy-start(f32[96,192]{1,0:T(8,128)} %param.57) | copy-start | bytes 221188
  246.4 5.6 %copy-start.10 = (f32[96,192]{1,0:T(8,128)S(1)}, f32[96,192]{1,0:T(8,128)}, u32[]{:S(2)}) copy-start(f32[96,192]{1,0:T(8,128)} %param.48) | copy-start | bytes 221188
  246.4 5.6 %copy-start.11 = (f32[96,192]{1,0:T(8,128)S(1)}, f32[96,192]{1,0:T(8,128)}, u32[]{:S(2)}) copy-start(f32[96,192]{1,0:T(8,128)} %get-tuple-element.60) | copy-start | bytes 221188
  248.7 6.6 %copy-start.8 = (f32[256,150]{1,0:T(8,128)S(1)}, f32[256,150]{1,0:T(8,128)}, u32[]{:S(2)}) copy-start(f32[256,150]{1,0:T(8,128)} %get-tuple-element.84) | copy-start | bytes 460804
  248.8 7.4 %copy-start.17 = (f32[96]{0:T(128)S(1)}, f32[96]{0:T(128)}, u32[]{:S(2)}) copy-start(f32[96]{0:T(128)} %param.54) | copy-start | bytes 1156
  248.8 7.4 %copy-start.18 = (f32[96]{0:T(128)S(1)}, f32[96]{0:T(128)}, u32[]{:S(2)}) copy-start(f32[96]{0:T(128)} %param.45) | copy-start | bytes 1156
  248.8 7.4 %copy-start.19 = (f32[96]{0:T(128)S(1)}, f32[96]{0:T(128)}, u32[]{:S(2)}) copy-start(f32[96]{0:T(128)} %param.51) | copy-start | bytes 1156
  248.8 7.4 %copy-start.20 = (f32[96]{0:T(128)S(1)}, f32[96]{0:T(128)}, u32[]{:S(2)}) copy-start(f32[96]{0:T(128)} %param.42) | copy-start | bytes 1156
  248.8 12.9 %copy-start = (f32[4,150,192]{2,1,0:T(8,128)S(1)}, f32[4,150,192]{2,1,0:T(8,128)}, u32[]{:S(2)}) copy-start(f32[4,150,192]{2,1,0:T(8,128)} %get-tuple-element.61) | copy-start | bytes 1382404
  252.1 12.2 %copy-start.13 = (f32[150,96]{1,0:T(8,128)S(1)}, f32[150,96]{1,0:T(8,128)}, u32[]{:S(2)}) copy-start(f32[150,96]{1,0:T(8,128)} %param.41) | copy-start | bytes 172804
  252.1 12.2 %copy-start.23 = (f32[150,96]{1,0:T(8,128)S(1)}, f32[150,96]{1,0:T(8,128)}, u32[]{:S(2)}) copy-start(f32[150,96]{1,0:T(8,128)} %param.59) | copy-start | bytes 172804
  252.1 12.2 %copy-start.24 = (f32[150,96]{1,0:T(8,128)S(1)}, f32[150,96]{1,0:T(8,128)}, u32[]{:S(2)}) copy-start(f32[150,96]{1,0:T(8,128)} %param.50) | copy-start | bytes 172804
  253.8 11.4 %copy-start.12 = (f32[96,192]{1,0:T(8,128)S(1)}, f32[96,192]{1,0:T(8,128)}, u32[]{:S(2)}) copy-start(f32[96,192]{1,0:T(8,128)} %param.40) | copy-start | bytes 221188
  253.9 11.4 %copy-start.21 = (f32[96,192]{1,0:T(8,128)S(1)}, f32[96,192]{1,0:T(8,128)}, u32[]{:S(2)}) copy-start(f32[96,192]{1,0:T(8,128)} %param.58) | copy-start | bytes 221188
  253.9 11.4 %copy-start.22 = (f32[96,192]{1,0:T(8,128)S(1)}, f32[96,192]{1,0:T(8,128)}, u32[]{:S(2)}) copy-start(f32[96,192]{1,0:T(8,128)} %param.49) | copy-start | bytes 221188
  256.1 10.1 %copy-start.3 = (f32[256,768]{1,0:T(8,128)S(1)}, f32[256,768]{1,0:T(8,128)}, u32[]{:S(2)}) copy-start(f32[256,768]{1,0:T(8,128)} %get-tuple-element.147) | copy-start | bytes 2359300
Sparse Core Ops, SparseCore 0:
  120.4 141.2 all-reduce.2

commit v3 on v1

v3 whole, which is shorter than its diff:
```python
import functools

import jax
import jax.numpy as jnp
from jax import lax
from jax.experimental import pallas as pl
from jax.experimental.pallas import tpu as pltpu
from jax.sharding import PartitionSpec as P

HD = 64
HALO = 128
BF = jnp.bfloat16
F32 = jnp.float32
MESH = pl.DeviceIdType.MESH
VMEM_LIMIT = 64 * 1024 * 1024 - 512 * 1024

epsilon_norm = 1e-05
epsilon_unit = 1e-06
masked_score = -1000000000.0
first_decay = 0.9
second_decay = 0.999
first_fix = 0.99997343860112
second_fix = 0.09520785288629
adam_epsilon = 1e-08
block_scale = 0.65
weight_decay = 0.05


def dot(left, right, dims=((1,), (0,))):
    return lax.dot_general(left, right, (dims, ((), ())), preferred_element_type=F32)


def layer_norm(values, gain):
    center = values - jnp.mean(values, axis=-1, keepdims=True)
    spread = jnp.mean(center * center, axis=-1, keepdims=True)
    return center * lax.rsqrt(spread + epsilon_norm) * gain


def norm_parts(values):
    center = values - jnp.mean(values, axis=-1, keepdims=True)
    spread = jnp.mean(center * center, axis=-1, keepdims=True)
    inverse = lax.rsqrt(spread + epsilon_norm)
    return center * inverse, inverse


def norm_back(gradient, xhat, inverse):
    return inverse * (
        gradient
        - jnp.mean(gradient, axis=-1, keepdims=True)
        - xhat * jnp.mean(gradient * xhat, axis=-1, keepdims=True)
    )


def unit_parts(values):
    inverse = lax.rsqrt(jnp.sum(values * values, axis=-1, keepdims=True) + epsilon_unit)
    return values * inverse, inverse


def unit_back(gradient, unit, inverse):
    return inverse * (gradient - unit * jnp.sum(unit * gradient, axis=-1, keepdims=True))


def adamw_update(current, gradient, mean_old, square_old, step_scale, decay_rate):
    mean_new = first_decay * mean_old + (1.0 - first_decay) * gradient
    square_new = second_decay * square_old + (1.0 - second_decay) * gradient * gradient
    moved = mean_new / first_fix / (jnp.sqrt(square_new / second_fix) + adam_epsilon)
    return (step_scale * (moved + decay_rate * current), mean_new)


class Place:
    def __init__(self):
        dp, z = lax.axis_index("dp"), lax.axis_index("tensor")
        self.dp, self.z = dp, z
        self.core, self.col, self.row = dp % 2, (dp // 2) % 2, dp // 4
        self.x = (dp + 2 * (1 - 2 * self.col), z)
        self.y = (dp + 4 * (1 - 2 * self.row), z)
        self.sibling = (dp + 1 - 2 * self.core, z)

    def along(self, j):
        return (self.dp, (self.z + j) % 4)


def greet(place):
    barrier = pltpu.get_barrier_semaphore()
    targets = [place.x, place.y, place.sibling] + [place.along(j) for j in (1, 2, 3)]
    for target in targets:
        pl.semaphore_signal(barrier, inc=1, device_id=target, device_id_type=MESH)
    pl.semaphore_wait(barrier, 6)


def remote(source, target_ref, sends, receives, device):
    return pltpu.make_async_remote_copy(
        src_ref=source,
        dst_ref=target_ref,
        send_sem=sends,
        recv_sem=receives,
        device_id=device,
        device_id_type=MESH,
    )


class Line:
    def __init__(self, place, full, sends, receives):
        self.copies = [
            remote(
                full.at[place.z], full.at[place.z], sends.at[k], receives.at[k], place.along(k + 1)
            )
            for k in range(3)
        ]

    def start(self):
        for copy in self.copies:
            copy.start()

    def wait(self):
        for copy in self.copies:
            copy.wait_recv()

    def drain(self):
        for copy in self.copies:
            copy.wait_send()


class Gather:
    def __init__(self, place, full, sends, receives, w):
        self.place, self.full, self.w = place, full, w
        self.sends, self.receives = sends, receives
        self.flat = len(full.shape) == 5

    def copy(self, k):
        place, full = self.place, self.full
        row, col, core, z = place.row, place.col, place.core, place.z
        if k < 3:
            view, target = full.at[z, row, col, core], place.along(k + 1)
        elif k < 15:
            j = (k - 3) // 3
            if self.flat:
                view = full.at[row, col, core]
            else:
                view = full.at[(z + j) % 4, row, col, core]
            target = (place.x, place.y, place.sibling)[(k - 3) % 3]
        elif k < 17:
            spot = (row, 1 - col, core) if k == 15 else (1 - row, col, core)
            if self.flat:
                half = full.shape[3] // 2
                view = full.at[spot + (pl.ds((k - 15) * half, half),)]
            else:
                view = full.at[(pl.ds((k - 15) * 2, 2),) + spot]
            target = place.y if k == 15 else place.x
        else:
            spot = ((row, 1 - col, core), (1 - row, col, core), (1 - row, 1 - col, core))[k - 17]
            view = full.at[spot] if self.flat else full.at[(slice(None),) + spot]
            target = place.sibling
        return remote(view, view, self.sends.at[self.w, k], self.receives.at[self.w, k], target)

    def pieces(self):
        return range(1 if self.flat else 4)

    def start(self):
        if not self.flat:
            for k in range(3):
                self.copy(k).start()
        for k in (3, 4, 5):
            self.copy(k).start()

    def spread(self):
        if not self.flat:
            for j in (1, 2, 3):
                self.copy(j - 1).wait_recv()
                for k in range(3):
                    self.copy(3 + 3 * (4 - j) + k).start()

    def forward(self):
        for j in self.pieces():
            self.copy(3 + 3 * j).wait_recv()
        self.copy(15).start()
        self.copy(17).start()
        for j in self.pieces():
            self.copy(4 + 3 * j).wait_recv()
        self.copy(16).start()
        self.copy(18).start()

    def across(self):
        self.copy(15).wait_recv()
        self.copy(16).wait_recv()
        self.copy(19).start()

    def last(self):
        for j in self.pieces():
            self.copy(5 + 3 * j).wait_recv()
        for k in (17, 18, 19):
            self.copy(k).wait_recv()

    def drain(self):
        if not self.flat:
            for k in range(3):
                self.copy(k).wait_send()
        for j in self.pieces():
            for k in range(3):
                self.copy(3 + 3 * j + k).wait_send()
        for k in range(15, 20):
            self.copy(k).wait_send()


class Scatter:
    def __init__(self, place, grad, buffers, sends, receives, w):
        self.place, self.grad, self.w = place, grad, w
        self.sends, self.receives = sends, receives
        self.r1, self.r2a, self.r2b, self.r3a, self.r3b, self.r4 = buffers

    def copy(self, k):
        place, r1 = self.place, self.r1
        row, col, core = place.row, place.col, place.core
        if k == 0:
            pair = (self.grad.at[:, :, :, 1 - core], r1, place.sibling)
        elif k == 1:
            pair = (r1.at[0:2, :, 1 - col], self.r2a, place.x)
        elif k == 2:
            pair = (r1.at[2:4, 1 - row], self.r2b, place.y)
        elif k == 3:
            pair = (r1.at[0:2, 1 - row, col], self.r3a, place.y)
        elif k == 4:
            pair = (r1.at[2:4, row, 1 - col], self.r3b, place.x)
        else:
            peer = place.along(k - 4)
            pair = (r1.at[peer[1], row, col], self.r4.at[k - 5], peer)
        return remote(
            pair[0], pair[1], self.sends.at[self.w, k], self.receives.at[self.w, k], pair[2]
        )

    def add(self, index, other):
        ref = self.r1
        ref[index] = (ref[index].astype(F32) + other.astype(F32)).astype(ref.dtype)

    def start(self):
        self.copy(0).start()

    def planes(self):
        core = self.place.core
        self.copy(0).wait_recv()

        def step(i, carry):
            t, y = i // 2, i % 2
            self.add((t, y), self.grad[t, y, :, core])
            return carry

        lax.fori_loop(0, 8, step, 0)
        self.copy(1).start()
        self.copy(2).start()

    def lines(self):
        col, row = self.place.col, self.place.row
        self.copy(1).wait_recv()
        for t in range(2):
            for y in range(2):
                self.add((t, y, col), self.r2a[t, y])
        self.copy(3).start()
        self.copy(2).wait_recv()
        for t in range(2):
            for x in range(2):
                self.add((2 + t, row, x), self.r2b[t, x])
        self.copy(4).start()

    def points(self):
        col, row = self.place.col, self.place.row
        self.copy(3).wait_recv()
        for t in range(2):
            self.add((t, row, col), self.r3a[t])
        self.copy(4).wait_recv()
        for t in range(2):
            self.add((2 + t, row, col), self.r3b[t])
        for k in (5, 6, 7):
            self.copy(k).start()

    def result(self):
        place = self.place
        for k in (5, 6, 7):
            self.copy(k).wait_recv()
        total = self.r1[place.z, place.row, place.col].astype(F32)
        for j in range(3):
            total = total + self.r4[j].astype(F32)
        return total

    def drain(self):
        for k in range(8):
            self.copy(k).wait_send()


def scatter_buffers(rows, cols, dtype):
    return [
        pltpu.VMEM((4, 2, 2, rows, cols), dtype),
        pltpu.VMEM((2, 2, rows, cols), dtype),
        pltpu.VMEM((2, 2, rows, cols), dtype),
        pltpu.VMEM((2, rows, cols), dtype),
        pltpu.VMEM((2, rows, cols), dtype),
        pltpu.VMEM((3, rows, cols), dtype),
    ]


HEAD_SET = 3
SPAN = 3 * HD
CUT = HEAD_SET * SPAN
TILE_ROWS, TILE_COLS = 16, 256


def whole(value):
    return value.reshape(-1, value.shape[-1])


def gelu_parts(values):
    cumulative = 0.5 * (1.0 + lax.erf(values * 0.7071067811865476))
    density = 0.3989422804014327 * jnp.exp(-0.5 * values * values)
    return values * cumulative, cumulative + values * density


def halo_copies(place, window, own, semaphores):
    before = remote(
        window.at[pl.ds(HALO, HALO)],
        window.at[pl.ds(HALO + own, HALO)],
        semaphores.at[0],
        semaphores.at[1],
        place.along(3),
    )
    after = remote(
        window.at[pl.ds(own, HALO)],
        window.at[pl.ds(0, HALO)],
        semaphores.at[2],
        semaphores.at[3],
        place.along(1),
    )
    return before, after


def loader(inputs, places, semaphores):
    return [
        pltpu.make_async_copy(source, target, semaphores.at[n])
        for n, (source, target) in enumerate(zip(inputs, places))
    ]


def step_kernel(*refs):
    inputs, outputs, held = refs[:12], refs[12:22], refs[22:34]
    (
        tokens,
        segments,
        mask_grad,
        gain_one,
        attend_weight,
        output_weight,
        gain_two,
        up_weight,
        down_weight,
        patch_weight,
        class_weight,
        class_embed,
    ) = held
    results = refs[34:44]
    (
        masks,
        d_resid,
        share_p,
        share_d,
        share_u,
        share_a,
        share_n,
        class_all,
        class_row,
        class_sum,
    ) = results
    (
        full_a,
        full_u,
        full_d,
        full_p,
        full_c,
        full_e,
        grad_d,
        grad_u,
        grad_p,
        grad_n,
        grad_c,
        joint,
        attended,
        resid_one,
        norm_two,
        hidden,
        slope,
        total,
        window,
        back_window,
        norm_one,
        embed,
        embed_wide,
        resid_low,
        unit_low,
        class_low,
        stack_p,
        stack_s,
        seg_wide,
        seg_col,
        seg_row,
        class_wide,
        r4_a,
    ) = refs[44:77]
    buffers = refs[77:107]
    (
        gather_sends,
        gather_receives,
        scatter_sends,
        scatter_receives,
        line_sems,
        halo_sems,
        in_sems,
        out_sems,
    ) = refs[107:]
    loads = loader(inputs, held, in_sems)
    stores = loader(results, outputs, out_sems)
    for n in (11, 3, 6, 0, 4, 5, 10, 7, 8, 9, 1, 2):
        loads[n].start()

    place = Place()
    z, row, col, core = place.z, place.row, place.col, place.core
    own, width = tokens.shape
    span = own + 2 * HALO
    piece = width // 8
    narrow = patch_weight.shape[1]
    classes = class_embed.shape[0]
    mine = slice(HALO, HALO + own)
    ge, ga, gc, gu, gd, gp, gs = (
        Gather(place, full, gather_sends, gather_receives, w)
        for w, full in enumerate((full_e, full_a, full_c, full_u, full_d, full_p, class_sum))
    )
    sp, sd, su, sn, sc = (
        Scatter(place, g, buffers[6 * w : 6 * w + 6], scatter_sends, scatter_receives, w)
        for w, g in enumerate((grad_p, grad_d, grad_u, grad_n, grad_c))
    )
    a_buffers = (
        full_d.at[:, :, :, 0],
        full_d.at[0:2, :, 0, 1],
        full_d.at[2:4, :, 0, 1],
        full_d.at[0:2, 0, 1, 1],
        full_d.at[2:4, 0, 1, 1],
        r4_a,
    )
    grad_a = full_u
    sa = Scatter(place, grad_a, a_buffers, scatter_sends, scatter_receives, 5)
    line_row = Line(place, class_row, line_sems.at[0], line_sems.at[1])
    line_all = Line(place, class_all, line_sems.at[2], line_sems.at[3])

    embed_wide[...] = jnp.zeros_like(embed_wide)
    for n in (11, 3, 6):
        loads[n].wait()
    embed_wide[0:classes] = class_embed[...]
    embed_wide[classes : classes + 1] = gain_one[...]
    embed_wide[classes + 1 : classes + 2] = gain_two[...]
    full_e[row, col, core] = embed_wide[...].astype(BF)
    greet(place)
    ge.start()
    loads[0].wait()
    window[mine] = tokens[...]
    before, after = halo_copies(place, window, own, halo_sems.at[0])
    before.start()
    after.start()
    loads[4].wait()
    loads[5].wait()
    full_a[z, row, col, core, :, 0:CUT] = attend_weight[...].astype(BF)
    full_a[z, row, col, core, :, CUT:] = output_weight[...].T.astype(BF)
    ga.start()
    loads[10].wait()
    full_c[row, col, core] = class_weight[...].astype(BF)
    gc.start()
    class_row[z] = class_weight[...].astype(BF)
    line_row.start()
    loads[7].wait()
    full_u[z, row, col, core] = up_weight[...].astype(BF)
    gu.start()
    loads[8].wait()
    loads[9].wait()
    full_d[z, row, col, core] = down_weight[...].astype(BF)
    full_p[z, row, col, core] = patch_weight[...].astype(BF)

    loads[1].wait()
    loads[2].wait()
    seg_wide[...] = jnp.full_like(seg_wide, -1.0)
    seg_wide[:, HALO : HALO + segments.shape[1]] = segments[...].astype(F32)
    seg_row[...] = seg_wide[:, pl.ds(pl.multiple_of(z * own, 128), span)]
    seg_col[...] = jnp.broadcast_to(seg_row[...], (8, span)).T[:, 0:1]

    ge.forward()
    ge.across()
    ga.spread()
    ge.last()
    gd.start()
    gc.forward()
    before.wait_recv()
    after.wait_recv()
    for d in range(8):
        embed[:, d * piece : (d + 1) * piece] = full_e[d // 4, (d // 2) % 2, d % 2]
    gains = embed[classes : classes + 2, :].astype(F32)
    gain_first, gain_second = gains[0:1], gains[1:2]

    def first_norm(i, carry):
        rows = pl.ds(pl.multiple_of(i * 128, 128), 128)
        xhat, _ = norm_parts(window[rows].astype(F32))
        norm_one[rows] = (xhat * gain_first).astype(BF)
        return carry

    lax.fori_loop(0, span // 128, first_norm, 0)
    gu.spread()
    ga.forward()
    gc.across()
    ga.across()
    gc.last()
    gd.spread()
    gp.start()
    class_all[z] = dot(embed[...], whole(full_c[...]))
    line_all.start()
    line_row.wait()
    stores[8].start()
    ga.last()

    def project(t, carry):
        joint[t] = dot(norm_one[...], whole(full_a[t])[:, :CUT]).astype(BF)
        return carry

    lax.fori_loop(0, 4, project, 0)
    gu.forward()

    def attend(t, carry):
        for h in range(HEAD_SET):
            q_cols = slice(h * SPAN, h * SPAN + HD)
            k_cols = slice(h * SPAN + HD, h * SPAN + 2 * HD)
            v_cols = slice(h * SPAN + 2 * HD, h * SPAN + 3 * HD)
            for b in range(own // 128):
                near = slice(b * 128, b * 128 + 384)
                rows = slice(HALO + b * 128, HALO + (b + 1) * 128)
                scores = dot(joint[t, rows, q_cols], joint[t, near, k_cols], ((1,), (1,)))
                match = seg_col[rows] == seg_row[:, near]
                scores = jnp.where(match, scores * HD**-0.5, masked_score)
                exponent = jnp.exp(scores - jnp.max(scores, axis=-1, keepdims=True))
                row_total = jnp.sum(exponent, axis=-1, keepdims=True)
                prob = (exponent / row_total).astype(BF)
                attended[t, b * 128 : (b + 1) * 128, h * HD : (h + 1) * HD] = dot(
                    prob, joint[t, near, v_cols]
                ).astype(BF)
        return carry

    lax.fori_loop(0, 2, attend, 0)
    gp.spread()
    gu.across()
    lax.fori_loop(2, 4, attend, 0)
    gd.forward()
    resid_one[...] = tokens[...].astype(F32)

    def output(t, carry):
        resid_one[...] += dot(attended[t], whole(full_a[t])[:, CUT:], ((1,), (1,)))
        return carry

    lax.fori_loop(0, 4, output, 0)
    xhat, _ = norm_parts(resid_one[...])
    norm_two[...] = (xhat * gain_second).astype(BF)
    line_all.wait()
    stores[7].start()
    class_square = jnp.zeros((class_all.shape[1], 1), F32)
    for t in range(4):
        class_square += jnp.sum(class_all[t] * class_all[t], axis=-1, keepdims=True)
    class_inverse = lax.rsqrt(class_square + epsilon_unit)
    for t in range(4):
        class_low[t] = (class_all[t] * class_inverse).astype(BF)
    gu.last()
    gp.forward()

    def expand(t, carry):
        value, derivative = gelu_parts(dot(norm_two[...], whole(full_u[t])))
        hidden[t] = value.astype(BF)
        slope[t] = derivative.astype(BF)
        return carry

    lax.fori_loop(0, 4, expand, 0)
    gd.across()
    gp.across()
    gd.last()
    total[...] = resid_one[...]

    def contract(t, carry):
        total[...] += dot(hidden[t], whole(full_d[t]), ((1,), (1,)))
        return carry

    lax.fori_loop(0, 4, contract, 0)
    resid_low[...] = total[...].astype(BF)
    gp.last()

    square = jnp.zeros((own, 1), F32)
    pieces = []
    for t in range(4):
        value = dot(resid_low[...], whole(full_p[t]))
        square += jnp.sum(value * value, axis=-1, keepdims=True)
        pieces.append(value)
    inverse = lax.rsqrt(square + epsilon_unit)
    products = jnp.zeros((class_low.shape[1], own), F32)
    for t in range(4):
        pieces[t] = pieces[t] * inverse
        unit_low[t] = pieces[t].astype(BF)
        products += dot(class_low[t], unit_low[t], ((1,), (1,)))
    products = products[:classes]
    centred = products - jnp.mean(products, axis=0, keepdims=True)
    spread = jnp.mean(centred * centred, axis=0, keepdims=True)
    mask_inverse = lax.rsqrt(spread + epsilon_norm)
    centred = centred * mask_inverse
    masks[...] = centred
    stores[0].start()
    d_masks = mask_grad[...]
    d_products = mask_inverse * (
        d_masks
        - jnp.mean(d_masks, axis=0, keepdims=True)
        - centred * jnp.mean(d_masks * centred, axis=0, keepdims=True)
    )
    d_products = d_products.astype(BF)
    along = jnp.zeros((own, 1), F32)
    d_pieces = []
    for t in range(4):
        value = dot(d_products, class_low[t, :classes], ((0,), (0,)))
        along += jnp.sum(value * pieces[t], axis=-1, keepdims=True)
        d_pieces.append(value)
    flipped = resid_low[...].T
    d_total = jnp.zeros((own, width), F32)
    for t in range(4):
        value = (inverse * (d_pieces[t] - pieces[t] * along)).astype(BF)
        grad_p[t] = dot(flipped, value).astype(BF).reshape(grad_p.shape[1:])
        d_total += dot(value, whole(full_p[t]), ((1,), (1,)))
    sp.start()
    d_resid[...] = d_total
    branch = d_total.astype(BF)
    flipped = branch.T

    def down(t, carry):
        grad_d[t] = dot(flipped, hidden[t]).astype(BF).reshape(grad_d.shape[1:])
        return carry

    lax.fori_loop(0, 4, down, 0)
    sd.start()
    sp.planes()
    flipped = norm_two[...].T

    def up(t, carry):
        back = dot(branch, whole(full_d[t])) * slope[t].astype(F32)
        back = back.astype(BF)
        slope[t] = back
        grad_u[t] = dot(flipped, back).astype(BF).reshape(grad_u.shape[1:])
        return carry

    lax.fori_loop(0, 4, up, 0)
    sd.planes()
    for transfer in (ge, ga, gc, gu, gd, gp):
        transfer.drain()
    su.start()
    class_wide[...] = jnp.zeros_like(class_wide)
    for t in range(4):
        class_wide[0:classes, t * narrow : (t + 1) * narrow] = dot(
            d_products, unit_low[t]
        )
    grad_c[...] = jnp.zeros_like(grad_c)
    tiles = width // TILE_COLS
    for i in range(class_wide.shape[0] // TILE_ROWS * tiles):
        r, q = i // tiles, i % tiles
        grad_c[i // 8, (i // 4) % 2, (i // 2) % 2, i % 2] = class_wide[
            r * TILE_ROWS : (r + 1) * TILE_ROWS, q * TILE_COLS : (q + 1) * TILE_COLS
        ].astype(BF)
    sc.start()
    total[...] = jnp.zeros_like(total)

    def narrow_back(t, carry):
        total[...] += dot(slope[t], whole(full_u[t]), ((1,), (1,)))
        return carry

    lax.fori_loop(0, 4, narrow_back, 0)
    su.planes()
    sc.planes()
    xhat, inverse = norm_parts(resid_one[...])
    gain_two_sum = jnp.sum(total[...] * xhat, axis=0, keepdims=True)
    d_resid[...] += norm_back(total[...] * gain_second, xhat, inverse)
    back_window[mine] = d_resid[...].astype(BF)
    back_before, back_after = halo_copies(place, back_window, own, halo_sems.at[1])
    back_before.start()
    back_after.start()
    sp.lines()
    flipped = back_window[mine].T

    def outer(t, carry):
        block = dot(flipped, attended[t]).astype(BF)
        grad_a[t, :, :, :, :, CUT:] = block.reshape((2, 2, 2, piece, width - CUT))
        return carry

    lax.fori_loop(0, 4, outer, 0)
    sc.lines()
    back_before.wait_recv()
    back_after.wait_recv()

    def attended_back(t, carry):
        value = dot(back_window[...], whole(full_a[t])[:, CUT:]).astype(BF)
        slope[t, :, 0:narrow] = value[0:own]
        slope[t, :, 256 : 256 + narrow] = value[own:span]
        return carry

    lax.fori_loop(0, 4, attended_back, 0)
    sd.lines()
    sp.points()
    sc.points()
    stack_p[...] = jnp.zeros_like(stack_p)
    stack_s[...] = jnp.zeros_like(stack_s)

    def attend_back(t, carry):
        for h in range(HEAD_SET):
            q_cols = slice(h * SPAN, h * SPAN + HD)
            k_cols = slice(h * SPAN + HD, h * SPAN + 2 * HD)
            v_cols = slice(h * SPAN + 2 * HD, h * SPAN + 3 * HD)
            for b in range(4):
                rows = slice(b * 128, (b + 1) * 128)
                low_key, high_key = max(b - 1, 0) * 128, min(b + 2, 4) * 128
                near = slice(low_key, high_key)
                key = joint[t, near, k_cols]
                scores = dot(joint[t, rows, q_cols], key, ((1,), (1,)))
                match = seg_col[rows] == seg_row[:, near]
                scores = jnp.where(match, scores * HD**-0.5, masked_score)
                exponent = jnp.exp(scores - jnp.max(scores, axis=-1, keepdims=True))
                prob = exponent / jnp.sum(exponent, axis=-1, keepdims=True)
                d_cols = slice(b // 2 * 256 + h * HD, b // 2 * 256 + (h + 1) * HD)
                d_rows = slice(b % 2 * 128, (b % 2 + 1) * 128)
                d_prob = dot(slope[t, d_rows, d_cols], joint[t, near, v_cols], ((1,), (1,)))
                delta = jnp.sum(prob * d_prob, axis=-1, keepdims=True)
                d_scores = (prob * (d_prob - delta)).astype(BF)
                prob = prob.astype(BF)
                first, last = max(low_key, HALO), min(high_key, HALO + own)
                place_in = slice(first - HALO, last - HALO)
                part = slice(first - low_key, last - low_key)
                stack_p[rows, place_in] = prob[:, part]
                stack_s[rows, place_in] = d_scores[:, part]
                if b in (1, 2):
                    hidden[t, (b - 1) * 128 : b * 128, q_cols] = (
                        dot(d_scores, key) * HD**-0.5
                    ).astype(BF)
            hidden[t, :, k_cols] = (
                dot(stack_s[...], joint[t, :, q_cols], ((0,), (0,))) * HD**-0.5
            ).astype(BF)
            d_value = dot(stack_p[0:own], slope[t, :, h * HD : (h + 1) * HD], ((0,), (0,)))
            d_value += dot(
                stack_p[own:span], slope[t, :, 256 + h * HD : 256 + (h + 1) * HD], ((0,), (0,))
            )
            hidden[t, :, v_cols] = d_value.astype(BF)
        return carry

    lax.fori_loop(0, 2, attend_back, 0)
    su.lines()
    class_sum[z, row, col, core] = sc.result().astype(BF)
    gs.start()
    lax.fori_loop(2, 4, attend_back, 0)
    gs.spread()
    flipped = norm_one[mine].T

    def attend_grad(t, carry):
        block = dot(flipped, hidden[t, :, :CUT]).astype(BF)
        grad_a[t, :, :, :, :, :CUT] = block.reshape((2, 2, 2, piece, CUT))
        return carry

    lax.fori_loop(0, 4, attend_grad, 0)
    sa.start()
    sd.points()
    sa.planes()
    total[...] = jnp.zeros_like(total)

    def joint_back(t, carry):
        total[...] += dot(hidden[t, :, :CUT], whole(full_a[t])[:, :CUT], ((1,), (1,)))
        return carry

    lax.fori_loop(0, 4, joint_back, 0)
    su.points()
    gs.forward()
    xhat, inverse = norm_parts(tokens[...].astype(F32))
    gain_one_sum = jnp.sum(total[...] * xhat, axis=0, keepdims=True)
    d_resid[...] += norm_back(total[...] * gain_first, xhat, inverse)
    stores[1].start()
    grad_n[...] = jnp.zeros_like(grad_n)
    for d in range(8):
        cols = slice(d * piece, (d + 1) * piece)
        for t in range(4):
            spot = (t, d // 4, (d // 2) % 2, d % 2)
            grad_n[spot + (slice(0, 1), slice(0, piece))] = gain_one_sum[:, cols]
            grad_n[spot + (slice(1, 2), slice(0, piece))] = gain_two_sum[:, cols]
    sn.start()
    sn.planes()
    share_p[...] = sp.result()
    stores[2].start()
    sa.lines()
    sn.lines()
    gs.across()
    share_d[...] = sd.result()
    stores[3].start()
    gs.last()
    stores[9].start()
    sa.points()
    sn.points()
    share_u[...] = su.result()
    stores[4].start()
    share_n[...] = sn.result()
    stores[6].start()
    share_a[...] = sa.result()
    stores[5].start()
    for copy in (before, after, back_before, back_after):
        copy.wait_send()
    for transfer in (gs, sp, sd, su, sn, sc, sa, line_row, line_all):
        transfer.drain()
    for store in stores:
        store.wait()


def vmem_specs(count):
    return [pl.BlockSpec(memory_space=pltpu.VMEM)] * count


def any_specs(count):
    return [pl.BlockSpec(memory_space=pl.ANY)] * count


def step_call(tokens, segments, mask_grad, params):
    own, width = tokens.shape
    gain_one, attend, output, gain_two, up, down, patch, classed, embed = params
    classes = embed.shape[0]
    rows_e = -(-(classes + 2) // 32) * 32
    piece, high, narrow = up.shape[0], up.shape[1], patch.shape[1]
    span = own + 2 * HALO
    low = lambda *shape: pltpu.VMEM(shape, BF)
    wide = lambda *shape: pltpu.VMEM(shape, F32)
    shape = jax.ShapeDtypeStruct
    operands = (tokens, segments, mask_grad, gain_one[None], attend, output, gain_two[None])
    operands += tuple(params[4:])
    outs = [
        shape((classes, own), F32),
        shape((own, width), F32),
        shape((piece, narrow), F32),
        shape((piece, high), F32),
        shape((piece, high), F32),
        shape((piece, width), F32),
        shape((8, 128), F32),
        shape((4, rows_e, narrow), F32),
        shape((4, piece, narrow), BF),
        shape((4, 2, 2, 2, TILE_ROWS, TILE_COLS), BF),
    ]
    scratch = [pltpu.VMEM(v.shape, v.dtype) for v in operands]
    scratch += [pltpu.VMEM(v.shape, v.dtype) for v in outs]
    scratch += [
        low(4, 2, 2, 2, piece, width),
        low(4, 2, 2, 2, piece, high),
        low(4, 2, 2, 2, piece, high),
        low(4, 2, 2, 2, piece, narrow),
        low(2, 2, 2, piece, narrow),
        low(2, 2, 2, rows_e, piece),
        low(4, 2, 2, 2, piece, high),
        low(4, 2, 2, 2, piece, high),
        low(4, 2, 2, 2, piece, narrow),
        wide(4, 2, 2, 2, 8, 128),
        low(4, 2, 2, 2, TILE_ROWS, TILE_COLS),
        low(4, span, CUT),
        low(4, own, narrow),
        wide(own, width),
        low(own, width),
        low(4, own, high),
        low(4, own, high),
        wide(own, width),
        low(span, width),
        low(span, width),
        low(span, width),
        low(rows_e, width),
        wide(rows_e, piece),
        low(own, width),
        low(4, own, narrow),
        low(4, rows_e, narrow),
        low(span, own),
        low(span, own),
        wide(1, segments.shape[1] + 2 * HALO),
        wide(span, 1),
        wide(1, span),
        wide(rows_e, width),
        low(3, piece, width),
    ]
    for rows, cols, dtype in (
        (piece, narrow, BF),
        (piece, high, BF),
        (piece, high, BF),
        (8, 128, F32),
        (TILE_ROWS, TILE_COLS, BF),
    ):
        scratch += scatter_buffers(rows, cols, dtype)
    scratch += [
        pltpu.SemaphoreType.DMA((7, 20)),
        pltpu.SemaphoreType.DMA((7, 20)),
        pltpu.SemaphoreType.DMA((6, 8)),
        pltpu.SemaphoreType.DMA((6, 8)),
        pltpu.SemaphoreType.DMA((4, 3)),
        pltpu.SemaphoreType.DMA((2, 4)),
        pltpu.SemaphoreType.DMA((len(operands),)),
        pltpu.SemaphoreType.DMA((len(outs),)),
    ]
    return pl.pallas_call(
        step_kernel,
        out_shape=outs,
        in_specs=any_specs(len(operands)),
        out_specs=any_specs(len(outs)),
        scratch_shapes=scratch,
        compiler_params=pltpu.CompilerParams(
            collective_id=0, has_side_effects=True, vmem_limit_bytes=VMEM_LIMIT
        ),
    )(*operands)


def update_kernel(*refs):
    inputs, outputs, held = refs[:37], refs[37:57], refs[57:94]
    class_back, sum_wide, in_sems, out_sems = refs[94:]
    masks, token_grad, share_p, share_d, share_u, share_a, share_n = held[:7]
    class_all, class_row, class_sum = held[7:10]
    params, means, squares = held[10:19], held[19:28], held[28:37]
    loads = loader(inputs, held, in_sems)
    stores = loader(held[:2] + squares + means, outputs, out_sems)
    order = (0, 3, 6, 4, 5, 2, 1, 8, 7)
    for n in (6, 0, 1, 2, 4, 3, 5, 7, 8, 9):
        loads[n].start()
    for n in order:
        for k in (10, 19, 28):
            loads[k + n].start()
    for n in range(10):
        loads[n].wait()
        if n < 2:
            stores[n].start()

    def update(n, gradient):
        scale = block_scale if n < 6 else 1.0
        decay = 0.0 if n in (0, 3) else weight_decay
        for k in (10, 19, 28):
            if k + n != 18:
                loads[k + n].wait()
        squares[n][...], means[n][...] = adamw_update(
            params[n][...], gradient, means[n][...], squares[n][...], scale, decay
        )
        stores[2 + n].start()
        stores[11 + n].start()

    piece = share_p.shape[0]
    update(0, share_n[0:1, 0:piece])
    update(3, share_n[1:2, 0:piece])
    update(6, share_p[...])
    update(4, share_u[...])
    update(5, share_d[...])
    update(2, share_a[:, CUT:].T)
    update(1, share_a[:, :CUT])

    classes = params[8].shape[0]
    narrow = class_all.shape[2]
    tiles = sum_wide.shape[1] // TILE_COLS
    for i in range(sum_wide.shape[0] // TILE_ROWS * tiles):
        r, q = i // tiles, i % tiles
        sum_wide[
            r * TILE_ROWS : (r + 1) * TILE_ROWS, q * TILE_COLS : (q + 1) * TILE_COLS
        ] = class_sum[i // 8, (i // 4) % 2, (i // 2) % 2, i % 2].astype(F32)
    square = jnp.zeros((classes, 1), F32)
    for t in range(4):
        value = class_all[t, :classes]
        square += jnp.sum(value * value, axis=-1, keepdims=True)
    inverse = lax.rsqrt(square + epsilon_unit)
    along = jnp.zeros((classes, 1), F32)
    for t in range(4):
        unit = class_all[t, :classes] * inverse
        d_unit = sum_wide[:classes, t * narrow : (t + 1) * narrow]
        along += jnp.sum(unit * d_unit, axis=-1, keepdims=True)
    share_embed = jnp.zeros((classes, piece), F32)
    loads[18].wait()
    embed_low = params[8][...].astype(BF)
    for t in range(4):
        unit = class_all[t, :classes] * inverse
        d_unit = sum_wide[:classes, t * narrow : (t + 1) * narrow]
        value = (inverse * (d_unit - unit * along)).astype(BF)
        class_back[t] = value
        share_embed += dot(value, class_row[t], ((1,), (1,)))
    update(8, share_embed)
    update(7, dot(embed_low, class_back[lax.axis_index("tensor")], ((0,), (0,))))
    for store in stores:
        store.wait()


def update_call(results, params, means, squares):
    flat = lambda arrays: [a[None] if a.ndim == 1 else a for a in arrays]
    params, means, squares = flat(params), flat(means), flat(squares)
    classes, narrow = params[8].shape[0], params[7].shape[1]
    rows_e, width = results[7].shape[1], results[1].shape[1]
    operands = (*results, *params, *means, *squares)
    shape = jax.ShapeDtypeStruct
    outs = [shape(r.shape, F32) for r in results[:2]]
    outs += [shape(p.shape, F32) for p in params] * 2
    return pl.pallas_call(
        update_kernel,
        out_shape=outs,
        in_specs=any_specs(len(operands)),
        out_specs=any_specs(len(outs)),
        scratch_shapes=[pltpu.VMEM(v.shape, v.dtype) for v in operands]
        + [
            pltpu.VMEM((4, classes, narrow), BF),
            pltpu.VMEM((rows_e, width), F32),
            pltpu.SemaphoreType.DMA((len(operands),)),
            pltpu.SemaphoreType.DMA((len(outs),)),
        ],
        compiler_params=pltpu.CompilerParams(vmem_limit_bytes=VMEM_LIMIT),
    )(*operands)


def finish(masks, token_grad, grads, params, means, squares):
    scales = (block_scale,) * 6 + (1.0,) * 3
    decays = (0.0, weight_decay, weight_decay, 0.0) + (weight_decay,) * 5
    new = [adamw_update(*v) for v in zip(params, grads, means, squares, scales, decays)]
    return (masks, token_grad) + tuple(n[0] for n in new) + tuple(n[1] for n in new)


def gather_plain(shards, embed):
    def full(s):
        return lax.all_gather(lax.all_gather(s, "dp", axis=0), "tensor", axis=0)

    return [full(s) for s in shards] + [lax.all_gather(embed, "dp", axis=0)]


def scatter_plain(grads):
    def share(g):
        part = lax.psum_scatter(g, "dp", scatter_dimension=1, tiled=True)
        return lax.psum_scatter(part, "tensor", scatter_dimension=0, tiled=True)[0]

    return [share(g).astype(F32) for g in grads]


def with_halo(rows, parts):
    forward = [(i, i + 1) for i in range(parts - 1)]
    backward = [(i + 1, i) for i in range(parts - 1)]
    before = lax.ppermute(rows[-HALO:], "tensor", forward)
    after = lax.ppermute(rows[:HALO], "tensor", backward)
    return jnp.concatenate((before, rows, after), axis=0)


def local_plain(
    parts,
    tokens,
    segments,
    mask_grad,
    gain_one,
    attend_weight,
    output_weight,
    gain_two,
    up_weight,
    down_weight,
    patch_weight,
    class_weight,
    class_embed,
    *moments,
):
    means, squares = moments[:9], moments[9:]
    own = tokens.shape[0]
    width = tokens.shape[1]
    classes = class_embed.shape[0]
    dp_index = lax.axis_index("dp")
    tensor_index = lax.axis_index("tensor")
    low = lambda v: v.astype(BF)

    shard_a = jnp.concatenate((low(attend_weight), low(output_weight).T), axis=1)
    shard_u = low(up_weight)
    shard_d = low(down_weight).T
    shard_p = jnp.concatenate((low(patch_weight), low(class_weight)), axis=1)
    rows_e = -(-(classes + 2) // 32) * 32
    shard_e = jnp.zeros((rows_e, class_embed.shape[1]), BF)
    shard_e = shard_e.at[:classes].set(low(class_embed))
    shard_e = shard_e.at[classes].set(low(gain_one)).at[classes + 1].set(low(gain_two))
    full_a, full_u, full_d, full_p, full_e = gather_plain(
        (shard_a, shard_u, shard_d, shard_p), shard_e
    )
    full_a, full_u, full_d, full_p = (
        v.reshape(v.shape[0], width, v.shape[-1]) for v in (full_a, full_u, full_d, full_p)
    )
    embed_rows = full_e.transpose(1, 0, 2).reshape(rows_e, width)
    embed = embed_rows[:classes]
    gain_first = embed_rows[classes].astype(F32)[None]
    gain_second = embed_rows[classes + 1].astype(F32)[None]

    cut = attend_weight.shape[1]
    heads = cut // (3 * HD)
    w_attend, w_output = full_a[:, :, :cut], full_a[:, :, cut:]
    narrow = patch_weight.shape[1]
    w_patch, w_class = full_p[:, :, :narrow], full_p[:, :, narrow:]
    w_patch = w_patch.transpose(1, 0, 2).reshape(width, -1)
    w_class = w_class.transpose(1, 0, 2).reshape(width, -1)

    window = with_halo(tokens, parts)
    token_wide = window.astype(F32)
    xhat_one, inverse_one = norm_parts(token_wide)
    norm_one = low(xhat_one * gain_first)
    joint = jnp.einsum("sd,tdn->stn", norm_one, w_attend, preferred_element_type=F32)
    joint = low(joint).reshape(own + 2 * HALO, parts * heads, 3, HD)
    queries, keys, values = joint[:, :, 0], joint[:, :, 1], joint[:, :, 2]
    padded = jnp.pad(segments[0], HALO, constant_values=-1)
    seg = lax.dynamic_slice_in_dim(padded, tensor_index * own, own + 2 * HALO, 0)
    scores = jnp.einsum("qhd,khd->hqk", queries, keys, preferred_element_type=F32) * HD**-0.5
    scores = jnp.where(seg[None, :, None] == seg[None, None, :], scores, masked_score)
    exponent = jnp.exp(scores - jnp.max(scores, axis=-1, keepdims=True))
    prob = exponent / jnp.sum(exponent, axis=-1, keepdims=True)
    prob_low = low(prob)
    mine = slice(HALO, HALO + own)
    attended = jnp.einsum(
        "hqk,khd->qhd", prob_low[:, mine], values, preferred_element_type=F32
    )
    attended = low(attended).reshape(own, parts, heads * HD)
    resid_one = token_wide[mine] + jnp.einsum(
        "stn,tdn->sd", attended, w_output, preferred_element_type=F32
    )
    xhat_two, inverse_two = norm_parts(resid_one)
    norm_two = low(xhat_two * gain_second)
    hidden_pre = jnp.einsum("sd,tdn->stn", norm_two, full_u, preferred_element_type=F32)
    hidden, gelu_back = jax.vjp(lambda v: jax.nn.gelu(v, approximate=False), hidden_pre)
    hidden = low(hidden)
    resid_two = resid_one + jnp.einsum(
        "stn,tdn->sd", hidden, full_d, preferred_element_type=F32
    )
    resid_low = low(resid_two)
    patch_feat = dot(resid_low, w_patch)
    patch_wide, patch_inverse = unit_parts(patch_feat)
    patch_unit = low(patch_wide)
    class_feat = dot(embed, w_class)
    class_wide, class_inverse = unit_parts(class_feat)
    class_unit = low(class_wide)
    products = dot(patch_unit, class_unit, ((1,), (1,)))
    masks, mask_inverse = norm_parts(products)
    d_products = low(norm_back(mask_grad, masks, mask_inverse))
    d_class_unit = lax.psum(dot(d_products, patch_unit, ((0,), (0,))), ("dp", "tensor"))
    d_patch_unit = dot(d_products, class_unit)
    d_patch_feat = low(unit_back(d_patch_unit, patch_wide, patch_inverse))
    grad_patch = dot(resid_low, d_patch_feat, ((0,), (0,)))
    d_resid_two = dot(d_patch_feat, w_patch, ((1,), (1,)))
    d_branch_two = low(d_resid_two)
    d_hidden = jnp.einsum("sd,tdn->stn", d_branch_two, full_d, preferred_element_type=F32)
    grad_down = jnp.einsum("sd,stn->tdn", d_branch_two, hidden, preferred_element_type=F32)
    d_hidden_pre = low(gelu_back(d_hidden)[0])
    grad_up = jnp.einsum("sd,stn->tdn", norm_two, d_hidden_pre, preferred_element_type=F32)
    d_norm_two = jnp.einsum("stn,tdn->sd", d_hidden_pre, full_u, preferred_element_type=F32)
    d_resid_one = d_resid_two + norm_back(d_norm_two * gain_second, xhat_two, inverse_two)
    grad_gain_two = jnp.sum(d_norm_two * xhat_two, axis=0)
    d_branch_one = with_halo(low(d_resid_one), parts)
    d_attended = low(
        jnp.einsum("sd,tdn->stn", d_branch_one, w_output, preferred_element_type=F32)
    )
    grad_output = jnp.einsum(
        "sd,stn->tdn", d_branch_one[mine], attended, preferred_element_type=F32
    )
    d_attended = d_attended.reshape(own + 2 * HALO, parts * heads, HD)
    d_prob = jnp.einsum("qhd,khd->hqk", d_attended, values, preferred_element_type=F32)
    delta = jnp.sum(prob * d_prob, axis=-1, keepdims=True)
    d_scores = low(prob * (d_prob - delta))
    d_query = jnp.einsum(
        "hqk,khd->qhd", d_scores[:, mine], keys, preferred_element_type=F32
    )
    d_key = jnp.einsum(
        "hqk,qhd->khd", d_scores[:, :, mine], queries, preferred_element_type=F32
    )
    d_value = jnp.einsum(
        "hqk,qhd->khd", prob_low[:, :, mine], d_attended, preferred_element_type=F32
    )
    d_joint = low(
        jnp.stack((d_query * HD**-0.5, d_key * HD**-0.5, d_value), axis=2)
    ).reshape(own, parts, cut)
    grad_attend = jnp.einsum(
        "sd,stn->tdn", norm_one[mine], d_joint, preferred_element_type=F32
    )
    d_norm_one = jnp.einsum("stn,tdn->sd", d_joint, w_attend, preferred_element_type=F32)
    token_grad = d_resid_one + norm_back(
        d_norm_one * gain_first, xhat_one[mine], inverse_one[mine]
    )
    grad_gain_one = jnp.sum(d_norm_one * xhat_one[mine], axis=0)

    grad_patch = grad_patch.reshape(width, parts, narrow).transpose(1, 0, 2)
    share_p, share_d, share_u, share_a = scatter_plain(
        [
            grad_patch,
            grad_down,
            grad_up,
            jnp.concatenate((grad_attend, grad_output), axis=2),
        ]
    )
    gains = lax.psum((grad_gain_one, grad_gain_two), ("dp", "tensor"))
    step = gain_one.shape[0]
    share_one, share_two = (lax.dynamic_slice_in_dim(g, dp_index * step, step, 0) for g in gains)
    d_class_feat = low(unit_back(d_class_unit, class_wide, class_inverse))
    d_class_own = lax.dynamic_slice_in_dim(d_class_feat, tensor_index * narrow, narrow, 1)
    share_class = dot(low(class_embed), d_class_own, ((0,), (0,)))
    class_rows = lax.dynamic_slice_in_dim(w_class, dp_index * step, step, 0)
    share_embed = dot(d_class_feat, class_rows, ((1,), (1,)))
    return finish(
        masks,
        token_grad,
        (
            share_one,
            share_a[:, :cut],
            share_a[:, cut:].T,
            share_two,
            share_u,
            share_d.T,
            share_p,
            share_class,
            share_embed,
        ),
        (
            gain_one,
            attend_weight,
            output_weight,
            gain_two,
            up_weight,
            down_weight,
            patch_weight,
            class_weight,
            class_embed,
        ),
        means,
        squares,
    )


def local_kernels(tokens, segments, mask_grad, *arrays):
    def turned(group):
        return (*group[:5], group[5].T, *group[6:])

    params, means, squares = (turned(arrays[n : n + 9]) for n in (0, 9, 18))
    results = step_call(tokens, segments, mask_grad.T, params)
    masks, token_grad, *new = update_call(results, params, means, squares)
    new = [n.reshape(p.shape) for n, p in zip(new, params * 2)]
    return (masks.T, token_grad, *turned(new[:9]), *turned(new[9:]))


def solution(mesh):
    parts = mesh.shape["tensor"]
    custom = mesh.shape["dp"] == 8 and parts == 4
    params = (
        P("dp"),
        P("dp", "tensor"),
        P("tensor", "dp"),
        P("dp"),
        P("dp", "tensor"),
        P("tensor", "dp"),
        P("dp", "tensor"),
        P("dp", "tensor"),
        P(None, "dp"),
    )
    rows = P(("dp", "tensor"), None)
    return jax.shard_map(
        local_kernels if custom else functools.partial(local_plain, parts),
        mesh=mesh,
        in_specs=(rows, P("dp", None), rows) + params * 3,
        out_specs=(rows, rows) + params * 2,
        check_vma=False,
    )
```

time: 438 us -> 214 us (0.49); the launches traced: 431 us -> 214 us
  matrix products: 76.5 us -> 0 us
  other arithmetic: 54.7 us -> 0 us
  blocking collectives: 40.2 us -> 0 us
  local copies, waits for them, and re-layouts: 32.1 us -> 0 us
  Pallas kernels: 194 us -> 213 us
  starting transfers between devices: 17.4 us -> 0 us
  between operations: 15.2 us -> 0.85 us
    dot_general x24 -> x0, matrix products: 51.5 us -> none  [the longest x9 8.09 us: dot(): lax.dot_general(left, right, (dims, ((), ())), preferred_element_type=F32)]
    psum x1 -> x0, blocking collectives: 40.2 us -> none  [local(): gains = lax.psum((grad_gain_one, grad_gain_two), ('dp', 'tensor'))]
    convert_element_type x14 -> x0, other arithmetic: 26.1 us -> none  [the longest x12 24.3 us: local(): low = lambda v: v.astype(BF)]
    sub x2 -> x0, matrix products: 24.2 us -> none  [the longest x1 13.7 us: local(): d_scores = low(prob * (d_prob - delta))]
    pallas_call x2, Pallas kernels: 194 us -> 213 us  [the longest x1 207 us: step_call(): pl.pallas_call(step_kernel, out_shape=outs, in_specs=any_specs(len(operan...]
    ppermute x4 -> x0, starting transfers between devices: 17.4 us -> none  [the longest x2 14.8 us: with_halo(): before = lax.ppermute(rows[-HALO:], 'tensor', forward)]
    unnamed x121 -> x0, local copies, waits for them, and re-layouts: 15.5 us -> none
    mul x7 -> x0, other arithmetic: 10.7 us -> none  [the longest x6 8.36 us: adamw_update(): return (step_scale * (moved + decay_rate * current), mean_new)]
  transfers between devices with their start and end apart: 5 -> 0, of which waited for: 0 -> 0; matrix products, arithmetic and copies ran while one was open for 20% -> 0% of each run, Pallas kernels for 45% -> 0%
where the time goes in v3:
time: 214 us
  Pallas kernels  213 us (100%)
    pallas_call x1, Pallas kernels, step_call(): pl.pallas_call(step_kernel, out_shape=outs, in_specs=any_specs(len(operan...  207 us
    pallas_call x1, Pallas kernels, update_call(): pl.pallas_call(update_kernel, out_shape=outs, in_specs=any_specs(len(oper...  6.15 us

profile of v3, /device:TPU:0, one launch (start us, length us, event | category | flops | bytes accessed | tf_op | source)
XLA Modules:
  0.0 214.2 jit_solution(5800831585141638228)
XLA Ops:
  0.7 207.2 %shard_map.437 = (f32[150,256]{1,0:T(8,128)}, f32[256,768]{1,0:T(8,128)}, f32[96,192]{1,0:T(8,128)}, f32[96,768]{1,0:T(8,128)}, f32[96,768]{1,0:T(8,128)}, /*ind...) custom-call(bf16[256,768]{1,0:T(8,128)(2,1)} %refs_0_.1, ...), custom_call_target="tpu_custom_call" | custom-call | tf_op jit(solution)/shard_map/pallas_call | solution.py:903
  207.8 6.2 %shard_map.438 = (f32[150,256]{1,0:T(8,128)}, f32[256,768]{1,0:T(8,128)}, f32[1,96]{1,0:T(1,128)}, f32[96,576]{1,0:T(8,128)}, f32[192,96]{1,0:T(8,128)}, /*index...) custom-call(f32[150,256]{1,0:T(8,128)} %get-tuple-element.50.refs_0_, ...), custom_call_target="tpu_custom_call" | custom-call | tf_op jit(solution)/shard_map/pallas_call | solution.py:997

commit v4 on v3

--- a/solution.py
+++ b/solution.py
@@ -313,22 +313,66 @@
     return values * cumulative, cumulative + values * density
 
 
-def halo_copies(place, window, own, semaphores):
-    before = remote(
-        window.at[pl.ds(HALO, HALO)],
-        window.at[pl.ds(HALO + own, HALO)],
-        semaphores.at[0],
-        semaphores.at[1],
-        place.along(3),
-    )
-    after = remote(
-        window.at[pl.ds(own, HALO)],
-        window.at[pl.ds(0, HALO)],
-        semaphores.at[2],
-        semaphores.at[3],
-        place.along(1),
-    )
-    return before, after
+class Halo:
+    def __init__(self, place, window, own, semaphores):
+        edge = HALO + own
+        self.place, self.window, self.edge = place, window, edge
+        self.down = remote(
+            window.at[pl.ds(HALO, HALO)],
+            window.at[pl.ds(edge, HALO)],
+            semaphores.at[0],
+            semaphores.at[1],
+            place.along(3),
+        )
+        self.up = remote(
+            window.at[pl.ds(own, HALO)],
+            window.at[pl.ds(0, HALO)],
+            semaphores.at[2],
+            semaphores.at[3],
+            place.along(1),
+        )
+
+    def start(self):
+        z, window = self.place.z, self.window
+        blank = jnp.zeros((HALO, window.shape[1]), window.dtype)
+
+        @pl.when(z > 0)
+        def _():
+            self.down.start()
+
+        @pl.when(z < 3)
+        def _():
+            self.up.start()
+
+        @pl.when(z == 0)
+        def _():
+            window[0:HALO] = blank
+
+        @pl.when(z == 3)
+        def _():
+            window[self.edge : self.edge + HALO] = blank
+
+    def wait(self):
+        z = self.place.z
+
+        @pl.when(z < 3)
+        def _():
+            self.down.wait_recv()
+
+        @pl.when(z > 0)
+        def _():
+            self.up.wait_recv()
+
+    def drain(self):
+        z = self.place.z
+
+        @pl.when(z > 0)
+        def _():
+            self.down.wait_send()
+
+        @pl.when(z < 3)
+        def _():
+            self.up.wait_send()
 
 
 def loader(inputs, places, semaphores):
@@ -387,22 +431,21 @@
         slope,
         total,
         window,
-        back_window,
         norm_one,
         embed,
         embed_wide,
         resid_low,
         unit_low,
         class_low,
-        stack_p,
-        stack_s,
+        probs,
+        stack,
         seg_wide,
         seg_col,
         seg_row,
         class_wide,
         r4_a,
-    ) = refs[44:77]
-    buffers = refs[77:107]
+    ) = refs[44:76]
+    buffers = refs[76:106]
     (
         gather_sends,
         gather_receives,
@@ -412,7 +455,7 @@
         halo_sems,
         in_sems,
         out_sems,
-    ) = refs[107:]
+    ) = refs[106:]
     loads = loader(inputs, held, in_sems)
     stores = loader(results, outputs, out_sems)
     for n in (11, 3, 6, 0, 4, 5, 10, 7, 8, 9, 1, 2):
@@ -434,16 +477,26 @@
         Scatter(place, g, buffers[6 * w : 6 * w + 6], scatter_sends, scatter_receives, w)
         for w, g in enumerate((grad_p, grad_d, grad_u, grad_n, grad_c))
     )
-    a_buffers = (
-        full_d.at[:, :, :, 0],
-        full_d.at[0:2, :, 0, 1],
-        full_d.at[2:4, :, 0, 1],
-        full_d.at[0:2, 0, 1, 1],
-        full_d.at[2:4, 0, 1, 1],
-        r4_a,
-    )
     grad_a = full_u
-    sa = Scatter(place, grad_a, a_buffers, scatter_sends, scatter_receives, 5)
+    parts = (slice(0, piece // 2), slice(piece // 2, piece))
+    sa = [
+        Scatter(
+            place,
+            grad_a.at[:, :, :, :, part],
+            (
+                full_d.at[:, :, :, 0, part],
+                full_d.at[0:2, :, 0, 1, part],
+                full_d.at[2:4, :, 0, 1, part],
+                full_d.at[0:2, 0, 1, 1, part],
+                full_d.at[2:4, 0, 1, 1, part],
+                r4_a.at[:, part],
+            ),
+            scatter_sends,
+            scatter_receives,
+            5 + n,
+        )
+        for n, part in enumerate(parts)
+    ]
     line_row = Line(place, class_row, line_sems.at[0], line_sems.at[1])
     line_all = Line(place, class_all, line_sems.at[2], line_sems.at[3])
 
@@ -458,9 +511,8 @@
     ge.start()
     loads[0].wait()
     window[mine] = tokens[...]
-    before, after = halo_copies(place, window, own, halo_sems.at[0])
-    before.start()
-    after.start()
+    halo = Halo(place, window, own, halo_sems.at[0])
+    halo.start()
     loads[4].wait()
     loads[5].wait()
     full_a[z, row, col, core, :, 0:CUT] = attend_weight[...].astype(BF)
@@ -469,8 +521,6 @@
     loads[10].wait()
     full_c[row, col, core] = class_weight[...].astype(BF)
     gc.start()
-    class_row[z] = class_weight[...].astype(BF)
-    line_row.start()
     loads[7].wait()
     full_u[z, row, col, core] = up_weight[...].astype(BF)
     gu.start()
@@ -492,8 +542,7 @@
     ge.last()
     gd.start()
     gc.forward()
-    before.wait_recv()
-    after.wait_recv()
+    halo.wait()
     for d in range(8):
         embed[:, d * piece : (d + 1) * piece] = full_e[d // 4, (d // 2) % 2, d % 2]
     gains = embed[classes : classes + 2, :].astype(F32)
@@ -513,10 +562,8 @@
     gc.last()
     gd.spread()
     gp.start()
-    class_all[z] = dot(embed[...], whole(full_c[...]))
+    class_all[z] = dot(embed[...], whole(full_c[...])).astype(BF)
     line_all.start()
-    line_row.wait()
-    stores[8].start()
     ga.last()
 
     def project(t, carry):
@@ -525,30 +572,37 @@
 
     lax.fori_loop(0, 4, project, 0)
     gu.forward()
+
+    probs[...] = jnp.zeros_like(probs)
 
     def attend(t, carry):
         for h in range(HEAD_SET):
             q_cols = slice(h * SPAN, h * SPAN + HD)
             k_cols = slice(h * SPAN + HD, h * SPAN + 2 * HD)
             v_cols = slice(h * SPAN + 2 * HD, h * SPAN + 3 * HD)
-            for b in range(own // 128):
-                near = slice(b * 128, b * 128 + 384)
-                rows = slice(HALO + b * 128, HALO + (b + 1) * 128)
+            for b in range(4):
+                rows = slice(b * 128, (b + 1) * 128)
+                near = slice(max(b - 1, 0) * 128, min(b + 2, 4) * 128)
                 scores = dot(joint[t, rows, q_cols], joint[t, near, k_cols], ((1,), (1,)))
                 match = seg_col[rows] == seg_row[:, near]
                 scores = jnp.where(match, scores * HD**-0.5, masked_score)
                 exponent = jnp.exp(scores - jnp.max(scores, axis=-1, keepdims=True))
                 row_total = jnp.sum(exponent, axis=-1, keepdims=True)
                 prob = (exponent / row_total).astype(BF)
-                attended[t, b * 128 : (b + 1) * 128, h * HD : (h + 1) * HD] = dot(
-                    prob, joint[t, near, v_cols]
-                ).astype(BF)
+                probs[t, h, rows, near] = prob
+                if b in (1, 2):
+                    attended[t, (b - 1) * 128 : b * 128, h * HD : (h + 1) * HD] = dot(
+                        prob, joint[t, near, v_cols]
+                    ).astype(BF)
+
+        @pl.when(t == 1)
+        def _():
+            gp.spread()
+            gu.across()
+
         return carry
 
-    lax.fori_loop(0, 2, attend, 0)
-    gp.spread()
-    gu.across()
-    lax.fori_loop(2, 4, attend, 0)
+    lax.fori_loop(0, 4, attend, 0)
     gd.forward()
     resid_one[...] = tokens[...].astype(F32)
 
@@ -563,10 +617,11 @@
     stores[7].start()
     class_square = jnp.zeros((class_all.shape[1], 1), F32)
     for t in range(4):
-        class_square += jnp.sum(class_all[t] * class_all[t], axis=-1, keepdims=True)
+        value = class_all[t].astype(F32)
+        class_square += jnp.sum(value * value, axis=-1, keepdims=True)
     class_inverse = lax.rsqrt(class_square + epsilon_unit)
     for t in range(4):
-        class_low[t] = (class_all[t] * class_inverse).astype(BF)
+        class_low[t] = (class_all[t].astype(F32) * class_inverse).astype(BF)
     gu.last()
     gp.forward()
 
@@ -623,15 +678,17 @@
         along += jnp.sum(value * pieces[t], axis=-1, keepdims=True)
         d_pieces.append(value)
     flipped = resid_low[...].T
+    for t in range(4):
+        d_pieces[t] = (inverse * (d_pieces[t] - pieces[t] * along)).astype(BF)
+        grad_p[t] = dot(flipped, d_pieces[t]).astype(BF).reshape(grad_p.shape[1:])
+    sp.start()
     d_total = jnp.zeros((own, width), F32)
     for t in range(4):
-        value = (inverse * (d_pieces[t] - pieces[t] * along)).astype(BF)
-        grad_p[t] = dot(flipped, value).astype(BF).reshape(grad_p.shape[1:])
-        d_total += dot(value, whole(full_p[t]), ((1,), (1,)))
-    sp.start()
+        d_total += dot(d_pieces[t], whole(full_p[t]), ((1,), (1,)))
     d_resid[...] = d_total
     branch = d_total.astype(BF)
     flipped = branch.T
+    sp.planes()
 
     def down(t, carry):
         grad_d[t] = dot(flipped, hidden[t]).astype(BF).reshape(grad_d.shape[1:])
@@ -639,7 +696,8 @@
 
     lax.fori_loop(0, 4, down, 0)
     sd.start()
-    sp.planes()
+    class_row[z] = class_weight[...].astype(BF)
+    line_row.start()
     flipped = norm_two[...].T
 
     def up(t, carry):
@@ -647,18 +705,36 @@
         back = back.astype(BF)
         slope[t] = back
         grad_u[t] = dot(flipped, back).astype(BF).reshape(grad_u.shape[1:])
+
+        @pl.when(t == 1)
+        def _():
+            sd.planes()
+
         return carry
 
     lax.fori_loop(0, 4, up, 0)
-    sd.planes()
     for transfer in (ge, ga, gc, gu, gd, gp):
         transfer.drain()
     su.start()
+    total[...] = jnp.zeros_like(total)
+
+    def narrow_back(t, carry):
+        total[...] += dot(slope[t], whole(full_u[t]), ((1,), (1,)))
+        return carry
+
+    lax.fori_loop(0, 4, narrow_back, 0)
+    su.planes()
+    xhat, inverse = norm_parts(resid_one[...])
+    gain_two_sum = jnp.sum(total[...] * xhat, axis=0, keepdims=True)
+    d_resid[...] += norm_back(total[...] * gain_second, xhat, inverse)
+    halo.drain()
+    window[mine] = d_resid[...].astype(BF)
+    back_halo = Halo(place, window, own, halo_sems.at[1])
+    back_halo.start()
+    sp.lines()
     class_wide[...] = jnp.zeros_like(class_wide)
     for t in range(4):
-        class_wide[0:classes, t * narrow : (t + 1) * narrow] = dot(
-            d_products, unit_low[t]
-        )
+        class_wide[0:classes, t * narrow : (t + 1) * narrow] = dot(d_products, unit_low[t])
     grad_c[...] = jnp.zeros_like(grad_c)
     tiles = width // TILE_COLS
     for i in range(class_wide.shape[0] // TILE_ROWS * tiles):
@@ -667,24 +743,7 @@
             r * TILE_ROWS : (r + 1) * TILE_ROWS, q * TILE_COLS : (q + 1) * TILE_COLS
         ].astype(BF)
     sc.start()
-    total[...] = jnp.zeros_like(total)
-
-    def narrow_back(t, carry):
-        total[...] += dot(slope[t], whole(full_u[t]), ((1,), (1,)))
-        return carry
-
-    lax.fori_loop(0, 4, narrow_back, 0)
-    su.planes()
-    sc.planes()
-    xhat, inverse = norm_parts(resid_one[...])
-    gain_two_sum = jnp.sum(total[...] * xhat, axis=0, keepdims=True)
-    d_resid[...] += norm_back(total[...] * gain_second, xhat, inverse)
-    back_window[mine] = d_resid[...].astype(BF)
-    back_before, back_after = halo_copies(place, back_window, own, halo_sems.at[1])
-    back_before.start()
-    back_after.start()
-    sp.lines()
-    flipped = back_window[mine].T
+    flipped = window[mine].T
 
     def outer(t, carry):
         block = dot(flipped, attended[t]).astype(BF)
@@ -692,22 +751,20 @@
         return carry
 
     lax.fori_loop(0, 4, outer, 0)
-    sc.lines()
-    back_before.wait_recv()
-    back_after.wait_recv()
+    sc.planes()
+    back_halo.wait()
 
     def attended_back(t, carry):
-        value = dot(back_window[...], whole(full_a[t])[:, CUT:]).astype(BF)
+        value = dot(window[...], whole(full_a[t])[:, CUT:]).astype(BF)
         slope[t, :, 0:narrow] = value[0:own]
         slope[t, :, 256 : 256 + narrow] = value[own:span]
         return carry
 
     lax.fori_loop(0, 4, attended_back, 0)
     sd.lines()
-    sp.points()
-    sc.points()
-    stack_p[...] = jnp.zeros_like(stack_p)
-    stack_s[...] = jnp.zeros_like(stack_s)
+    line_row.wait()
+    stores[8].start()
+    stack[...] = jnp.zeros_like(stack)
 
     def attend_back(t, carry):
         for h in range(HEAD_SET):
@@ -718,43 +775,45 @@
                 rows = slice(b * 128, (b + 1) * 128)
                 low_key, high_key = max(b - 1, 0) * 128, min(b + 2, 4) * 128
                 near = slice(low_key, high_key)
-                key = joint[t, near, k_cols]
-                scores = dot(joint[t, rows, q_cols], key, ((1,), (1,)))
-                match = seg_col[rows] == seg_row[:, near]
-                scores = jnp.where(match, scores * HD**-0.5, masked_score)
-                exponent = jnp.exp(scores - jnp.max(scores, axis=-1, keepdims=True))
-                prob = exponent / jnp.sum(exponent, axis=-1, keepdims=True)
+                prob = probs[t, h, rows, near].astype(F32)
                 d_cols = slice(b // 2 * 256 + h * HD, b // 2 * 256 + (h + 1) * HD)
                 d_rows = slice(b % 2 * 128, (b % 2 + 1) * 128)
                 d_prob = dot(slope[t, d_rows, d_cols], joint[t, near, v_cols], ((1,), (1,)))
                 delta = jnp.sum(prob * d_prob, axis=-1, keepdims=True)
                 d_scores = (prob * (d_prob - delta)).astype(BF)
-                prob = prob.astype(BF)
                 first, last = max(low_key, HALO), min(high_key, HALO + own)
-                place_in = slice(first - HALO, last - HALO)
-                part = slice(first - low_key, last - low_key)
-                stack_p[rows, place_in] = prob[:, part]
-                stack_s[rows, place_in] = d_scores[:, part]
+                stack[rows, first - HALO : last - HALO] = d_scores[
+                    :, first - low_key : last - low_key
+                ]
                 if b in (1, 2):
                     hidden[t, (b - 1) * 128 : b * 128, q_cols] = (
-                        dot(d_scores, key) * HD**-0.5
+                        dot(d_scores, joint[t, near, k_cols]) * HD**-0.5
                     ).astype(BF)
             hidden[t, :, k_cols] = (
-                dot(stack_s[...], joint[t, :, q_cols], ((0,), (0,))) * HD**-0.5
+                dot(stack[...], joint[t, :, q_cols], ((0,), (0,))) * HD**-0.5
             ).astype(BF)
-            d_value = dot(stack_p[0:own], slope[t, :, h * HD : (h + 1) * HD], ((0,), (0,)))
-            d_value += dot(
-                stack_p[own:span], slope[t, :, 256 + h * HD : 256 + (h + 1) * HD], ((0,), (0,))
-            )
+            d_value = jnp.zeros((own, HD), F32)
+            for half in range(2):
+                d_value += dot(
+                    probs[t, h, half * own : (half + 1) * own, mine],
+                    slope[t, :, half * 256 + h * HD : half * 256 + (h + 1) * HD],
+                    ((0,), (0,)),
+                )
             hidden[t, :, v_cols] = d_value.astype(BF)
+
+        @pl.when(t == 0)
+        def _():
+            sp.points()
+            sc.lines()
+
+        @pl.when(t == 2)
+        def _():
+            su.lines()
+            sc.points()
+
         return carry
 
-    lax.fori_loop(0, 2, attend_back, 0)
-    su.lines()
-    class_sum[z, row, col, core] = sc.result().astype(BF)
-    gs.start()
-    lax.fori_loop(2, 4, attend_back, 0)
-    gs.spread()
+    lax.fori_loop(0, 4, attend_back, 0)
     flipped = norm_one[mine].T
 
     def attend_grad(t, carry):
@@ -763,9 +822,14 @@
         return carry
 
     lax.fori_loop(0, 4, attend_grad, 0)
-    sa.start()
+    for chunk in sa:
+        chunk.start()
     sd.points()
-    sa.planes()
+    class_sum[z, row, col, core] = sc.result().astype(BF)
+    gs.start()
+    for chunk in sa:
+        chunk.planes()
+    gs.spread()
     total[...] = jnp.zeros_like(total)
 
     def joint_back(t, carry):
@@ -788,26 +852,27 @@
             grad_n[spot + (slice(1, 2), slice(0, piece))] = gain_two_sum[:, cols]
     sn.start()
     sn.planes()
+    sa[0].lines()
     share_p[...] = sp.result()
     stores[2].start()
-    sa.lines()
+    gs.across()
     sn.lines()
-    gs.across()
+    sa[1].lines()
     share_d[...] = sd.result()
     stores[3].start()
     gs.last()
     stores[9].start()
-    sa.points()
+    sa[0].points()
     sn.points()
     share_u[...] = su.result()
     stores[4].start()
+    sa[1].points()
     share_n[...] = sn.result()
     stores[6].start()
-    share_a[...] = sa.result()
+    for chunk, part in zip(sa, parts):
+        share_a[part] = chunk.result()
     stores[5].start()
-    for copy in (before, after, back_before, back_after):
-        copy.wait_send()
-    for transfer in (gs, sp, sd, su, sn, sc, sa, line_row, line_all):
+    for transfer in (gs, sp, sd, su, sn, sc, *sa, line_row, line_all, back_halo):
         transfer.drain()
     for store in stores:
         store.wait()
@@ -841,7 +906,7 @@
         shape((piece, high), F32),
         shape((piece, width), F32),
         shape((8, 128), F32),
-        shape((4, rows_e, narrow), F32),
+        shape((4, rows_e, narrow), BF),
         shape((4, piece, narrow), BF),
         shape((4, 2, 2, 2, TILE_ROWS, TILE_COLS), BF),
     ]
@@ -868,13 +933,12 @@
         wide(own, width),
         low(span, width),
         low(span, width),
-        low(span, width),
         low(rows_e, width),
         wide(rows_e, piece),
         low(own, width),
         low(4, own, narrow),
         low(4, rows_e, narrow),
-        low(span, own),
+        low(4, HEAD_SET, span, span),
         low(span, own),
         wide(1, segments.shape[1] + 2 * HALO),
         wide(span, 1),
@@ -893,8 +957,8 @@
     scratch += [
         pltpu.SemaphoreType.DMA((7, 20)),
         pltpu.SemaphoreType.DMA((7, 20)),
-        pltpu.SemaphoreType.DMA((6, 8)),
-        pltpu.SemaphoreType.DMA((6, 8)),
+        pltpu.SemaphoreType.DMA((7, 8)),
+        pltpu.SemaphoreType.DMA((7, 8)),
         pltpu.SemaphoreType.DMA((4, 3)),
         pltpu.SemaphoreType.DMA((2, 4)),
         pltpu.SemaphoreType.DMA((len(operands),)),
@@ -962,19 +1026,19 @@
         ] = class_sum[i // 8, (i // 4) % 2, (i // 2) % 2, i % 2].astype(F32)
     square = jnp.zeros((classes, 1), F32)
     for t in range(4):
-        value = class_all[t, :classes]
+        value = class_all[t, :classes].astype(F32)
         square += jnp.sum(value * value, axis=-1, keepdims=True)
     inverse = lax.rsqrt(square + epsilon_unit)
     along = jnp.zeros((classes, 1), F32)
     for t in range(4):
-        unit = class_all[t, :classes] * inverse
+        unit = class_all[t, :classes].astype(F32) * inverse
         d_unit = sum_wide[:classes, t * narrow : (t + 1) * narrow]
         along += jnp.sum(unit * d_unit, axis=-1, keepdims=True)
     share_embed = jnp.zeros((classes, piece), F32)
     loads[18].wait()
     embed_low = params[8][...].astype(BF)
     for t in range(4):
-        unit = class_all[t, :classes] * inverse
+        unit = class_all[t, :classes].astype(F32) * inverse
         d_unit = sum_wide[:classes, t * narrow : (t + 1) * narrow]
         value = (inverse * (d_unit - unit * along)).astype(BF)
         class_back[t] = value

time: 214 us -> 199 us (0.930)
  Pallas kernels: 213 us -> 198 us
    pallas_call x1, Pallas kernels: 207 us -> 192 us  [step_call(): pl.pallas_call(step_kernel, out_shape=outs, in_specs=any_specs(len(operan...]
where the time goes in v4:
time: 199 us; the launch traced here: 198 us
  Pallas kernels  198 us (99%)
    pallas_call x1, Pallas kernels, step_call(): pl.pallas_call(step_kernel, out_shape=outs, in_specs=any_specs(len(operan...  192 us
    pallas_call x1, Pallas kernels, update_call(): pl.pallas_call(update_kernel, out_shape=outs, in_specs=any_specs(len(oper...  6.05 us

profile of v4, /device:TPU:0, one launch (start us, length us, event | category | flops | bytes accessed | tf_op | source)
XLA Modules:
  0.0 198.5 jit_solution(13182970091335512373)
XLA Ops:
  0.7 191.6 %shard_map.437 = (f32[150,256]{1,0:T(8,128)}, f32[256,768]{1,0:T(8,128)}, f32[96,192]{1,0:T(8,128)}, f32[96,768]{1,0:T(8,128)}, f32[96,768]{1,0:T(8,128)}, /*ind...) custom-call(bf16[256,768]{1,0:T(8,128)(2,1)} %refs_0_.1, ...), custom_call_target="tpu_custom_call" | custom-call | tf_op jit(solution)/shard_map/pallas_call | solution.py:967
  192.3 6.1 %shard_map.438 = (f32[150,256]{1,0:T(8,128)}, f32[256,768]{1,0:T(8,128)}, f32[1,96]{1,0:T(1,128)}, f32[96,576]{1,0:T(8,128)}, f32[192,96]{1,0:T(8,128)}, /*index...) custom-call(f32[150,256]{1,0:T(8,128)} %get-tuple-element.50.refs_0_, ...), custom_call_target="tpu_custom_call" | custom-call | tf_op jit(solution)/shard_map/pallas_call | solution.py:1061

commit v5 on v4

--- a/solution.py
+++ b/solution.py
@@ -131,7 +131,9 @@
         place, full = self.place, self.full
         row, col, core, z = place.row, place.col, place.core, place.z
         if k < 3:
-            view, target = full.at[z, row, col, core], place.along(k + 1)
+            view, target = full.at[z - k, row, col, core], place.along(1)
+        elif k >= 20:
+            view, target = full.at[z + k - 20, row, col, core], place.along(3)
         elif k < 15:
             j = (k - 3) // 3
             if self.flat:
@@ -157,18 +159,46 @@
         return range(1 if self.flat else 4)
 
     def start(self):
-        if not self.flat:
-            for k in range(3):
-                self.copy(k).start()
         for k in (3, 4, 5):
             self.copy(k).start()
 
-    def spread(self):
-        if not self.flat:
-            for j in (1, 2, 3):
-                self.copy(j - 1).wait_recv()
-                for k in range(3):
-                    self.copy(3 + 3 * (4 - j) + k).start()
+    def line(self):
+        z = self.place.z
+
+        @pl.when(z < 3)
+        def _():
+            self.copy(0).start()
+
+        @pl.when(z > 0)
+        def _():
+            self.copy(20).start()
+
+    def hop(self, h):
+        z = self.place.z
+
+        @pl.when(z >= h)
+        def _():
+            self.copy(h - 1).wait_recv()
+            if h < 3:
+
+                @pl.when(z < 3)
+                def _():
+                    self.copy(h).start()
+
+            for k in range(3):
+                self.copy(3 + 3 * (4 - h) + k).start()
+
+        @pl.when(z + h <= 3)
+        def _():
+            self.copy(19 + h).wait_recv()
+            if h < 3:
+
+                @pl.when(z > 0)
+                def _():
+                    self.copy(20 + h).start()
+
+            for k in range(3):
+                self.copy(3 + 3 * h + k).start()
 
     def forward(self):
         for j in self.pieces():
@@ -192,9 +222,18 @@
             self.copy(k).wait_recv()
 
     def drain(self):
+        z = self.place.z
         if not self.flat:
             for k in range(3):
-                self.copy(k).wait_send()
+
+                @pl.when((z < 3) & (z >= k))
+                def _(k=k):
+                    self.copy(k).wait_send()
+
+                @pl.when((z > 0) & (z + k <= 3))
+                def _(k=k):
+                    self.copy(20 + k).wait_send()
+
         for j in self.pieces():
             for k in range(3):
                 self.copy(3 + 3 * j + k).wait_send()
@@ -245,6 +284,8 @@
             return carry
 
         lax.fori_loop(0, 8, step, 0)
+
+    def spread(self):
         self.copy(1).start()
         self.copy(2).start()
 
@@ -478,7 +519,8 @@
         for w, g in enumerate((grad_p, grad_d, grad_u, grad_n, grad_c))
     )
     grad_a = full_u
-    parts = (slice(0, piece // 2), slice(piece // 2, piece))
+    third = piece // 3
+    parts = [slice(n * third, (n + 1) * third) for n in range(3)]
     sa = [
         Scatter(
             place,
@@ -518,16 +560,21 @@
     full_a[z, row, col, core, :, 0:CUT] = attend_weight[...].astype(BF)
     full_a[z, row, col, core, :, CUT:] = output_weight[...].T.astype(BF)
     ga.start()
+    ga.line()
     loads[10].wait()
     full_c[row, col, core] = class_weight[...].astype(BF)
     gc.start()
     loads[7].wait()
     full_u[z, row, col, core] = up_weight[...].astype(BF)
     gu.start()
+    gu.line()
     loads[8].wait()
+    full_d[z, row, col, core] = down_weight[...].astype(BF)
+    gd.start()
     loads[9].wait()
-    full_d[z, row, col, core] = down_weight[...].astype(BF)
     full_p[z, row, col, core] = patch_weight[...].astype(BF)
+    gp.start()
+    ga.hop(1)
 
     loads[1].wait()
     loads[2].wait()
@@ -537,10 +584,12 @@
     seg_col[...] = jnp.broadcast_to(seg_row[...], (8, span)).T[:, 0:1]
 
     ge.forward()
+    ga.hop(2)
     ge.across()
-    ga.spread()
+    ga.hop(3)
+    gd.line()
+    gu.hop(1)
     ge.last()
-    gd.start()
     gc.forward()
     halo.wait()
     for d in range(8):
@@ -555,15 +604,17 @@
         return carry
 
     lax.fori_loop(0, span // 128, first_norm, 0)
-    gu.spread()
+    gu.hop(2)
     ga.forward()
     gc.across()
+    gu.hop(3)
+    gp.line()
+    gd.hop(1)
     ga.across()
     gc.last()
-    gd.spread()
-    gp.start()
     class_all[z] = dot(embed[...], whole(full_c[...])).astype(BF)
     line_all.start()
+    gd.hop(2)
     ga.last()
 
     def project(t, carry):
@@ -571,6 +622,8 @@
         return carry
 
     lax.fori_loop(0, 4, project, 0)
+    gd.hop(3)
+    gp.hop(1)
     gu.forward()
 
     probs[...] = jnp.zeros_like(probs)
@@ -595,15 +648,22 @@
                         prob, joint[t, near, v_cols]
                     ).astype(BF)
 
+        @pl.when(t == 0)
+        def _():
+            gp.hop(2)
+
         @pl.when(t == 1)
         def _():
-            gp.spread()
+            gp.hop(3)
             gu.across()
 
+        @pl.when(t == 2)
+        def _():
+            gd.forward()
+
         return carry
 
     lax.fori_loop(0, 4, attend, 0)
-    gd.forward()
     resid_one[...] = tokens[...].astype(F32)
 
     def output(t, carry):
@@ -689,6 +749,7 @@
     branch = d_total.astype(BF)
     flipped = branch.T
     sp.planes()
+    sp.spread()
 
     def down(t, carry):
         grad_d[t] = dot(flipped, hidden[t]).astype(BF).reshape(grad_d.shape[1:])
@@ -709,6 +770,7 @@
         @pl.when(t == 1)
         def _():
             sd.planes()
+            sd.spread()
 
         return carry
 
@@ -752,6 +814,7 @@
 
     lax.fori_loop(0, 4, outer, 0)
     sc.planes()
+    sc.spread()
     back_halo.wait()
 
     def attended_back(t, carry):
@@ -762,6 +825,7 @@
 
     lax.fori_loop(0, 4, attended_back, 0)
     sd.lines()
+    su.spread()
     line_row.wait()
     stores[8].start()
     stack[...] = jnp.zeros_like(stack)
@@ -808,8 +872,8 @@
 
         @pl.when(t == 2)
         def _():
-            su.lines()
             sc.points()
+            sd.points()
 
         return carry
 
@@ -824,12 +888,15 @@
     lax.fori_loop(0, 4, attend_grad, 0)
     for chunk in sa:
         chunk.start()
-    sd.points()
+    su.lines()
+    sa[0].planes()
+    sa[0].spread()
+    sa[1].planes()
+    sa[1].spread()
     class_sum[z, row, col, core] = sc.result().astype(BF)
     gs.start()
-    for chunk in sa:
-        chunk.planes()
-    gs.spread()
+    gs.line()
+    sa[2].planes()
     total[...] = jnp.zeros_like(total)
 
     def joint_back(t, carry):
@@ -837,8 +904,8 @@
         return carry
 
     lax.fori_loop(0, 4, joint_back, 0)
+    gs.hop(1)
     su.points()
-    gs.forward()
     xhat, inverse = norm_parts(tokens[...].astype(F32))
     gain_one_sum = jnp.sum(total[...] * xhat, axis=0, keepdims=True)
     d_resid[...] += norm_back(total[...] * gain_first, xhat, inverse)
@@ -851,22 +918,29 @@
             grad_n[spot + (slice(0, 1), slice(0, piece))] = gain_one_sum[:, cols]
             grad_n[spot + (slice(1, 2), slice(0, piece))] = gain_two_sum[:, cols]
     sn.start()
+    sa[0].lines()
+    sa[2].spread()
+    gs.hop(2)
     sn.planes()
-    sa[0].lines()
+    sn.spread()
     share_p[...] = sp.result()
     stores[2].start()
-    gs.across()
+    gs.hop(3)
+    sa[1].lines()
+    sa[0].points()
+    gs.forward()
     sn.lines()
-    sa[1].lines()
     share_d[...] = sd.result()
     stores[3].start()
+    sa[1].points()
+    sa[2].lines()
+    sn.points()
+    gs.across()
+    share_u[...] = su.result()
+    stores[4].start()
     gs.last()
     stores[9].start()
-    sa[0].points()
-    sn.points()
-    share_u[...] = su.result()
-    stores[4].start()
-    sa[1].points()
+    sa[2].points()
     share_n[...] = sn.result()
     stores[6].start()
     for chunk, part in zip(sa, parts):
@@ -955,10 +1029,10 @@
     ):
         scratch += scatter_buffers(rows, cols, dtype)
     scratch += [
-        pltpu.SemaphoreType.DMA((7, 20)),
-        pltpu.SemaphoreType.DMA((7, 20)),
-        pltpu.SemaphoreType.DMA((7, 8)),
-        pltpu.SemaphoreType.DMA((7, 8)),
+        pltpu.SemaphoreType.DMA((7, 23)),
+        pltpu.SemaphoreType.DMA((7, 23)),
+        pltpu.SemaphoreType.DMA((8, 8)),
+        pltpu.SemaphoreType.DMA((8, 8)),
         pltpu.SemaphoreType.DMA((4, 3)),
         pltpu.SemaphoreType.DMA((2, 4)),
         pltpu.SemaphoreType.DMA((len(operands),)),

time: 199 us -> 183 us (0.920)
  Pallas kernels: 198 us -> 181 us
    pallas_call x1, Pallas kernels: 192 us -> 175 us  [step_call(): pl.pallas_call(step_kernel, out_shape=outs, in_specs=any_specs(len(operan...]
where the time goes in v5:
time: 183 us; the launch traced here: 182 us
  Pallas kernels  181 us (99%)
    pallas_call x1, Pallas kernels, step_call(): pl.pallas_call(step_kernel, out_shape=outs, in_specs=any_specs(len(operan...  175 us
    pallas_call x1, Pallas kernels, update_call(): pl.pallas_call(update_kernel, out_shape=outs, in_specs=any_specs(len(oper...  6.05 us

profile of v5, /device:TPU:0, one launch (start us, length us, event | category | flops | bytes accessed | tf_op | source)
XLA Modules:
  0.0 182.2 jit_solution(13591999819666629194)
XLA Ops:
  0.7 175.3 %shard_map.437 = (f32[150,256]{1,0:T(8,128)}, f32[256,768]{1,0:T(8,128)}, f32[96,192]{1,0:T(8,128)}, f32[96,768]{1,0:T(8,128)}, f32[96,768]{1,0:T(8,128)}, /*ind...) custom-call(bf16[256,768]{1,0:T(8,128)(2,1)} %refs_0_.1, ...), custom_call_target="tpu_custom_call" | custom-call | tf_op jit(solution)/shard_map/pallas_call | solution.py:1041
  176.0 6.1 %shard_map.438 = (f32[150,256]{1,0:T(8,128)}, f32[256,768]{1,0:T(8,128)}, f32[1,96]{1,0:T(1,128)}, f32[96,576]{1,0:T(8,128)}, f32[192,96]{1,0:T(8,128)}, /*index...) custom-call(f32[150,256]{1,0:T(8,128)} %get-tuple-element.50.refs_0_, ...), custom_call_target="tpu_custom_call" | custom-call | tf_op jit(solution)/shard_map/pallas_call | solution.py:1135

commit v6 on v5

--- a/solution.py
+++ b/solution.py
@@ -241,6 +241,103 @@
             self.copy(k).wait_send()
 
 
+class PlaneGather:
+    def __init__(self, place, full, sends, receives, w):
+        self.place, self.full, self.w = place, full, w
+        self.sends, self.receives = sends, receives
+
+    def copy(self, k):
+        place, full = self.place, self.full
+        row, col, core, z = place.row, place.col, place.core, place.z
+        half = full.shape[4] // 2
+        if k < 3:
+            view, target = full.at[z, row, col, core], (place.x, place.y, place.sibling)[k]
+        elif k == 3:
+            view, target = full.at[z, row, 1 - col, core, 0:half], place.y
+        elif k == 4:
+            view, target = full.at[z, 1 - row, col, core, half : 2 * half], place.x
+        elif k < 8:
+            spot = ((row, 1 - col), (1 - row, col), (1 - row, 1 - col))[k - 5]
+            view, target = full.at[z, spot[0], spot[1], core], place.sibling
+        elif k < 11:
+            view, target = full.at[z - (k - 8), :, :, core], place.along(1)
+        elif k < 14:
+            view, target = full.at[z + k - 11, :, :, core], place.along(3)
+        else:
+            view, target = full.at[(z + k - 13) % 4, :, :, core], place.sibling
+        return remote(view, view, self.sends.at[self.w, k], self.receives.at[self.w, k], target)
+
+    def start(self):
+        for k in range(3):
+            self.copy(k).start()
+
+    def forward(self):
+        self.copy(0).wait_recv()
+        self.copy(3).start()
+        self.copy(5).start()
+        self.copy(1).wait_recv()
+        self.copy(4).start()
+        self.copy(6).start()
+
+    def across(self):
+        z = self.place.z
+        self.copy(3).wait_recv()
+        self.copy(4).wait_recv()
+
+        @pl.when(z < 3)
+        def _():
+            self.copy(8).start()
+
+        @pl.when(z > 0)
+        def _():
+            self.copy(11).start()
+
+        self.copy(7).start()
+
+    def hop(self, h):
+        z = self.place.z
+
+        @pl.when(z >= h)
+        def _():
+            self.copy(7 + h).wait_recv()
+            if h < 3:
+
+                @pl.when(z < 3)
+                def _():
+                    self.copy(8 + h).start()
+
+            self.copy(13 + 4 - h).start()
+
+        @pl.when(z + h <= 3)
+        def _():
+            self.copy(10 + h).wait_recv()
+            if h < 3:
+
+                @pl.when(z > 0)
+                def _():
+                    self.copy(11 + h).start()
+
+            self.copy(13 + h).start()
+
+    def last(self):
+        for k in (2, 5, 6, 7, 14, 15, 16):
+            self.copy(k).wait_recv()
+
+    def drain(self):
+        z = self.place.z
+        for k in (0, 1, 2, 3, 4, 5, 6, 7, 14, 15, 16):
+            self.copy(k).wait_send()
+        for k in range(3):
+
+            @pl.when((z < 3) & (z >= k))
+            def _(k=k):
+                self.copy(8 + k).wait_send()
+
+            @pl.when((z > 0) & (z + k <= 3))
+            def _(k=k):
+                self.copy(11 + k).wait_send()
+
+
 class Scatter:
     def __init__(self, place, grad, buffers, sends, receives, w):
         self.place, self.grad, self.w = place, grad, w
@@ -250,8 +347,9 @@
     def copy(self, k):
         place, r1 = self.place, self.r1
         row, col, core = place.row, place.col, place.core
-        if k == 0:
-            pair = (self.grad.at[:, :, :, 1 - core], r1, place.sibling)
+        if k in (0, 8):
+            half = slice(0, 2) if k == 0 else slice(2, 4)
+            pair = (self.grad.at[half, :, :, 1 - core], r1.at[half], place.sibling)
         elif k == 1:
             pair = (r1.at[0:2, :, 1 - col], self.r2a, place.x)
         elif k == 2:
@@ -271,23 +369,25 @@
         ref = self.r1
         ref[index] = (ref[index].astype(F32) + other.astype(F32)).astype(ref.dtype)
 
-    def start(self):
-        self.copy(0).start()
-
-    def planes(self):
+    def start(self, halves=(0, 1)):
+        for half in halves:
+            self.copy(8 * half).start()
+
+    def planes(self, halves=(0, 1)):
         core = self.place.core
-        self.copy(0).wait_recv()
-
-        def step(i, carry):
-            t, y = i // 2, i % 2
-            self.add((t, y), self.grad[t, y, :, core])
-            return carry
-
-        lax.fori_loop(0, 8, step, 0)
-
-    def spread(self):
-        self.copy(1).start()
-        self.copy(2).start()
+        for half in halves:
+            self.copy(8 * half).wait_recv()
+
+            def step(i, carry):
+                t, y = 2 * half + i // 2, i % 2
+                self.add((t, y), self.grad[t, y, :, core])
+                return carry
+
+            lax.fori_loop(0, 4, step, 0)
+
+    def spread(self, halves=(0, 1)):
+        for half in halves:
+            self.copy(1 + half).start()
 
     def lines(self):
         col, row = self.place.col, self.place.row
@@ -321,6 +421,90 @@
         for j in range(3):
             total = total + self.r4[j].astype(F32)
         return total
+
+    def drain(self):
+        for k in range(9):
+            self.copy(k).wait_send()
+
+
+class LineScatter:
+    def __init__(self, place, grad, buffers, sends, receives, w):
+        self.place, self.grad, self.w = place, grad, w
+        self.sends, self.receives = sends, receives
+        self.r1, self.r2a, self.r2b, self.r3a, self.r3b, self.r4 = buffers
+
+    def copy(self, k):
+        place, r1 = self.place, self.r1
+        row, col, core, z = place.row, place.col, place.core, place.z
+        half = r1.shape[3] // 2
+        if k == 0:
+            pair = (self.grad.at[:, :, :, 1 - core], r1, place.sibling)
+        elif k == 1:
+            pair = (r1.at[z, :, 1 - col, 0:half], self.r2a, place.x)
+        elif k == 2:
+            pair = (r1.at[z, 1 - row, :, half : 2 * half], self.r2b, place.y)
+        elif k == 3:
+            pair = (r1.at[z, 1 - row, col, 0:half], self.r3a, place.y)
+        elif k == 4:
+            pair = (r1.at[z, row, 1 - col, half : 2 * half], self.r3b, place.x)
+        else:
+            peer = place.along(k - 4)
+            pair = (r1.at[peer[1]], self.r4.at[k - 5], peer)
+        return remote(
+            pair[0], pair[1], self.sends.at[self.w, k], self.receives.at[self.w, k], pair[2]
+        )
+
+    def add(self, index, other):
+        ref = self.r1
+        ref[index] = (ref[index].astype(F32) + other.astype(F32)).astype(ref.dtype)
+
+    def start(self):
+        self.copy(0).start()
+
+    def planes(self):
+        core = self.place.core
+        self.copy(0).wait_recv()
+
+        def step(i, carry):
+            t, y = i // 2, i % 2
+            self.add((t, y), self.grad[t, y, :, core])
+            return carry
+
+        lax.fori_loop(0, 8, step, 0)
+        for k in (5, 6, 7):
+            self.copy(k).start()
+
+    def depth(self):
+        z = self.place.z
+        for k in (5, 6, 7):
+            self.copy(k).wait_recv()
+        for y in range(2):
+            for x in range(2):
+                value = self.r1[z, y, x].astype(F32)
+                for j in range(3):
+                    value = value + self.r4[j, y, x].astype(F32)
+                self.r1[z, y, x] = value.astype(self.r1.dtype)
+        self.copy(1).start()
+        self.copy(2).start()
+
+    def lines(self):
+        place, half = self.place, self.r1.shape[3] // 2
+        self.copy(1).wait_recv()
+        for y in range(2):
+            self.add((place.z, y, place.col, slice(0, half)), self.r2a[y])
+        self.copy(3).start()
+        self.copy(2).wait_recv()
+        for x in range(2):
+            self.add((place.z, place.row, x, slice(half, 2 * half)), self.r2b[x])
+        self.copy(4).start()
+
+    def result(self, out):
+        place, half = self.place, self.r1.shape[3] // 2
+        for k, part in ((3, slice(0, half)), (4, slice(half, 2 * half))):
+            self.copy(k).wait_recv()
+            other = self.r3a if k == 3 else self.r3b
+            mine = self.r1[place.z, place.row, place.col, part]
+            out[part] = mine.astype(F32) + other[...].astype(F32)
 
     def drain(self):
         for k in range(8):
@@ -511,11 +695,15 @@
     classes = class_embed.shape[0]
     mine = slice(HALO, HALO + own)
     ge, ga, gc, gu, gd, gp, gs = (
-        Gather(place, full, gather_sends, gather_receives, w)
+        (PlaneGather if full is full_p else Gather)(
+            place, full, gather_sends, gather_receives, w
+        )
         for w, full in enumerate((full_e, full_a, full_c, full_u, full_d, full_p, class_sum))
     )
     sp, sd, su, sn, sc = (
-        Scatter(place, g, buffers[6 * w : 6 * w + 6], scatter_sends, scatter_receives, w)
+        (LineScatter if g is grad_p else Scatter)(
+            place, g, buffers[6 * w : 6 * w + 6], scatter_sends, scatter_receives, w
+        )
         for w, g in enumerate((grad_p, grad_d, grad_u, grad_n, grad_c))
     )
     grad_a = full_u
@@ -568,12 +756,12 @@
     full_u[z, row, col, core] = up_weight[...].astype(BF)
     gu.start()
     gu.line()
+    loads[9].wait()
+    full_p[z, row, col, core] = patch_weight[...].astype(BF)
+    gp.start()
     loads[8].wait()
     full_d[z, row, col, core] = down_weight[...].astype(BF)
     gd.start()
-    loads[9].wait()
-    full_p[z, row, col, core] = patch_weight[...].astype(BF)
-    gp.start()
     ga.hop(1)
 
     loads[1].wait()
@@ -582,15 +770,14 @@
     seg_wide[:, HALO : HALO + segments.shape[1]] = segments[...].astype(F32)
     seg_row[...] = seg_wide[:, pl.ds(pl.multiple_of(z * own, 128), span)]
     seg_col[...] = jnp.broadcast_to(seg_row[...], (8, span)).T[:, 0:1]
-
+    gc.forward()
+    gd.line()
     ge.forward()
+    gu.hop(1)
+    ge.across()
     ga.hop(2)
-    ge.across()
     ga.hop(3)
-    gd.line()
-    gu.hop(1)
     ge.last()
-    gc.forward()
     halo.wait()
     for d in range(8):
         embed[:, d * piece : (d + 1) * piece] = full_e[d // 4, (d // 2) % 2, d % 2]
@@ -604,28 +791,29 @@
         return carry
 
     lax.fori_loop(0, span // 128, first_norm, 0)
+    gp.forward()
     gu.hop(2)
+    gp.across()
     ga.forward()
     gc.across()
-    gu.hop(3)
-    gp.line()
     gd.hop(1)
+    gc.last()
     ga.across()
-    gc.last()
     class_all[z] = dot(embed[...], whole(full_c[...])).astype(BF)
     line_all.start()
+    class_row[z] = class_weight[...].astype(BF)
+    line_row.start()
+    ga.last()
     gd.hop(2)
-    ga.last()
-
     def project(t, carry):
         joint[t] = dot(norm_one[...], whole(full_a[t])[:, :CUT]).astype(BF)
         return carry
 
     lax.fori_loop(0, 4, project, 0)
+    gu.hop(3)
+    gu.forward()
+    gp.hop(1)
     gd.hop(3)
-    gp.hop(1)
-    gu.forward()
-
     probs[...] = jnp.zeros_like(probs)
 
     def attend(t, carry):
@@ -654,12 +842,16 @@
 
         @pl.when(t == 1)
         def _():
+            gu.across()
             gp.hop(3)
-            gu.across()
 
         @pl.when(t == 2)
         def _():
             gd.forward()
+
+        @pl.when(t == 3)
+        def _():
+            gp.last()
 
         return carry
 
@@ -673,8 +865,32 @@
     lax.fori_loop(0, 4, output, 0)
     xhat, _ = norm_parts(resid_one[...])
     norm_two[...] = (xhat * gain_second).astype(BF)
+    gu.last()
+    def expand(t, carry):
+        value, derivative = gelu_parts(dot(norm_two[...], whole(full_u[t])))
+        hidden[t] = value.astype(BF)
+        slope[t] = derivative.astype(BF)
+
+        @pl.when(t == 3)
+        def _():
+            gd.across()
+            gd.last()
+
+        return carry
+
+    lax.fori_loop(0, 4, expand, 0)
+    total[...] = resid_one[...]
+
+    def contract(t, carry):
+        total[...] += dot(hidden[t], whole(full_d[t]), ((1,), (1,)))
+        return carry
+
+    lax.fori_loop(0, 4, contract, 0)
+    resid_low[...] = total[...].astype(BF)
     line_all.wait()
     stores[7].start()
+    line_row.wait()
+    stores[8].start()
     class_square = jnp.zeros((class_all.shape[1], 1), F32)
     for t in range(4):
         value = class_all[t].astype(F32)
@@ -682,28 +898,6 @@
     class_inverse = lax.rsqrt(class_square + epsilon_unit)
     for t in range(4):
         class_low[t] = (class_all[t].astype(F32) * class_inverse).astype(BF)
-    gu.last()
-    gp.forward()
-
-    def expand(t, carry):
-        value, derivative = gelu_parts(dot(norm_two[...], whole(full_u[t])))
-        hidden[t] = value.astype(BF)
-        slope[t] = derivative.astype(BF)
-        return carry
-
-    lax.fori_loop(0, 4, expand, 0)
-    gd.across()
-    gp.across()
-    gd.last()
-    total[...] = resid_one[...]
-
-    def contract(t, carry):
-        total[...] += dot(hidden[t], whole(full_d[t]), ((1,), (1,)))
-        return carry
-
-    lax.fori_loop(0, 4, contract, 0)
-    resid_low[...] = total[...].astype(BF)
-    gp.last()
 
     square = jnp.zeros((own, 1), F32)
     pieces = []
@@ -749,16 +943,23 @@
     branch = d_total.astype(BF)
     flipped = branch.T
     sp.planes()
-    sp.spread()
 
     def down(t, carry):
         grad_d[t] = dot(flipped, hidden[t]).astype(BF).reshape(grad_d.shape[1:])
+
+        @pl.when(t == 1)
+        def _():
+            sd.start((0,))
+
+        @pl.when(t == 3)
+        def _():
+            sd.start((1,))
+            sd.planes((0,))
+            sd.spread((0,))
+
         return carry
 
     lax.fori_loop(0, 4, down, 0)
-    sd.start()
-    class_row[z] = class_weight[...].astype(BF)
-    line_row.start()
     flipped = norm_two[...].T
 
     def up(t, carry):
@@ -767,10 +968,10 @@
         slope[t] = back
         grad_u[t] = dot(flipped, back).astype(BF).reshape(grad_u.shape[1:])
 
-        @pl.when(t == 1)
-        def _():
-            sd.planes()
-            sd.spread()
+        @pl.when(t == 0)
+        def _():
+            sd.planes((1,))
+            sd.spread((1,))
 
         return carry
 
@@ -793,7 +994,6 @@
     window[mine] = d_resid[...].astype(BF)
     back_halo = Halo(place, window, own, halo_sems.at[1])
     back_halo.start()
-    sp.lines()
     class_wide[...] = jnp.zeros_like(class_wide)
     for t in range(4):
         class_wide[0:classes, t * narrow : (t + 1) * narrow] = dot(d_products, unit_low[t])
@@ -824,10 +1024,9 @@
         return carry
 
     lax.fori_loop(0, 4, attended_back, 0)
+    sc.lines()
     sd.lines()
     su.spread()
-    line_row.wait()
-    stores[8].start()
     stack[...] = jnp.zeros_like(stack)
 
     def attend_back(t, carry):
@@ -867,36 +1066,27 @@
 
         @pl.when(t == 0)
         def _():
-            sp.points()
-            sc.lines()
+            sc.points()
+            sp.depth()
+
+        @pl.when(t == 1)
+        def _():
+            class_sum[z, row, col, core] = sc.result().astype(BF)
+            gs.start()
+            gs.line()
 
         @pl.when(t == 2)
         def _():
-            sc.points()
+            gs.hop(1)
             sd.points()
 
+        @pl.when(t == 3)
+        def _():
+            gs.hop(2)
+
         return carry
 
     lax.fori_loop(0, 4, attend_back, 0)
-    flipped = norm_one[mine].T
-
-    def attend_grad(t, carry):
-        block = dot(flipped, hidden[t, :, :CUT]).astype(BF)
-        grad_a[t, :, :, :, :, :CUT] = block.reshape((2, 2, 2, piece, CUT))
-        return carry
-
-    lax.fori_loop(0, 4, attend_grad, 0)
-    for chunk in sa:
-        chunk.start()
-    su.lines()
-    sa[0].planes()
-    sa[0].spread()
-    sa[1].planes()
-    sa[1].spread()
-    class_sum[z, row, col, core] = sc.result().astype(BF)
-    gs.start()
-    gs.line()
-    sa[2].planes()
     total[...] = jnp.zeros_like(total)
 
     def joint_back(t, carry):
@@ -904,12 +1094,8 @@
         return carry
 
     lax.fori_loop(0, 4, joint_back, 0)
-    gs.hop(1)
-    su.points()
     xhat, inverse = norm_parts(tokens[...].astype(F32))
     gain_one_sum = jnp.sum(total[...] * xhat, axis=0, keepdims=True)
-    d_resid[...] += norm_back(total[...] * gain_first, xhat, inverse)
-    stores[1].start()
     grad_n[...] = jnp.zeros_like(grad_n)
     for d in range(8):
         cols = slice(d * piece, (d + 1) * piece)
@@ -918,31 +1104,50 @@
             grad_n[spot + (slice(0, 1), slice(0, piece))] = gain_one_sum[:, cols]
             grad_n[spot + (slice(1, 2), slice(0, piece))] = gain_two_sum[:, cols]
     sn.start()
+    flipped = norm_one[mine].T
+
+    def attend_grad(t, carry):
+        block = dot(flipped, hidden[t, :, :CUT]).astype(BF)
+        grad_a[t, :, :, :, :, :CUT] = block.reshape((2, 2, 2, piece, CUT))
+        return carry
+
+    lax.fori_loop(0, 4, attend_grad, 0)
+    for chunk in sa:
+        chunk.start()
+    sn.planes()
+    sn.spread()
+    su.lines()
+    sp.lines()
+    sa[0].planes()
+    sa[0].spread()
+    sa[1].planes()
+    sa[1].spread()
+    gs.hop(3)
+    sa[2].planes()
+    d_resid[...] += norm_back(total[...] * gain_first, xhat, inverse)
+    stores[1].start()
+    sn.lines()
+    su.points()
     sa[0].lines()
     sa[2].spread()
-    gs.hop(2)
-    sn.planes()
-    sn.spread()
-    share_p[...] = sp.result()
+    sn.points()
+    sp.result(share_p)
     stores[2].start()
-    gs.hop(3)
+    gs.forward()
     sa[1].lines()
     sa[0].points()
-    gs.forward()
-    sn.lines()
+    gs.across()
     share_d[...] = sd.result()
     stores[3].start()
+    share_n[...] = sn.result()
+    stores[6].start()
+    sa[2].lines()
     sa[1].points()
-    sa[2].lines()
-    sn.points()
-    gs.across()
+    gs.last()
+    stores[9].start()
     share_u[...] = su.result()
     stores[4].start()
-    gs.last()
-    stores[9].start()
     sa[2].points()
-    share_n[...] = sn.result()
-    stores[6].start()
     for chunk, part in zip(sa, parts):
         share_a[part] = chunk.result()
     stores[5].start()
@@ -1020,8 +1225,15 @@
         wide(rows_e, width),
         low(3, piece, width),
     ]
+    scratch += [
+        low(4, 2, 2, piece, narrow),
+        low(2, piece // 2, narrow),
+        low(2, piece // 2, narrow),
+        low(piece // 2, narrow),
+        low(piece // 2, narrow),
+        low(3, 2, 2, piece, narrow),
+    ]
     for rows, cols, dtype in (
-        (piece, narrow, BF),
         (piece, high, BF),
         (piece, high, BF),
         (8, 128, F32),
@@ -1031,8 +1243,8 @@
     scratch += [
         pltpu.SemaphoreType.DMA((7, 23)),
         pltpu.SemaphoreType.DMA((7, 23)),
-        pltpu.SemaphoreType.DMA((8, 8)),
-        pltpu.SemaphoreType.DMA((8, 8)),
+        pltpu.SemaphoreType.DMA((8, 9)),
+        pltpu.SemaphoreType.DMA((8, 9)),
         pltpu.SemaphoreType.DMA((4, 3)),
         pltpu.SemaphoreType.DMA((2, 4)),
         pltpu.SemaphoreType.DMA((len(operands),)),

time: 183 us -> 175 us (0.956)
  Pallas kernels: 181 us -> 174 us
    pallas_call x1, Pallas kernels: 175 us -> 168 us  [step_call(): pl.pallas_call(step_kernel, out_shape=outs, in_specs=any_specs(len(operan...]
where the time goes in v6:
time: 175 us
  Pallas kernels  174 us (99%)
    pallas_call x1, Pallas kernels, step_call(): pl.pallas_call(step_kernel, out_shape=outs, in_specs=any_specs(len(operan...  168 us
    pallas_call x1, Pallas kernels, update_call(): pl.pallas_call(update_kernel, out_shape=outs, in_specs=any_specs(len(oper...  6.05 us

profile of v6, /device:TPU:0, one launch (start us, length us, event | category | flops | bytes accessed | tf_op | source)
XLA Modules:
  0.0 174.9 jit_solution(17101564305864558)
XLA Ops:
  0.7 168.0 %shard_map.437 = (f32[150,256]{1,0:T(8,128)}, f32[256,768]{1,0:T(8,128)}, f32[96,192]{1,0:T(8,128)}, f32[96,768]{1,0:T(8,128)}, f32[96,768]{1,0:T(8,128)}, /*ind...) custom-call(bf16[256,768]{1,0:T(8,128)(2,1)} %refs_0_.1, ...), custom_call_target="tpu_custom_call" | custom-call | tf_op jit(solution)/shard_map/pallas_call | solution.py:1253
  168.7 6.1 %shard_map.438 = (f32[150,256]{1,0:T(8,128)}, f32[256,768]{1,0:T(8,128)}, f32[1,96]{1,0:T(1,128)}, f32[96,576]{1,0:T(8,128)}, f32[192,96]{1,0:T(8,128)}, /*index...) custom-call(f32[150,256]{1,0:T(8,128)} %get-tuple-element.50.refs_0_, ...), custom_call_target="tpu_custom_call" | custom-call | tf_op jit(solution)/shard_map/pallas_call | solution.py:1347

commit v7 on v6

--- a/solution.py
+++ b/solution.py
@@ -1270,16 +1270,15 @@
     params, means, squares = held[10:19], held[19:28], held[28:37]
     loads = loader(inputs, held, in_sems)
     stores = loader(held[:2] + squares + means, outputs, out_sems)
-    order = (0, 3, 6, 4, 5, 2, 1, 8, 7)
-    for n in (6, 0, 1, 2, 4, 3, 5, 7, 8, 9):
+    order = (8, 7, 4, 5, 1, 2, 6, 0, 3)
+    for n in (7, 8, 9, 18, 0, 1, 6, 2, 4, 3, 5):
         loads[n].start()
     for n in order:
         for k in (10, 19, 28):
-            loads[k + n].start()
-    for n in range(10):
+            if k + n != 18:
+                loads[k + n].start()
+    for n in (7, 8, 9):
         loads[n].wait()
-        if n < 2:
-            stores[n].start()
 
     def update(n, gradient):
         scale = block_scale if n < 6 else 1.0
@@ -1294,14 +1293,6 @@
         stores[11 + n].start()
 
     piece = share_p.shape[0]
-    update(0, share_n[0:1, 0:piece])
-    update(3, share_n[1:2, 0:piece])
-    update(6, share_p[...])
-    update(4, share_u[...])
-    update(5, share_d[...])
-    update(2, share_a[:, CUT:].T)
-    update(1, share_a[:, :CUT])
-
     classes = params[8].shape[0]
     narrow = class_all.shape[2]
     tiles = sum_wide.shape[1] // TILE_COLS
@@ -1331,6 +1322,18 @@
         share_embed += dot(value, class_row[t], ((1,), (1,)))
     update(8, share_embed)
     update(7, dot(embed_low, class_back[lax.axis_index("tensor")], ((0,), (0,))))
+    for n in range(7):
+        loads[n].wait()
+        if n < 2:
+            stores[n].start()
+    update(4, share_u[...])
+    update(5, share_d[...])
+    update(1, share_a[:, :CUT])
+    update(2, share_a[:, CUT:].T)
+    update(6, share_p[...])
+    update(0, share_n[0:1, 0:piece])
+    update(3, share_n[1:2, 0:piece])
+
     for store in stores:
         store.wait()
 

time: 175 us -> 174 us (level)
  no operation moved by 1% of the time
where the time goes in v7:
time: 174 us
  Pallas kernels  173 us (99%)
    pallas_call x1, Pallas kernels, step_call(): pl.pallas_call(step_kernel, out_shape=outs, in_specs=any_specs(len(operan...  168 us
    pallas_call x1, Pallas kernels, update_call(): pl.pallas_call(update_kernel, out_shape=outs, in_specs=any_specs(len(oper...  4.77 us

profile of v7, /device:TPU:0, one launch (start us, length us, event | category | flops | bytes accessed | tf_op | source)
XLA Modules:
  0.0 173.6 jit_solution(18078776308386419959)
XLA Ops:
  0.7 168.0 %shard_map.437 = (f32[150,256]{1,0:T(8,128)}, f32[256,768]{1,0:T(8,128)}, f32[96,192]{1,0:T(8,128)}, f32[96,768]{1,0:T(8,128)}, f32[96,768]{1,0:T(8,128)}, /*ind...) custom-call(bf16[256,768]{1,0:T(8,128)(2,1)} %refs_0_.1, ...), custom_call_target="tpu_custom_call" | custom-call | tf_op jit(solution)/shard_map/pallas_call | solution.py:1253
  168.7 4.8 %shard_map.438 = (f32[150,256]{1,0:T(8,128)}, f32[256,768]{1,0:T(8,128)}, f32[1,96]{1,0:T(1,128)}, f32[96,576]{1,0:T(8,128)}, f32[192,96]{1,0:T(8,128)}, /*index...) custom-call(f32[150,256]{1,0:T(8,128)} %get-tuple-element.50.refs_0_, ...), custom_call_target="tpu_custom_call" | custom-call | tf_op jit(solution)/shard_map/pallas_call | solution.py:1350
